TPU v7x, 32 devices: a whole 2x2x4 slice. The times are simulated.
32 devices in a mesh: dp: 8 (over z, x), tensor: 4 (over y, core).
Axes of the slice: x: 2, y: 2, z: 4, core: 2. Of those that a mesh axis runs over, the one named last changes fastest.
Arguments:
- activations: bfloat16 [2048, 6144], P('dp'), may hold values from -6 to 6
- pre_act: bfloat16 [2048, 24576], P('dp', 'tensor'), may hold values from -8 to 8
- grad_act: bfloat16 [2048, 24576], P('dp', 'tensor'), may hold values from -6 to 6
- kept_weight: bfloat16 [4, 576, 128, 128], P('tensor', 'dp'), may hold values from -0.15625 to 0.15625
- block_cols: int32 [4, 576], P('tensor'), may hold values from 0 to 47, as said below
Outputs:
- weight_grad: bfloat16 [4, 576, 128, 128], P('tensor', 'dp')
- act_grad: bfloat16 [2048, 6144], P('dp')
Inputs may be any that keep to these rules, and one draw needn't show every extreme that they name: `block_cols`: the kept blocks are listed block row by block row, 12 to a row; within one block row of one tensor index the 12 block columns are distinct.
All inputs are finite; a program needn't handle non-finite values.
Results may differ from a plain program's by a relative error of at most 0.0049.
Values may be sent and summed in bfloat16 or wider, within the bound.
No kernel may reach another device: no remote copies, remote signals or barrier semaphores. Data moves between devices by JAX's collectives and lax.ppermute only.
A program may use at most 256 MiB of HBM per device.

v0:
```python
import functools
import math

import jax
import jax.numpy as jnp
from jax import lax
from jax.experimental import pallas as pl
from jax.experimental.pallas import tpu as pltpu
from jax.sharding import PartitionSpec as P


gelu_coef = math.sqrt(2.0 / math.pi)


def gelu_slope(pre_vals):
    pre_wide = pre_vals.astype(jnp.float32)
    inner_arg = gelu_coef * (pre_wide + 0.044715 * pre_wide**3)
    tanh_val = jnp.tanh(inner_arg)
    return 0.5 * (1.0 + tanh_val) + 0.5 * pre_wide * (1.0 - tanh_val**2) * gelu_coef * (
        1.0 + 3.0 * 0.044715 * pre_wide**2
    )


def hidden_gradient(pre_act, grad_act):
    return (grad_act.astype(jnp.float32) * gelu_slope(pre_act)).astype(jnp.bfloat16)


def group_of(amount):
    chosen = 1
    for divisor in range(1, 9):
        if amount % divisor == 0:
            chosen = divisor
    return chosen


def local_any(activations, pre_act, grad_act, kept_weight, block_cols):
    block = kept_weight.shape[-1]
    tok_count, width = activations.shape
    blocks_d = width // block
    dp_size = lax.axis_size("dp")
    grad_scale = 1.0 / math.sqrt(tok_count * dp_size)
    act_blocks = activations.reshape(tok_count, blocks_d, block)
    hidden_grad = hidden_gradient(pre_act, grad_act)
    grad_blocks = hidden_grad.reshape(tok_count, -1, block)
    col_ids = block_cols[0]
    kept_all = col_ids.shape[0]
    per_row = kept_all // blocks_d
    col_table = col_ids.reshape(blocks_d, per_row)
    row_group = group_of(blocks_d)
    group_count = blocks_d // row_group
    gathered = lax.all_gather(kept_weight, "dp", axis=1, tiled=True)
    whole_weights = gathered[0].reshape(blocks_d, per_row, block, block)

    def with_terms(group_index):
        first_row = group_index * row_group
        col_pick = lax.dynamic_slice_in_dim(col_table, first_row, row_group, 0).reshape(-1)
        grad_group = jnp.take(grad_blocks, col_pick, axis=1).reshape(
            tok_count, row_group, per_row, block
        )
        weight_group = lax.dynamic_slice_in_dim(whole_weights, first_row, row_group, 0)
        act_part = jnp.einsum(
            "trkf,rkdf->trd", grad_group, weight_group, preferred_element_type=jnp.float32
        )
        act_group = lax.dynamic_slice_in_dim(act_blocks, first_row, row_group, 1)
        block_term = (
            jnp.einsum("tra,trkf->rkaf", act_group, grad_group, preferred_element_type=jnp.float32)
            * grad_scale
        )
        return (act_part, block_term)

    act_parts, block_terms = lax.map(with_terms, jnp.arange(group_count, dtype=jnp.int32))
    summed = lax.psum_scatter(
        block_terms.reshape(kept_all, block, block), "dp", scatter_dimension=0, tiled=True
    )
    weight_grad = summed.astype(jnp.bfloat16).reshape(1, -1, block, block)
    partial_value = jnp.transpose(act_parts, (1, 0, 2, 3)).reshape(tok_count, width)
    act_grad = lax.psum(partial_value, "tensor").astype(jnp.bfloat16)
    return (weight_grad, act_grad)


SIDE, NEAR, FAR = 1, 2, 4
SETS = (0, SIDE, FAR, FAR | SIDE)
CHUNKS = (6, 5, 3, 2)


def columns_of(chunk_refs, spans):
    return jnp.concatenate(
        [jnp.concatenate([ref[:, span] for span in spans], axis=1) for ref in chunk_refs], axis=0
    )


def spans_of(cols_ref, first, count, block):
    return [
        pl.ds(pl.multiple_of(cols_ref[first + k] * block, block), block) for k in range(count)
    ]


def weight_term_kernel(
    per_row, rows, first_row, grad_scale, act_count, hid_count, place_ref, cols_ref, *refs
):
    act_refs, hid_refs = refs[:act_count], refs[act_count : act_count + hid_count]
    acc_refs, out_ref = refs[act_count + hid_count : -1], refs[-1]
    step_rows = out_ref.shape[0] // per_row
    block = out_ref.shape[1]
    group = 4 if per_row % 4 == 0 else 1

    @pl.loop(0, step_rows)
    def _(step_row):
        row = first_row + pl.program_id(0) * step_rows + step_row
        first = (place_ref[0] * rows + row) * per_row
        lanes = pl.ds(pl.multiple_of(row * block, block), block)
        act_t = jnp.concatenate([ref[:, lanes] for ref in act_refs], axis=0).T
        for part in range(per_row // group):
            start = part * group
            hid = columns_of(hid_refs, spans_of(cols_ref, first + start, group, block))
            term = (
                lax.dot_general(
                    act_t, hid, (((1,), (0,)), ((), ())), preferred_element_type=jnp.float32
                )
                * grad_scale
            )
            for k in range(group):
                value = term[:, k * block : (k + 1) * block]
                at = step_row * per_row + start + k
                for acc_ref in acc_refs:
                    value = value + acc_ref[at]
                out_ref[at] = value.astype(out_ref.dtype)


def weight_terms(
    place, cols, acts, hids, acc, first_row, count, rows, per_row, block, grad_scale, kind
):
    tok = acts[0][0].shape[0]
    step_rows = next(k for k in (3, 2, 1) if count % k == 0)

    def act_spec(kind_of):
        if kind_of is None:
            return pl.BlockSpec((tok, rows * block), lambda s, place_ref, _: (0, place_ref[0]))
        return pl.BlockSpec(
            (tok, rows * block), lambda s, place_ref, _: (0, kind_of * 2 + place_ref[1])
        )

    chunks = [chunk for hid in hids for chunk in hid]
    accs = [] if acc is None else [acc]
    unit_spec = pl.BlockSpec((step_rows * per_row, block, block), lambda s, *_: (s, 0, 0))
    acc_spec = pl.BlockSpec(
        (step_rows * per_row, block, block), lambda s, *_: (first_row // step_rows + s, 0, 0)
    )
    kept = count * per_row
    return pl.pallas_call(
        functools.partial(
            weight_term_kernel, per_row, rows, first_row, grad_scale, len(acts), len(chunks)
        ),
        out_shape=jax.ShapeDtypeStruct((kept, block, block), kind),
        grid_spec=pltpu.PrefetchScalarGridSpec(
            num_scalar_prefetch=2,
            grid=(count // step_rows,),
            in_specs=[act_spec(entry[1]) for entry in acts]
            + [pl.BlockSpec(chunk.shape, lambda s, *_: (0, 0)) for chunk in chunks]
            + [acc_spec] * len(accs),
            out_specs=unit_spec,
        ),
        cost_estimate=pl.CostEstimate(
            flops=2 * kept * len(hids) * tok * block * block,
            bytes_accessed=2 * len(hids) * tok * chunks[0].shape[1] + 8 * kept * block * block,
            transcendentals=0,
        ),
        name="weight_terms",
    )(place, cols, *[entry[0] for entry in acts], *chunks, *accs)


def act_kernel(per_row, rows, set_count, hid_count, place_ref, cols_ref, *refs):
    hid_refs = refs[:hid_count]
    sources = refs[hid_count : hid_count + 2]
    outs = refs[hid_count + 2 : -2]
    held, sems = refs[-2:]
    unit = pl.program_id(0)
    block = held.shape[-1]
    near = jnp.where(unit == 0, place_ref[2], 1 - place_ref[2])

    def copy_of(source, into):
        return pltpu.make_async_copy(source, held.at[into], sems.at[into])

    @pl.when(unit == 0)
    def _():
        for index, source in enumerate(sources):
            @pl.when(place_ref[2] == place_ref[1])
            def _():
                copy_of(source, index).start()

            @pl.when(place_ref[2] != place_ref[1])
            def _():
                copy_of(source, 1 - index).start()

    copy_of(sources[0], unit).wait()

    @pl.loop(0, rows)
    def _(row):
        first = ((place_ref[0] + NEAR * near) * rows + row) * per_row
        hid = columns_of(hid_refs, spans_of(cols_ref, first, per_row, block))
        weight = jnp.concatenate([held[unit, row * per_row + k] for k in range(per_row)], axis=1)
        part = lax.dot_general(
            hid, weight, (((1,), (1,)), ((), ())), preferred_element_type=jnp.float32
        ).astype(jnp.bfloat16)
        tok = part.shape[0] // set_count
        lanes = pl.ds(pl.multiple_of(row * block, block), block)

        @pl.when(unit == 0)
        def _():
            for k in range(set_count):
                outs[2 * k][:, lanes] = part[k * tok : (k + 1) * tok]

        @pl.when(unit == 1)
        def _():
            for k in range(set_count):
                outs[2 * k + 1][:, lanes] = part[k * tok : (k + 1) * tok]


def act_partials(place, cols, hids, weights, rows, per_row):
    block = weights[0].shape[-1]
    chunks = [chunk for hid in hids for chunk in hid]
    tok = sum(chunk.shape[0] for chunk in hids[0])
    out = pl.BlockSpec((tok, rows * block), lambda s, *_: (0, 0))
    shape = jax.ShapeDtypeStruct((tok, rows * block), jnp.bfloat16)
    kept = 2 * rows * per_row
    return pl.pallas_call(
        functools.partial(act_kernel, per_row, rows, len(hids), len(chunks)),
        out_shape=(shape,) * (2 * len(hids)),
        grid_spec=pltpu.PrefetchScalarGridSpec(
            num_scalar_prefetch=2,
            grid=(2,),
            in_specs=[pl.BlockSpec(chunk.shape, lambda s, *_: (0, 0)) for chunk in chunks]
            + [pl.BlockSpec(memory_space=pl.ANY)] * 2,
            out_specs=[out] * (2 * len(hids)),
            scratch_shapes=[
                pltpu.VMEM((2, rows * per_row, block, block), jnp.bfloat16),
                pltpu.SemaphoreType.DMA((2,)),
            ],
        ),
        cost_estimate=pl.CostEstimate(
            flops=2 * kept * len(hids) * tok * block * block,
            bytes_accessed=2 * len(hids) * tok * chunks[0].shape[1] + 2 * kept * block * block,
            transcendentals=0,
        ),
        name="act_partials",
    )(place, cols, *chunks, *weights)


def put_kernel(count, place_ref, *refs):
    ins, out_ref, sems = refs[:count], refs[-2], refs[-1]
    copies = []
    for index, ref in enumerate(ins):
        tok, span = ref.shape
        into = out_ref.at[
            pl.ds(pl.multiple_of(place_ref[count + index] * tok, tok), tok),
            pl.ds(pl.multiple_of(place_ref[index] * span, span), span),
        ]
        copies.append(pltpu.make_async_copy(ref, into, sems.at[index]))
        copies[-1].start()
    for copy in copies:
        copy.wait()


def put_units(units, parts, arrays, whole, shape):
    given = [] if whole is None else [whole]
    count = len(arrays)
    return pl.pallas_call(
        functools.partial(put_kernel, count),
        out_shape=jax.ShapeDtypeStruct(shape, jnp.bfloat16),
        grid_spec=pltpu.PrefetchScalarGridSpec(
            num_scalar_prefetch=1,
            grid=(1,),
            in_specs=[pl.BlockSpec(array.shape, lambda s, *_: (0, 0)) for array in arrays]
            + [pl.BlockSpec(memory_space=pl.ANY)] * len(given),
            out_specs=pl.BlockSpec(memory_space=pl.ANY),
            scratch_shapes=[pltpu.SemaphoreType.DMA((count,))],
        ),
        input_output_aliases={count + 1: 0} if given else {},
        cost_estimate=pl.CostEstimate(
            flops=0, bytes_accessed=4 * count * arrays[0].size, transcendentals=0
        ),
        name="put_units",
    )(jnp.stack(units + parts).astype(jnp.int32), *arrays, *given)


def add_up(left, right):
    return (left.astype(jnp.float32) + right.astype(jnp.float32)).astype(jnp.bfloat16)


def after(value, *others):
    return lax.optimization_barrier((value, *others))[0]


def local_bits(*arrays):
    return local_bits_body(*arrays)


def local_bits_body(activations, pre_act, grad_act, kept_weight, block_cols):
    block = kept_weight.shape[-1]
    tok, width = activations.shape
    dp_size, tensor_size = lax.axis_size("dp"), lax.axis_size("tensor")
    kept = kept_weight.shape[1]
    cols = block_cols[0]
    per_row = cols.shape[0] // (width // block)
    rows = kept // per_row
    span = rows * block
    grad_scale = 1.0 / math.sqrt(tok * dp_size)
    place = lax.axis_index("dp")
    near = (place // NEAR) % 2
    t_place = lax.axis_index("tensor")
    core = t_place % 2

    def swap(value, bits):
        return lax.ppermute(value, "dp", [(d, d ^ bits) for d in range(dp_size)])

    def partner(value, bit):
        return lax.ppermute(value, "tensor", [(t, t ^ bit) for t in range(tensor_size)])

    hid_own, hid_side, hid_far = [], [], []
    cut = 0
    for part in CHUNKS:
        rows_of = slice(cut, cut + part * tok // sum(CHUNKS))
        cut = rows_of.stop
        pre_part = after(pre_act[rows_of], *hid_own[-1:])
        index = len(hid_own)
        hid_own.append(hidden_gradient(pre_part, grad_act[rows_of]))
        if not hid_far:
            hid_far.append(swap(hid_own[0], FAR))
        hid_side.append(swap(hid_own[-1], SIDE))

    share = tok // tensor_size
    mine_share = lax.dynamic_slice_in_dim(activations, t_place * share, share, 0)
    mine_share = after(mine_share, hid_own[-1])

    def share_for(bits):
        wanted = (place ^ bits) & (FAR | SIDE)
        options = [
            jnp.concatenate(
                [
                    mine_share[:, (base + NEAR * j) * span : (base + NEAR * j + 1) * span]
                    for j in range(2)
                ],
                axis=1,
            )
            for base in SETS
        ]
        chosen = options[0]
        for base, option in zip(SETS[1:], options[1:]):
            chosen = jnp.where(wanted == base, option, chosen)
        return chosen

    shares = [swap(share_for(bits), bits) for bits in SETS[1:]]
    own_weight = kept_weight[0]
    near_weight = swap(after(own_weight, hid_own[-1]), NEAR)
    pieces = {0: jnp.concatenate(shares, axis=1)}
    bit = tensor_size // 2
    while bit:
        held = sorted(pieces)
        got = partner(jnp.concatenate([pieces[k] for k in held], axis=0), bit)
        for index, k in enumerate(held):
            pieces[k ^ bit] = got[index * share : (index + 1) * share]
        bit //= 2
    their_acts = jnp.zeros((tok, 3 * 2 * span), activations.dtype)
    for k, value in pieces.items():
        their_acts = lax.dynamic_update_slice_in_dim(
            their_acts, value, (t_place ^ k) * share, 0
        )
    own_acts = (activations, None)
    set_acts = [(their_acts, s) for s in range(3)]

    near_place = jnp.stack([place ^ NEAR, 1 - near]).astype(jnp.int32)
    own_place = jnp.stack([place, near]).astype(jnp.int32)
    act_place = jnp.stack([place & (FAR | SIDE), near, core]).astype(jnp.int32)
    terms = functools.partial(
        weight_terms,
        cols=cols,
        first_row=0,
        count=rows,
        rows=rows,
        per_row=per_row,
        block=block,
        grad_scale=grad_scale,
    )
    first_terms = functools.partial(
        terms, acts=[own_acts, set_acts[0]], hids=[hid_own, hid_side], acc=None, kind=jnp.float32
    )
    weights = (own_weight, near_weight)

    def acts_of(hids, *others):
        return act_partials(after(act_place, *others), cols, hids, weights, rows, per_row)

    def core_sum(keep, give):
        return add_up(keep, partner(give, 1))

    def rest_sum(half, first_bit):
        bit = first_bit
        while bit < tensor_size:
            half = add_up(half, partner(half, bit))
            bit *= 2
        return half

    hid_both = [swap(hid_far[0], SIDE)]
    hid_far.append(swap(after(hid_own[1], hid_far[0]), FAR))
    near_sum = first_terms(after(near_place, hid_far[1]))
    own_sum = first_terms(after(own_place, near_sum))
    hid_both.append(swap(hid_far[1], SIDE))
    hid_far.append(swap(after(hid_own[2], hid_far[1]), FAR))
    third = after(hid_far[2], own_sum)
    hid_both.append(swap(third, SIDE))
    hid_far.append(swap(after(hid_own[3], third), FAR))
    first_acts = acts_of([hid_own, hid_side], third)
    halves = [rest_sum(core_sum(first_acts[2 * k], first_acts[2 * k + 1]), 2) for k in range(2)]
    fourth = after(hid_far[3], *halves)
    hid_both.append(swap(fourth, SIDE))
    far_acts = acts_of([hid_far], fourth)
    far_core = core_sum(far_acts[0], far_acts[1])

    sent = terms(
        after(near_place, far_core),
        acts=[set_acts[1], set_acts[2]],
        hids=[hid_far, hid_both],
        acc=near_sum,
        kind=jnp.bfloat16,
    )
    came = swap(sent, NEAR)
    both_acts = acts_of([hid_both], sent)
    both_core = core_sum(both_acts[0], both_acts[1])
    halves.append(rest_sum(far_core, 2))

    turn = (t_place // 2) % 2
    cut = tok // 2
    quarter = add_up(
        lax.dynamic_slice_in_dim(both_core, turn * cut, cut, 0),
        partner(lax.dynamic_slice_in_dim(both_core, (1 - turn) * cut, cut, 0), 2),
    )
    quarter = swap(rest_sum(quarter, 4), FAR | SIDE)
    quarters = [quarter, partner(quarter, 2)]

    own_sum = terms(
        after(own_place, both_core),
        acts=[set_acts[1], set_acts[2]],
        hids=[hid_far, hid_both],
        acc=own_sum,
        kind=jnp.float32,
    )
    weight_grad = (own_sum + came.astype(jnp.float32)).astype(jnp.bfloat16)

    unit = (place & (FAR | SIDE)) + NEAR * core
    mine = [halves[0], swap(halves[1], SIDE), swap(halves[2], FAR)]
    other = [partner(half, 1) for half in mine]
    units = [unit ^ bits for bits in SETS[:3]]
    whole = put_units(
        units + [u ^ NEAR for u in units], [core * 0] * 6, mine + other, None, activations.shape
    )
    last = unit ^ SETS[3]
    act_grad = put_units(
        [last, last, last ^ NEAR, last ^ NEAR],
        [turn, 1 - turn] * 2,
        quarters + [partner(value, 1) for value in quarters],
        whole,
        activations.shape,
    )
    return (weight_grad[None], act_grad)


def fits_bits(mesh, activations, kept_weight):
    dp_size, tensor_size = mesh.shape["dp"], mesh.shape["tensor"]
    block = kept_weight.shape[-1]
    kept_all = kept_weight.shape[1]
    per_row = kept_all // (activations.shape[1] // block)
    return (
        dp_size == 2 * FAR
        and tensor_size >= 4
        and tensor_size & (tensor_size - 1) == 0
        and kept_all % (dp_size * per_row) == 0
        and activations.shape[0] % (dp_size * tensor_size * 16) == 0
        and activations.shape[0] % (dp_size * sum(CHUNKS) * 16) == 0
        and activations.shape[0] // dp_size <= 512
    )


def solution(mesh):
    def whole(activations, pre_act, grad_act, kept_weight, block_cols):
        fits = fits_bits(mesh, activations, kept_weight)
        return jax.shard_map(
            local_bits if fits else local_any,
            mesh=mesh,
            in_specs=(
                P("dp", None),
                P("dp", "tensor"),
                P("dp", "tensor"),
                P("tensor", "dp", None, None),
                P("tensor", None),
            ),
            out_specs=(P("tensor", "dp", None, None), P("dp", None)),
            check_vma=False,
        )(activations, pre_act, grad_act, kept_weight, block_cols)

    return whole
```

profile of v0, /device:TPU:0, one launch (start us, length us, event | category | flops | bytes accessed | tf_op | source)
XLA Modules:
  0.0 394.0 jit_solution(3039841477836768907)
XLA Ops:
  4.8 3.9 fusion.17.refs_3_.refs_1_
  23.0 12.0 %collective-permute-done.4 = bf16[64,1536]{1,0:T(8,128)(2,1)S(1)} collective-permute-done((bf16[64,1536]{1,0:T(8,128)(2,1)S(1)}, bf16[64,1536]{1,0:T(8,128)(2,1)S(1)}, u32[]{:S(2)}, u32[]{:S(2)}) %collective-permute-start.4) | collective-permute-done | bytes 196640 | tf_op jit(solution)/shard_map/ppermute | solution.py:314
  44.4 7.9 %collective-permute-done.6 = bf16[64,4608]{1,0:T(8,128)(2,1)S(1)} collective-permute-done((bf16[64,4608]{1,0:T(8,128)(2,1)S(1)}, bf16[64,4608]{1,0:T(8,128)(2,1)S(1)}, u32[]{:S(2)}, u32[]{:S(2)}) %collective-permute-start.6) | collective-permute-done | bytes 589856 | tf_op jit(solution)/shard_map/ppermute | solution.py:317
  56.0 36.5 %collective-permute-done.refs_0_.refs_2_ = bf16[96,6144]{1,0:T(8,128)(2,1)} collective-permute-done((bf16[96,6144]{1,0:T(8,128)(2,1)S(1)}, bf16[96,6144]{1,0:T(8,128)(2,1)}, u32[]{:S(2)}, u32[]{:S(2)}) %collective-permute-start) | collective-permute-done | bytes 1179680 | tf_op jit(solution)/shard_map/ppermute | solution.py:314
  95.4 67.6 %collective-permute-done.1.refs_1_.refs_3_ = bf16[80,6144]{1,0:T(8,128)(2,1)S(1)} collective-permute-done((bf16[80,6144]{1,0:T(8,128)(2,1)}, bf16[80,6144]{1,0:T(8,128)(2,1)S(1)}, u32[]{:S(2)}, u32[]{:S(2)}) %collective-permute-start.1) | collective-permute-done | bytes 983072 | tf_op jit(solution)/shard_map/ppermute | solution.py:314
  169.0 7.1 %collective-permute-done.10.refs_8_.refs_6_ = bf16[48,6144]{1,0:T(8,128)(2,1)S(1)} collective-permute-done((bf16[48,6144]{1,0:T(8,128)(2,1)}, bf16[48,6144]{1,0:T(8,128)(2,1)S(1)}, u32[]{:S(2)}, u32[]{:S(2)}) %collective-permute-start.10) | collective-permute-done | bytes 589856 | tf_op jit(solution)/shard_map/ppermute | solution.py:314
  176.9 9.4 %weight_terms.4.refs_10_ = f32[72,128,128]{2,1,0:T(8,128)} custom-call(s32[2]{0:T(128)} %pad_add_fusion.2.place_ref, s32[576]{0:T(1024)} %reduce.cols_ref, bf16[256,6144]{1,0:T(8,128)(2,1)} %refs_0_.3, bf16[256,4608]{1,0:T(8,128)(2,1)} %copy-done, bf16[96,6144]{1,0:T(8,128)(2,1)} %copy-done.1, bf16[80,6144]{1,0:T(8,128)(2,1)} %fusion.17.refs_3_.refs_1_, ...), custom_call_target="tpu_custom_call" | custom-call | flops 1207959552 | bytes 15728640 | tf_op jit(solution)/shard_map/weight_terms/pallas_call | solution.py:150
  186.3 9.2 %weight_terms.5.refs_10_ = f32[72,128,128]{2,1,0:T(8,128)} custom-call(s32[2]{0:T(128)} %pad_add_fusion.place_ref, s32[576]{0:T(1024)} %reduce.cols_ref, bf16[256,6144]{1,0:T(8,128)(2,1)} %refs_0_.3, bf16[256,4608]{1,0:T(8,128)(2,1)} %copy-done, bf16[96,6144]{1,0:T(8,128)(2,1)} %copy-done.1, bf16[80,6144]{1,0:T(8,128)(2,1)} %fusion.17.refs_3_.refs_1_, ...), custom_call_target="tpu_custom_call" | custom-call | flops 1207959552 | bytes 15728640 | tf_op jit(solution)/shard_map/weight_terms/pallas_call | solution.py:150
  195.5 13.8 %act_partials.3 = (bf16[256,768]{1,0:T(8,128)(2,1)}, bf16[256,768]{1,0:T(8,128)(2,1)}, bf16[256,768]{1,0:T(8,128)(2,1)}, bf16[256,768]{1,0:T(8,128)(2,1)}) custom-call(s32[3]{0:T(128)} %pad_add_fusion.1.place_ref, s32[576]{0:T(1024)} %reduce.cols_ref, bf16[96,6144]{1,0:T(8,128)(2,1)} %copy-done.1, bf16[80,6144]{1,0:T(8,128)(2,1)} %fusion.17.refs_3_.refs_1_, ...), custom_call_target="tpu_custom_call" | custom-call | flops 2415919104 | bytes 11010048 | tf_op jit(solution)/shard_map/act_partials/pallas_call | solution.py:226
  225.2 6.7 %collective-permute-done.17 = bf16[256,768]{1,0:T(8,128)(2,1)S(1)} collective-permute-done((bf16[256,768]{1,0:T(8,128)(2,1)S(1)}, bf16[256,768]{1,0:T(8,128)(2,1)S(1)}, u32[]{:S(2)}, u32[]{:S(2)}) %collective-permute-start.17) | collective-permute-done | bytes 393248 | tf_op jit(solution)/shard_map/ppermute | solution.py:317
  232.8 5.0 %collective-permute-done.12.refs_3_.refs_5_ = bf16[32,6144]{1,0:T(8,128)(2,1)S(1)} collective-permute-done((bf16[32,6144]{1,0:T(8,128)(2,1)}, bf16[32,6144]{1,0:T(8,128)(2,1)S(1)}, u32[]{:S(2)}, u32[]{:S(2)}) %collective-permute-start.12) | collective-permute-done | bytes 393248 | tf_op jit(solution)/shard_map/ppermute | solution.py:314
  238.6 9.9 %act_partials.4 = (bf16[256,768]{1,0:T(8,128)(2,1)}, bf16[256,768]{1,0:T(8,128)(2,1)}) custom-call(s32[3]{0:T(128)} %pad_add_fusion.1.place_ref, s32[576]{0:T(1024)} %reduce.cols_ref, bf16[96,6144]{1,0:T(8,128)(2,1)} %collective-permute-done.refs_0_.refs_2_, bf16[80,6144]{1,0:T(8,128)(2,1)} %copy-done.3, ...), custom_call_target="tpu_custom_call" | custom-call | flops 1207959552 | bytes 7864320 | tf_op jit(solution)/shard_map/act_partials/pallas_call | solution.py:226
  252.5 13.2 %collective-permute-done.20.refs_7_.refs_1_ = bf16[80,6144]{1,0:T(8,128)(2,1)S(1)} collective-permute-done((bf16[80,6144]{1,0:T(8,128)(2,1)S(1)}, bf16[80,6144]{1,0:T(8,128)(2,1)S(1)}, u32[]{:S(2)}, u32[]{:S(2)}) %collective-permute-start.20) | collective-permute-done | bytes 983072 | tf_op jit(solution)/shard_map/ppermute | solution.py:314
  265.7 12.7 %collective-permute-done.21.refs_8_.refs_2_ = bf16[48,6144]{1,0:T(8,128)(2,1)} collective-permute-done((bf16[48,6144]{1,0:T(8,128)(2,1)}, bf16[48,6144]{1,0:T(8,128)(2,1)}, u32[]{:S(2)}, u32[]{:S(2)}) %collective-permute-start.21) | collective-permute-done | bytes 589856 | tf_op jit(solution)/shard_map/ppermute | solution.py:314
  278.5 6.9 %collective-permute-done.22.refs_9_.refs_3_ = bf16[32,6144]{1,0:T(8,128)(2,1)S(1)} collective-permute-done((bf16[32,6144]{1,0:T(8,128)(2,1)}, bf16[32,6144]{1,0:T(8,128)(2,1)S(1)}, u32[]{:S(2)}, u32[]{:S(2)}) %collective-permute-start.22) | collective-permute-done | bytes 393248 | tf_op jit(solution)/shard_map/ppermute | solution.py:314
  286.1 9.5 %weight_terms.6 = bf16[72,128,128]{2,1,0:T(8,128)(2,1)} custom-call(s32[2]{0:T(128)} %pad_add_fusion.2.place_ref, s32[576]{0:T(1024)} %reduce.cols_ref, bf16[256,4608]{1,0:T(8,128)(2,1)} %copy-done, bf16[256,4608]{1,0:T(8,128)(2,1)} %copy-done, bf16[96,6144]{1,0:T(8,128)(2,1)} %collective-permute-done.refs_0_.refs_2_, bf16[80,6144]{1,0:T(8,128)(2,1)} %copy-done.3, ...), custom_call_target="tpu_custom_call" | custom-call | flops 1207959552 | bytes 15728640 | tf_op jit(solution)/shard_map/weight_terms/pallas_call | solution.py:150
  295.6 6.6 %collective-permute-start.24 = (bf16[72,128,128]{2,1,0:T(8,128)(2,1)}, bf16[72,128,128]{2,1,0:T(8,128)(2,1)S(1)}, u32[]{:S(2)}, u32[]{:S(2)}) collective-permute-start(bf16[72,128,128]{2,1,0:T(8,128)(2,1)} %weight_terms.6), channel_id=1, source_target_pairs={{0,8},{4,12},{8,0},{12,4},{16,24},{20,28},{24,16},{28,20},{1,9},{5... | collective-permute-start | bytes 7077896 | tf_op jit(solution)/shard_map/ppermute | solution.py:314
  302.2 9.9 %act_partials.5 = (bf16[256,768]{1,0:T(8,128)(2,1)}, bf16[256,768]{1,0:T(8,128)(2,1)}) custom-call(s32[3]{0:T(128)} %pad_add_fusion.1.place_ref, s32[576]{0:T(1024)} %reduce.cols_ref, bf16[96,6144]{1,0:T(8,128)(2,1)} %copy-done.2, bf16[80,6144]{1,0:T(8,128)(2,1)} %copy-done.5, bf16[48,6144]{1,0:T(8,128)(2,1)} %collective-permute-done.21.refs_8_.refs_2_, ...), custom_call_target="tpu_custom_call" | custom-call | flops 1207959552 | bytes 7864320 | tf_op jit(solution)/shard_map/act_partials/pallas_call | solution.py:226
  317.1 7.3 %collective-permute-done.31 = bf16[256,768]{1,0:T(8,128)(2,1)} collective-permute-done((bf16[256,768]{1,0:T(8,128)(2,1)S(1)}, bf16[256,768]{1,0:T(8,128)(2,1)}, u32[]{:S(2)}, u32[]{:S(2)}) %collective-permute-start.31) | collective-permute-done | bytes 393248 | tf_op jit(solution)/shard_map/ppermute | solution.py:317
  329.5 32.8 %collective-permute-done.32.refs_2_ = bf16[256,768]{1,0:T(8,128)(2,1)S(1)} collective-permute-done((bf16[256,768]{1,0:T(8,128)(2,1)S(1)}, bf16[256,768]{1,0:T(8,128)(2,1)S(1)}, u32[]{:S(2)}, u32[]{:S(2)}) %collective-permute-start.32) | collective-permute-done | bytes 393248 | tf_op jit(solution)/shard_map/ppermute | solution.py:314
  365.7 4.8 %collective-permute-done.27.refs_1_ = bf16[128,768]{1,0:T(8,128)(2,1)} collective-permute-done((bf16[128,768]{1,0:T(8,128)(2,1)}, bf16[128,768]{1,0:T(8,128)(2,1)}, u32[]{:S(2)}, u32[]{:S(2)}) %collective-permute-start.27) | collective-permute-done | bytes 196640 | tf_op jit(solution)/shard_map/ppermute | solution.py:317
  371.7 9.9 %weight_terms.7 = f32[72,128,128]{2,1,0:T(8,128)} custom-call(s32[2]{0:T(128)} %pad_add_fusion.place_ref, s32[576]{0:T(1024)} %reduce.cols_ref, bf16[256,4608]{1,0:T(8,128)(2,1)} %copy-done, bf16[256,4608]{1,0:T(8,128)(2,1)} %copy-done, bf16[96,6144]{1,0:T(8,128)(2,1)} %collective-permute-done.refs_0_.refs_2_, bf16[80,6144]{1,0:T(8,128)(2,1)} %copy-done.3, ...), custom_call_target="tpu_custom_call" | custom-call | flops 1207959552 | bytes 15728640 | tf_op jit(solution)/shard_map/weight_terms/pallas_call | solution.py:150
  381.6 3.7 put_units.2.refs_4_
  389.5 4.5 %fusion.12 = bf16[1,72,128,128]{3,2,1,0:T(8,128)(2,1)} fusion(f32[72,128,128]{2,1,0:T(8,128)} %weight_terms.7, bf16[72,128,128]{2,1,0:T(8,128)(2,1)S(1)} %collective-permute-done.24), kind=kLoop, calls=%fused_computation.21 | loop fusion | flops 3538944 | bytes 9437184 | tf_op jit(solution)/shard_map/broadcast_in_dim | solution.py:463
  (143 shorter events, 82.1 us)
Async XLA Ops:
  18.1 16.9 %collective-permute-start.4 = (bf16[64,1536]{1,0:T(8,128)(2,1)S(1)}, bf16[64,1536]{1,0:T(8,128)(2,1)S(1)}, u32[]{:S(2)}, u32[]{:S(2)}) collective-permute-start(bf16[64,1536]{1,0:T(8,128)(2,1)S(1)} %select_select_fusion.1), channel_id=1, source_target_pairs={{0,16},{4,20},{8,24},{12,28},{16,0},{20,4},{24,8},{28,12},{1,17},{... | collective-permute-start | bytes 589832 | tf_op jit(solution)/shard_map/ppermute | solution.py:314
  20.9 17.1 %collective-permute-start.5 = (bf16[64,1536]{1,0:T(8,128)(2,1)S(1)}, bf16[64,1536]{1,0:T(8,128)(2,1)S(1)}, u32[]{:S(2)}, u32[]{:S(2)}) collective-permute-start(bf16[64,1536]{1,0:T(8,128)(2,1)S(1)} %select_select_fusion), channel_id=1, source_target_pairs={{0,20},{4,16},{8,28},{12,24},{16,4},{20,0},{24,12},{28,8},{1,21},{... | collective-permute-start | bytes 589832 | tf_op jit(solution)/shard_map/ppermute | solution.py:314
  39.7 52.9 %collective-permute-start = (bf16[96,6144]{1,0:T(8,128)(2,1)S(1)}, bf16[96,6144]{1,0:T(8,128)(2,1)}, u32[]{:S(2)}, u32[]{:S(2)}) collective-permute-start(bf16[96,6144]{1,0:T(8,128)(2,1)S(1)} %fusion.6.refs_2_.refs_0_), channel_id=1, source_target_pairs={{0,16},{4,20},{8,24},{12,28},{16,0},{20,4},{24,8},{28,12},{1,17},{... | collective-permute-start | bytes 3538952 | tf_op jit(solution)/shard_map/ppermute | solution.py:314
  39.7 137.2 %collective-permute-start.8 = (bf16[96,6144]{1,0:T(8,128)(2,1)S(1)}, bf16[96,6144]{1,0:T(8,128)(2,1)}, u32[]{:S(2)}, u32[]{:S(2)}) collective-permute-start(bf16[96,6144]{1,0:T(8,128)(2,1)S(1)} %fusion.6.refs_2_.refs_0_), channel_id=1, source_target_pairs={{0,4},{4,0},{8,12},{12,8},{16,20},{20,16},{24,28},{28,24},{1,5},{5... | collective-permute-start | bytes 3538952 | tf_op jit(solution)/shard_map/ppermute | solution.py:314
  41.2 135.7 %collective-permute-start.9 = (bf16[80,6144]{1,0:T(8,128)(2,1)}, bf16[80,6144]{1,0:T(8,128)(2,1)}, u32[]{:S(2)}, u32[]{:S(2)}) collective-permute-start(bf16[80,6144]{1,0:T(8,128)(2,1)} %fusion.17.refs_3_.refs_1_), channel_id=1, source_target_pairs={{0,4},{4,0},{8,12},{12,8},{16,20},{20,16},{24,28},{28,24},{1,5},{5... | collective-permute-start | bytes 2949128 | tf_op jit(solution)/shard_map/ppermute | solution.py:314
  41.7 122.8 %collective-permute-start.11 = (bf16[32,6144]{1,0:T(8,128)(2,1)}, bf16[32,6144]{1,0:T(8,128)(2,1)}, u32[]{:S(2)}, u32[]{:S(2)}) collective-permute-start(bf16[32,6144]{1,0:T(8,128)(2,1)} %fusion.39.refs_5_.refs_3_), channel_id=1, source_target_pairs={{0,4},{4,0},{8,12},{12,8},{16,20},{20,16},{24,28},{28,24},{1,5},{5... | collective-permute-start | bytes 1179656 | tf_op jit(solution)/shard_map/ppermute | solution.py:314
  53.5 39.0 %collective-permute-start.7 = (bf16[128,4608]{1,0:T(8,128)(2,1)}, bf16[128,4608]{1,0:T(8,128)(2,1)}, u32[]{:S(2)}, u32[]{:S(2)}) collective-permute-start(bf16[128,4608]{1,0:T(8,128)(2,1)} %pad_maximum_fusion), channel_id=1, source_target_pairs={{0,1},{1,0},{2,3},{3,2},{4,5},{5,4},{6,7},{7,6},{8,9},{9,8},{10,11... | collective-permute-start | bytes 3538952 | tf_op jit(solution)/shard_map/ppermute | solution.py:317
  92.6 102.9 %collective-permute-start.13 = (bf16[72,128,128]{2,1,0:T(8,128)(2,1)}, bf16[72,128,128]{2,1,0:T(8,128)(2,1)}, u32[]{:S(2)}, u32[]{:S(2)}) collective-permute-start(bf16[72,128,128]{2,1,0:T(8,128)(2,1)} %bitcast.6.refs_8_.refs_4_), channel_id=1, source_target_pairs={{0,8},{4,12},{8,0},{12,4},{16,24},{20,28},{24,16},{28,20},{1,9},{5... | collective-permute-start | bytes 7077896 | tf_op jit(solution)/shard_map/ppermute | solution.py:314
  92.6 70.5 %collective-permute-start.1 = (bf16[80,6144]{1,0:T(8,128)(2,1)}, bf16[80,6144]{1,0:T(8,128)(2,1)S(1)}, u32[]{:S(2)}, u32[]{:S(2)}) collective-permute-start(bf16[80,6144]{1,0:T(8,128)(2,1)} %fusion.17.refs_3_.refs_1_), channel_id=1, source_target_pairs={{0,16},{4,20},{8,24},{12,28},{16,0},{20,4},{24,8},{28,12},{1,17},{... | collective-permute-start | bytes 2949128 | tf_op jit(solution)/shard_map/ppermute | solution.py:314
  164.6 30.9 %collective-permute-start.2 = (bf16[48,6144]{1,0:T(8,128)(2,1)}, bf16[48,6144]{1,0:T(8,128)(2,1)}, u32[]{:S(2)}, u32[]{:S(2)}) collective-permute-start(bf16[48,6144]{1,0:T(8,128)(2,1)} %fusion.28.refs_4_.refs_2_), channel_id=1, source_target_pairs={{0,16},{4,20},{8,24},{12,28},{16,0},{20,4},{24,8},{28,12},{1,17},{... | collective-permute-start | bytes 1769480 | tf_op jit(solution)/shard_map/ppermute | solution.py:314
  213.8 18.1 %collective-permute-start.17 = (bf16[256,768]{1,0:T(8,128)(2,1)S(1)}, bf16[256,768]{1,0:T(8,128)(2,1)S(1)}, u32[]{:S(2)}, u32[]{:S(2)}) collective-permute-start(bf16[256,768]{1,0:T(8,128)(2,1)S(1)} %add_convert_fusion.5), channel_id=1, source_target_pairs={{0,2},{1,3},{2,0},{3,1},{4,6},{5,7},{6,4},{7,5},{8,10},{9,11},{10,... | collective-permute-start | bytes 1179656 | tf_op jit(solution)/shard_map/ppermute | solution.py:317
  215.6 36.9 %collective-permute-start.19 = (bf16[96,6144]{1,0:T(8,128)(2,1)}, bf16[96,6144]{1,0:T(8,128)(2,1)S(1)}, u32[]{:S(2)}, u32[]{:S(2)}) collective-permute-start(bf16[96,6144]{1,0:T(8,128)(2,1)} %collective-permute-done.refs_0_.refs_2_), channel_id=1, source_target_pairs={{0,4},{4,0},{8,12},{12,8},{16,20},{20,16},{24,28},{28,24},{1,5},{5... | collective-permute-start | bytes 3538952 | tf_op jit(solution)/shard_map/ppermute | solution.py:314
  217.1 48.6 %collective-permute-start.20 = (bf16[80,6144]{1,0:T(8,128)(2,1)S(1)}, bf16[80,6144]{1,0:T(8,128)(2,1)S(1)}, u32[]{:S(2)}, u32[]{:S(2)}) collective-permute-start(bf16[80,6144]{1,0:T(8,128)(2,1)S(1)} %copy-done.4), channel_id=1, source_target_pairs={{0,4},{4,0},{8,12},{12,8},{16,20},{20,16},{24,28},{28,24},{1,5},{5... | collective-permute-start | bytes 2949128 | tf_op jit(solution)/shard_map/ppermute | solution.py:314
  217.6 20.2 %collective-permute-start.12 = (bf16[32,6144]{1,0:T(8,128)(2,1)}, bf16[32,6144]{1,0:T(8,128)(2,1)S(1)}, u32[]{:S(2)}, u32[]{:S(2)}) collective-permute-start(bf16[32,6144]{1,0:T(8,128)(2,1)} %fusion.39.refs_5_.refs_3_), channel_id=1, source_target_pairs={{0,16},{4,20},{8,24},{12,28},{16,0},{20,4},{24,8},{28,12},{1,17},{... | collective-permute-start | bytes 1179656 | tf_op jit(solution)/shard_map/ppermute | solution.py:314
  248.5 29.9 %collective-permute-start.21 = (bf16[48,6144]{1,0:T(8,128)(2,1)}, bf16[48,6144]{1,0:T(8,128)(2,1)}, u32[]{:S(2)}, u32[]{:S(2)}) collective-permute-start(bf16[48,6144]{1,0:T(8,128)(2,1)} %collective-permute-done.2.refs_2_.refs_4_), channel_id=1, source_target_pairs={{0,4},{4,0},{8,12},{12,8},{16,20},{20,16},{24,28},{28,24},{1,5},{5... | collective-permute-start | bytes 1769480 | tf_op jit(solution)/shard_map/ppermute | solution.py:314
  250.1 35.3 %collective-permute-start.22 = (bf16[32,6144]{1,0:T(8,128)(2,1)}, bf16[32,6144]{1,0:T(8,128)(2,1)S(1)}, u32[]{:S(2)}, u32[]{:S(2)}) collective-permute-start(bf16[32,6144]{1,0:T(8,128)(2,1)} %copy-done.7), channel_id=1, source_target_pairs={{0,4},{4,0},{8,12},{12,8},{16,20},{20,16},{24,28},{28,24},{1,5},{5... | collective-permute-start | bytes 1179656 | tf_op jit(solution)/shard_map/ppermute | solution.py:314
  295.6 93.9 %collective-permute-start.24 = (bf16[72,128,128]{2,1,0:T(8,128)(2,1)}, bf16[72,128,128]{2,1,0:T(8,128)(2,1)S(1)}, u32[]{:S(2)}, u32[]{:S(2)}) collective-permute-start(bf16[72,128,128]{2,1,0:T(8,128)(2,1)} %weight_terms.6), channel_id=1, source_target_pairs={{0,8},{4,12},{8,0},{12,4},{16,24},{20,28},{24,16},{28,20},{1,9},{5... | collective-permute-start | bytes 7077896 | tf_op jit(solution)/shard_map/ppermute | solution.py:314
  312.8 16.8 %collective-permute-start.30 = (bf16[256,768]{1,0:T(8,128)(2,1)}, bf16[256,768]{1,0:T(8,128)(2,1)S(1)}, u32[]{:S(2)}, u32[]{:S(2)}) collective-permute-start(bf16[256,768]{1,0:T(8,128)(2,1)} %add_convert_fusion.4), channel_id=1, source_target_pairs={{0,4},{4,0},{8,12},{12,8},{16,20},{20,16},{24,28},{28,24},{1,5},{5... | collective-permute-start | bytes 1179656 | tf_op jit(solution)/shard_map/ppermute | solution.py:314
  314.3 50.7 %collective-permute-start.33 = (bf16[256,768]{1,0:T(8,128)(2,1)S(1)}, bf16[256,768]{1,0:T(8,128)(2,1)S(1)}, u32[]{:S(2)}, u32[]{:S(2)}) collective-permute-start(bf16[256,768]{1,0:T(8,128)(2,1)S(1)} %copy-done.13), channel_id=1, source_target_pairs={{0,1},{1,0},{2,3},{3,2},{4,5},{5,4},{6,7},{7,6},{8,9},{9,8},{10,11... | collective-permute-start | bytes 1179656 | tf_op jit(solution)/shard_map/ppermute | solution.py:317
  325.5 36.9 %collective-permute-start.32 = (bf16[256,768]{1,0:T(8,128)(2,1)S(1)}, bf16[256,768]{1,0:T(8,128)(2,1)S(1)}, u32[]{:S(2)}, u32[]{:S(2)}) collective-permute-start(bf16[256,768]{1,0:T(8,128)(2,1)S(1)} %add_convert_fusion.1), channel_id=1, source_target_pairs={{0,16},{4,20},{8,24},{12,28},{16,0},{20,4},{24,8},{28,12},{1,17},{... | collective-permute-start | bytes 1179656 | tf_op jit(solution)/shard_map/ppermute | solution.py:314
  328.0 36.5 %collective-permute-start.26 = (bf16[128,768]{1,0:T(8,128)(2,1)S(1)}, bf16[128,768]{1,0:T(8,128)(2,1)}, u32[]{:S(2)}, u32[]{:S(2)}) collective-permute-start(bf16[128,768]{1,0:T(8,128)(2,1)S(1)} %add_convert_fusion.8), channel_id=1, source_target_pairs={{0,20},{4,16},{8,28},{12,24},{16,4},{20,0},{24,12},{28,8},{1,21},{... | collective-permute-start | bytes 589832 | tf_op jit(solution)/shard_map/ppermute | solution.py:314
  329.5 52.1 %collective-permute-start.34 = (bf16[256,768]{1,0:T(8,128)(2,1)S(1)}, bf16[256,768]{1,0:T(8,128)(2,1)}, u32[]{:S(2)}, u32[]{:S(2)}) collective-permute-start(bf16[256,768]{1,0:T(8,128)(2,1)S(1)} %collective-permute-done.30.refs_1_), channel_id=1, source_target_pairs={{0,1},{1,0},{2,3},{3,2},{4,5},{5,4},{6,7},{7,6},{8,9},{9,8},{10,11... | collective-permute-start | bytes 1179656 | tf_op jit(solution)/shard_map/ppermute | solution.py:317
  362.4 19.3 %collective-permute-start.35 = (bf16[256,768]{1,0:T(8,128)(2,1)S(1)}, bf16[256,768]{1,0:T(8,128)(2,1)}, u32[]{:S(2)}, u32[]{:S(2)}) collective-permute-start(bf16[256,768]{1,0:T(8,128)(2,1)S(1)} %collective-permute-done.32.refs_2_), channel_id=1, source_target_pairs={{0,1},{1,0},{2,3},{3,2},{4,5},{5,4},{6,7},{7,6},{8,9},{9,8},{10,11... | collective-permute-start | bytes 1179656 | tf_op jit(solution)/shard_map/ppermute | solution.py:317
  365.7 19.7 %collective-permute-start.28 = (bf16[128,768]{1,0:T(8,128)(2,1)}, bf16[128,768]{1,0:T(8,128)(2,1)S(1)}, u32[]{:S(2)}, u32[]{:S(2)}) collective-permute-start(bf16[128,768]{1,0:T(8,128)(2,1)} %collective-permute-done.26.refs_0_), channel_id=1, source_target_pairs={{0,1},{1,0},{2,3},{3,2},{4,5},{5,4},{6,7},{7,6},{8,9},{9,8},{10,11... | collective-permute-start | bytes 589832 | tf_op jit(solution)/shard_map/ppermute | solution.py:317
  (37 other events, 393.3 us)
where the time goes:
time: 396 us; the launch traced here: 394 us
  waiting for transfers between devices  235 us (59%)
  Pallas kernels  78 us (20%)
  starting transfers between devices  40 us (10%)
  other arithmetic  28.1 us (7%)
  local copies, waits for them, and re-layouts  11.7 us (3%)
    ppermute x20, waiting for transfers between devices, swap(): return lax.ppermute(value, 'dp', [(d, d ^ bits) for d in range(dp_size)])  201 us
    pallas_call x4, Pallas kernels, weight_terms(): pl.pallas_call(functools.partial(weight_term_kernel, per_row, rows, first...  37.9 us
    ppermute x16, waiting for transfers between devices, partner(): lax.ppermute(value, 'tensor', [(t, t ^ bit) for t in range(tensor_size)])  34 us
    pallas_call x3, Pallas kernels, act_partials(): pl.pallas_call(functools.partial(act_kernel, per_row, rows, len(hids), le...  33.5 us
    ppermute x20, starting transfers between devices, swap(): return lax.ppermute(value, 'dp', [(d, d ^ bits) for d in range(dp_size)])  32.9 us
    convert_element_type x4, other arithmetic, hidden_gradient(): (grad_act.astype(jnp.float32) * gelu_slope(pre_act)).astype(jnp.bfloat16)  11.7 us
    convert_element_type x8, other arithmetic, add_up(): (left.astype(jnp.float32) + right.astype(jnp.float32)).astype(jnp.bfloat16)  8.07 us
  transfers between devices with their start and end apart: 36, of which 19 were waited for; matrix products, arithmetic and copies ran while one was open for 4% of the time, Pallas kernels for 14%

commit v1 on v0

--- a/solution.py
+++ b/solution.py
@@ -80,7 +80,7 @@
 
 SIDE, NEAR, FAR = 1, 2, 4
 SETS = (0, SIDE, FAR, FAR | SIDE)
-CHUNKS = (6, 5, 3, 2)
+CHUNKS = (3, 5, 5, 3)
 
 
 def columns_of(chunk_refs, spans):
@@ -133,12 +133,11 @@
     tok = acts[0][0].shape[0]
     step_rows = next(k for k in (3, 2, 1) if count % k == 0)
 
-    def act_spec(kind_of):
-        if kind_of is None:
-            return pl.BlockSpec((tok, rows * block), lambda s, place_ref, _: (0, place_ref[0]))
-        return pl.BlockSpec(
-            (tok, rows * block), lambda s, place_ref, _: (0, kind_of * 2 + place_ref[1])
-        )
+    def act_spec(which):
+        def at(s, place_ref, _):
+            return (0, {"unit": place_ref[0], "near": place_ref[1]}.get(which, which))
+
+        return pl.BlockSpec((tok, rows * block), at)
 
     chunks = [chunk for hid in hids for chunk in hid]
     accs = [] if acc is None else [acc]
@@ -283,6 +282,30 @@
     )(jnp.stack(units + parts).astype(jnp.int32), *arrays, *given)
 
 
+def add_kernel(sum_ref, part_ref, *refs):
+    refs[-1][...] = (sum_ref[...] + part_ref[...].astype(jnp.float32)).astype(jnp.bfloat16)
+
+
+def add_part(total, part, index, size, whole):
+    steps = part.shape[0] // size
+    given = [] if whole is None else [whole]
+    shape = (size, *total.shape[1:])
+    at = pl.BlockSpec(shape, lambda s: (index * steps + s, 0, 0))
+    return pl.pallas_call(
+        add_kernel,
+        out_shape=jax.ShapeDtypeStruct(total.shape, jnp.bfloat16),
+        grid=(steps,),
+        in_specs=[at, pl.BlockSpec(shape, lambda s: (s, 0, 0))]
+        + [pl.BlockSpec(memory_space=pl.ANY)] * len(given),
+        out_specs=at,
+        input_output_aliases={2: 0} if given else {},
+        cost_estimate=pl.CostEstimate(
+            flops=part.size, bytes_accessed=8 * part.size, transcendentals=0
+        ),
+        name="add_part",
+    )(total, part, *given)
+
+
 def add_up(left, right):
     return (left.astype(jnp.float32) + right.astype(jnp.float32)).astype(jnp.bfloat16)
 
@@ -316,73 +339,73 @@
     def partner(value, bit):
         return lax.ppermute(value, "tensor", [(t, t ^ bit) for t in range(tensor_size)])
 
+    share = tok // tensor_size
+
+    def share_of(unit, bits, *others):
+        whole = after(activations, *others)
+        part = lax.dynamic_slice(whole, (t_place * share, unit * span), (share, span))
+        return swap(part, bits)
+
+    def gathered(parts, *others):
+        pieces = {0: jnp.concatenate([after(part, *others) for part in parts], axis=1)}
+        bit = tensor_size // 2
+        while bit:
+            held = sorted(pieces)
+            joined = jnp.concatenate([pieces[k] for k in held], axis=0)
+            got = partner(joined, bit)
+            for index, k in enumerate(held):
+                pieces[k ^ bit] = got[index * share : (index + 1) * share]
+            bit //= 2
+        whole = jnp.zeros((tok, pieces[0].shape[1]), activations.dtype)
+        for k, value in pieces.items():
+            whole = lax.dynamic_update_slice_in_dim(whole, value, (t_place ^ k) * share, 0)
+        return whole
+
     hid_own, hid_side, hid_far = [], [], []
     cut = 0
-    for part in CHUNKS:
+    for index, part in enumerate(CHUNKS):
         rows_of = slice(cut, cut + part * tok // sum(CHUNKS))
         cut = rows_of.stop
         pre_part = after(pre_act[rows_of], *hid_own[-1:])
-        index = len(hid_own)
         hid_own.append(hidden_gradient(pre_part, grad_act[rows_of]))
-        if not hid_far:
-            hid_far.append(swap(hid_own[0], FAR))
+        if index < 2:
+            hid_far.append(swap(hid_own[index], FAR))
         hid_side.append(swap(hid_own[-1], SIDE))
 
-    share = tok // tensor_size
-    mine_share = lax.dynamic_slice_in_dim(activations, t_place * share, share, 0)
-    mine_share = after(mine_share, hid_own[-1])
-
-    def share_for(bits):
-        wanted = (place ^ bits) & (FAR | SIDE)
-        options = [
-            jnp.concatenate(
-                [
-                    mine_share[:, (base + NEAR * j) * span : (base + NEAR * j + 1) * span]
-                    for j in range(2)
-                ],
-                axis=1,
-            )
-            for base in SETS
-        ]
-        chosen = options[0]
-        for base, option in zip(SETS[1:], options[1:]):
-            chosen = jnp.where(wanted == base, option, chosen)
-        return chosen
-
-    shares = [swap(share_for(bits), bits) for bits in SETS[1:]]
+    side_share = lax.dynamic_slice_in_dim(activations, t_place * share, share, 0)
+    options = [
+        jnp.concatenate(
+            [side_share[:, (base + NEAR * j) * span : (base + NEAR * j + 1) * span] for j in (0, 1)],
+            axis=1,
+        )
+        for base in SETS
+    ]
+    wanted = (place ^ SIDE) & (FAR | SIDE)
+    chosen = options[0]
+    for base, option in zip(SETS[1:], options[1:]):
+        chosen = jnp.where(wanted == base, option, chosen)
+    side_acts = gathered([swap(after(chosen, hid_own[0]), SIDE)])
+    near_shares = [
+        share_of(place ^ NEAR ^ FAR, FAR, hid_own[1]),
+        share_of(place ^ NEAR ^ FAR ^ SIDE, FAR | SIDE, hid_own[1]),
+    ]
     own_weight = kept_weight[0]
     near_weight = swap(after(own_weight, hid_own[-1]), NEAR)
-    pieces = {0: jnp.concatenate(shares, axis=1)}
-    bit = tensor_size // 2
-    while bit:
-        held = sorted(pieces)
-        got = partner(jnp.concatenate([pieces[k] for k in held], axis=0), bit)
-        for index, k in enumerate(held):
-            pieces[k ^ bit] = got[index * share : (index + 1) * share]
-        bit //= 2
-    their_acts = jnp.zeros((tok, 3 * 2 * span), activations.dtype)
-    for k, value in pieces.items():
-        their_acts = lax.dynamic_update_slice_in_dim(
-            their_acts, value, (t_place ^ k) * share, 0
-        )
-    own_acts = (activations, None)
-    set_acts = [(their_acts, s) for s in range(3)]
 
     near_place = jnp.stack([place ^ NEAR, 1 - near]).astype(jnp.int32)
     own_place = jnp.stack([place, near]).astype(jnp.int32)
     act_place = jnp.stack([place & (FAR | SIDE), near, core]).astype(jnp.int32)
     terms = functools.partial(
-        weight_terms,
-        cols=cols,
+        weight_terms, cols=cols, rows=rows, per_row=per_row, block=block, grad_scale=grad_scale
+    )
+    first_terms = functools.partial(
+        terms,
+        acts=[(activations, "unit"), (side_acts, "near")],
+        hids=[hid_own, hid_side],
+        acc=None,
         first_row=0,
         count=rows,
-        rows=rows,
-        per_row=per_row,
-        block=block,
-        grad_scale=grad_scale,
-    )
-    first_terms = functools.partial(
-        terms, acts=[own_acts, set_acts[0]], hids=[hid_own, hid_side], acc=None, kind=jnp.float32
+        kind=jnp.float32,
     )
     weights = (own_weight, near_weight)
 
@@ -399,67 +422,83 @@
             bit *= 2
         return half
 
+    turn = (t_place // 2) % 2
+    token_half = tok // 2
+
+    def quarter_sum(half):
+        keep = lax.dynamic_slice_in_dim(half, turn * token_half, token_half, 0)
+        give = lax.dynamic_slice_in_dim(half, (1 - turn) * token_half, token_half, 0)
+        return rest_sum(add_up(keep, partner(give, 2)), 4)
+
     hid_both = [swap(hid_far[0], SIDE)]
-    hid_far.append(swap(after(hid_own[1], hid_far[0]), FAR))
+    hid_far.append(swap(after(hid_own[2], hid_far[0]), FAR))
+    hid_both.append(swap(hid_far[1], SIDE))
+    hid_far.append(swap(after(hid_own[3], hid_far[1]), FAR))
     near_sum = first_terms(after(near_place, hid_far[1]))
     own_sum = first_terms(after(own_place, near_sum))
-    hid_both.append(swap(hid_far[1], SIDE))
-    hid_far.append(swap(after(hid_own[2], hid_far[1]), FAR))
-    third = after(hid_far[2], own_sum)
+    first_acts = acts_of([hid_own, hid_side], own_sum)
+    near_acts = gathered(near_shares, first_acts[0])
+    third = after(hid_far[2], first_acts[0])
     hid_both.append(swap(third, SIDE))
-    hid_far.append(swap(after(hid_own[3], third), FAR))
-    first_acts = acts_of([hid_own, hid_side], third)
+    own_shares = [
+        share_of(place ^ FAR, FAR, third), share_of(place ^ FAR ^ SIDE, FAR | SIDE, third)
+    ]
     halves = [rest_sum(core_sum(first_acts[2 * k], first_acts[2 * k + 1]), 2) for k in range(2)]
-    fourth = after(hid_far[3], *halves)
+    fourth = after(hid_far[3], near_acts, *halves)
     hid_both.append(swap(fourth, SIDE))
     far_acts = acts_of([hid_far], fourth)
     far_core = core_sum(far_acts[0], far_acts[1])
 
-    sent = terms(
-        after(near_place, far_core),
-        acts=[set_acts[1], set_acts[2]],
-        hids=[hid_far, hid_both],
-        acc=near_sum,
-        kind=jnp.bfloat16,
-    )
-    came = swap(sent, NEAR)
-    both_acts = acts_of([hid_both], sent)
+    cuts = 2 if rows % 2 == 0 else 1
+    came, last = [], far_core
+    for k in range(cuts):
+        last = terms(
+            after(near_place, last),
+            acts=[(near_acts, 0), (near_acts, 1)],
+            hids=[hid_far, hid_both],
+            acc=near_sum,
+            first_row=k * (rows // cuts),
+            count=rows // cuts,
+            kind=jnp.bfloat16,
+        )
+        came.append(swap(last, NEAR))
+    both_acts = acts_of([hid_both], last)
     both_core = core_sum(both_acts[0], both_acts[1])
-    halves.append(rest_sum(far_core, 2))
-
-    turn = (t_place // 2) % 2
-    cut = tok // 2
-    quarter = add_up(
-        lax.dynamic_slice_in_dim(both_core, turn * cut, cut, 0),
-        partner(lax.dynamic_slice_in_dim(both_core, (1 - turn) * cut, cut, 0), 2),
-    )
-    quarter = swap(rest_sum(quarter, 4), FAR | SIDE)
-    quarters = [quarter, partner(quarter, 2)]
-
+    quarters = []
+    for half, bits in ((far_core, FAR), (both_core, FAR | SIDE)):
+        quarter = swap(quarter_sum(half), bits)
+        quarters.append([quarter, partner(quarter, 2)])
+
+    own_acts = gathered(own_shares, both_core)
     own_sum = terms(
-        after(own_place, both_core),
-        acts=[set_acts[1], set_acts[2]],
+        own_place,
+        acts=[(own_acts, 0), (own_acts, 1)],
         hids=[hid_far, hid_both],
         acc=own_sum,
+        first_row=0,
+        count=rows,
         kind=jnp.float32,
     )
-    weight_grad = (own_sum + came.astype(jnp.float32)).astype(jnp.bfloat16)
+    weight_grad = None
+    for k, value in enumerate(came):
+        weight_grad = add_part(own_sum, value, k, per_row, weight_grad)
 
     unit = (place & (FAR | SIDE)) + NEAR * core
-    mine = [halves[0], swap(halves[1], SIDE), swap(halves[2], FAR)]
+    mine = [halves[0], swap(halves[1], SIDE)]
     other = [partner(half, 1) for half in mine]
-    units = [unit ^ bits for bits in SETS[:3]]
-    whole = put_units(
-        units + [u ^ NEAR for u in units], [core * 0] * 6, mine + other, None, activations.shape
-    )
-    last = unit ^ SETS[3]
+    units = [unit, unit ^ SIDE]
     act_grad = put_units(
-        [last, last, last ^ NEAR, last ^ NEAR],
-        [turn, 1 - turn] * 2,
-        quarters + [partner(value, 1) for value in quarters],
-        whole,
-        activations.shape,
-    )
+        units + [u ^ NEAR for u in units], [core * 0] * 4, mine + other, None, activations.shape
+    )
+    for bits, pair in zip((FAR, FAR | SIDE), quarters):
+        there = unit ^ bits
+        act_grad = put_units(
+            [there, there, there ^ NEAR, there ^ NEAR],
+            [turn, 1 - turn] * 2,
+            pair + [partner(value, 1) for value in pair],
+            act_grad,
+            activations.shape,
+        )
     return (weight_grad[None], act_grad)
 
 

time: 396 us -> 338 us (0.85)
  waiting for transfers between devices: 235 us -> 162 us
  Pallas kernels: 78 us -> 93.1 us
  other arithmetic: 28.1 us -> 19 us
  starting transfers between devices: 40 us -> 45.7 us
  local copies, waits for them, and re-layouts: 11.7 us -> 16.1 us
    ppermute x20 -> x23, waiting for transfers between devices: 201 us -> 131 us  [swap(): return lax.ppermute(value, 'dp', [(d, d ^ bits) for d in range(dp_size)])]
    pallas_call x0 -> x2, Pallas kernels: none -> 7.43 us  [add_part(): pl.pallas_call(add_kernel, out_shape=jax.ShapeDtypeStruct(total.shape, jn...]
    ppermute x16 -> x22, starting transfers between devices: 7.12 us -> 12.9 us  [partner(): lax.ppermute(value, 'tensor', [(t, t ^ bit) for t in range(tensor_size)])]
    pallas_call x4 -> x5, Pallas kernels: 37.9 us -> 43.3 us  [weight_terms(): pl.pallas_call(functools.partial(weight_term_kernel, per_row, rows, first...]
    broadcast_in_dim x1 -> x0, other arithmetic: 4.46 us -> none  [local_bits_body(): return (weight_grad[None], act_grad)]
    pallas_call x2 -> x3, Pallas kernels: 6.48 us -> 8.75 us  [put_units(): pl.pallas_call(functools.partial(put_kernel, count), out_shape=jax.ShapeD...]
    ppermute x16 -> x22, waiting for transfers between devices: 34 us -> 31.9 us  [partner(): lax.ppermute(value, 'tensor', [(t, t ^ bit) for t in range(tensor_size)])]
    ppermute x20 -> x23, starting transfers between devices: 32.9 us -> 32.7 us  [swap(): return lax.ppermute(value, 'dp', [(d, d ^ bits) for d in range(dp_size)])]
  transfers between devices with their start and end apart: 36 -> 45, of which waited for: 19 -> 17; matrix products, arithmetic and copies ran while one was open for 4% -> 8% of each run, Pallas kernels for 14% -> 27%
where the time goes in v1:
time: 338 us
  waiting for transfers between devices  162 us (48%)
  Pallas kernels  93.1 us (28%)
  starting transfers between devices  45.7 us (14%)
  other arithmetic  19 us (6%)
  local copies, waits for them, and re-layouts  16.1 us (5%)
    ppermute x23, waiting for transfers between devices, swap(): return lax.ppermute(value, 'dp', [(d, d ^ bits) for d in range(dp_size)])  131 us
    pallas_call x5, Pallas kernels, weight_terms(): pl.pallas_call(functools.partial(weight_term_kernel, per_row, rows, first...  43.3 us
    pallas_call x3, Pallas kernels, act_partials(): pl.pallas_call(functools.partial(act_kernel, per_row, rows, len(hids), le...  33.6 us
    ppermute x23, starting transfers between devices, swap(): return lax.ppermute(value, 'dp', [(d, d ^ bits) for d in range(dp_size)])  32.7 us
    ppermute x22, waiting for transfers between devices, partner(): lax.ppermute(value, 'tensor', [(t, t ^ bit) for t in range(tensor_size)])  31.9 us
    ppermute x22, starting transfers between devices, partner(): lax.ppermute(value, 'tensor', [(t, t ^ bit) for t in range(tensor_size)])  12.9 us
    convert_element_type x4, other arithmetic, hidden_gradient(): (grad_act.astype(jnp.float32) * gelu_slope(pre_act)).astype(jnp.bfloat16)  8.77 us
    pallas_call x3, Pallas kernels, put_units(): pl.pallas_call(functools.partial(put_kernel, count), out_shape=jax.ShapeD...  8.75 us
  transfers between devices with their start and end apart: 45, of which 17 were waited for; matrix products, arithmetic and copies ran while one was open for 8% of the time, Pallas kernels for 27%

profile of v1, /device:TPU:0, one launch (start us, length us, event | category | flops | bytes accessed | tf_op | source)
XLA Modules:
  0.0 337.6 jit_solution(13605444444856423862)
XLA Ops:
  4.8 4.1 %collective-permute-start = (bf16[48,6144]{1,0:T(8,128)(2,1)}, bf16[48,6144]{1,0:T(8,128)(2,1)}, u32[]{:S(2)}, u32[]{:S(2)}) collective-permute-start(bf16[48,6144]{1,0:T(8,128)(2,1)} %fusion.33.refs_2_.refs_0_), channel_id=1, source_target_pairs={{0,16},{4,20},{8,24},{12,28},{16,0},{20,4},{24,8},{28,12},{1,17},{... | collective-permute-start | bytes 1769480 | tf_op jit(solution)/shard_map/ppermute | solution.py:337
  23.1 4.9 %collective-permute-done.3 = bf16[64,1536]{1,0:T(8,128)(2,1)S(1)} collective-permute-done((bf16[64,1536]{1,0:T(8,128)(2,1)}, bf16[64,1536]{1,0:T(8,128)(2,1)S(1)}, u32[]{:S(2)}, u32[]{:S(2)}) %collective-permute-start.3) | collective-permute-done | bytes 196640 | tf_op jit(solution)/shard_map/ppermute | solution.py:337
  35.0 22.1 %collective-permute-done.refs_0_.refs_2_ = bf16[48,6144]{1,0:T(8,128)(2,1)} collective-permute-done((bf16[48,6144]{1,0:T(8,128)(2,1)}, bf16[48,6144]{1,0:T(8,128)(2,1)}, u32[]{:S(2)}, u32[]{:S(2)}) %collective-permute-start) | collective-permute-done | bytes 589856 | tf_op jit(solution)/shard_map/ppermute | solution.py:337
  62.0 15.2 %collective-permute-done.2.refs_1_.refs_3_ = bf16[80,6144]{1,0:T(8,128)(2,1)S(1)} collective-permute-done((bf16[80,6144]{1,0:T(8,128)(2,1)}, bf16[80,6144]{1,0:T(8,128)(2,1)S(1)}, u32[]{:S(2)}, u32[]{:S(2)}) %collective-permute-start.2) | collective-permute-done | bytes 983072 | tf_op jit(solution)/shard_map/ppermute | solution.py:337
  77.3 35.8 %collective-permute-done.9.refs_9_.refs_7_ = bf16[48,6144]{1,0:T(8,128)(2,1)S(1)} collective-permute-done((bf16[48,6144]{1,0:T(8,128)(2,1)S(1)}, bf16[48,6144]{1,0:T(8,128)(2,1)S(1)}, u32[]{:S(2)}, u32[]{:S(2)}) %collective-permute-start.9) | collective-permute-done | bytes 589856 | tf_op jit(solution)/shard_map/ppermute | solution.py:337
  117.5 9.3 %weight_terms.5.refs_10_ = f32[72,128,128]{2,1,0:T(8,128)} custom-call(s32[2]{0:T(128)} %pad_add_fusion.2.place_ref, s32[576]{0:T(1024)} %reduce.cols_ref, bf16[256,6144]{1,0:T(8,128)(2,1)} %refs_0_.3, bf16[256,1536]{1,0:T(8,128)(2,1)} %copy-done.8, bf16[48,6144]{1,0:T(8,128)(2,1)} %fusion.33.refs_2_.refs_0_, bf16[80,6144]{1,0:T(8,128)(2,1)} %fusion.11.refs_3_.refs_1_, ...), custom_call_target="tpu_custom_call" | custom-call | flops 1207959552 | bytes 15728640 | tf_op jit(solution)/shard_map/weight_terms/pallas_call | solution.py:149
  126.9 9.1 %weight_terms.6.refs_10_ = f32[72,128,128]{2,1,0:T(8,128)} custom-call(s32[2]{0:T(128)} %pad_add_fusion.place_ref, s32[576]{0:T(1024)} %reduce.cols_ref, bf16[256,6144]{1,0:T(8,128)(2,1)} %refs_0_.3, bf16[256,1536]{1,0:T(8,128)(2,1)} %copy-done.8, bf16[48,6144]{1,0:T(8,128)(2,1)} %fusion.33.refs_2_.refs_0_, bf16[80,6144]{1,0:T(8,128)(2,1)} %fusion.11.refs_3_.refs_1_, ...), custom_call_target="tpu_custom_call" | custom-call | flops 1207959552 | bytes 15728640 | tf_op jit(solution)/shard_map/weight_terms/pallas_call | solution.py:149
  136.8 13.7 %act_partials.3 = (bf16[256,768]{1,0:T(8,128)(2,1)}, bf16[256,768]{1,0:T(8,128)(2,1)}, bf16[256,768]{1,0:T(8,128)(2,1)}, bf16[256,768]{1,0:T(8,128)(2,1)}) custom-call(s32[3]{0:T(128)} %pad_add_fusion.1.place_ref, s32[576]{0:T(1024)} %reduce.cols_ref, bf16[48,6144]{1,0:T(8,128)(2,1)} %fusion.33.refs_2_.refs_0_, bf16[80,6144]{1,0:T(8,128)(2,1)} %fusion.11.refs_3_.refs_1_, ...), custom_call_target="tpu_custom_call" | custom-call | flops 2415919104 | bytes 11010048 | tf_op jit(solution)/shard_map/act_partials/pallas_call | solution.py:225
  152.6 3.8 %collective-permute-done.15 = bf16[64,1536]{1,0:T(8,128)(2,1)S(1)} collective-permute-done((bf16[64,1536]{1,0:T(8,128)(2,1)S(1)}, bf16[64,1536]{1,0:T(8,128)(2,1)S(1)}, u32[]{:S(2)}, u32[]{:S(2)}) %collective-permute-start.15) | collective-permute-done | bytes 196640 | tf_op jit(solution)/shard_map/ppermute | solution.py:340
  161.1 8.9 %collective-permute-done.18 = bf16[256,768]{1,0:T(8,128)(2,1)S(1)} collective-permute-done((bf16[256,768]{1,0:T(8,128)(2,1)S(1)}, bf16[256,768]{1,0:T(8,128)(2,1)S(1)}, u32[]{:S(2)}, u32[]{:S(2)}) %collective-permute-start.18) | collective-permute-done | bytes 393248 | tf_op jit(solution)/shard_map/ppermute | solution.py:340
  170.1 7.8 %collective-permute-done.20 = bf16[256,768]{1,0:T(8,128)(2,1)S(1)} collective-permute-done((bf16[256,768]{1,0:T(8,128)(2,1)S(1)}, bf16[256,768]{1,0:T(8,128)(2,1)S(1)}, u32[]{:S(2)}, u32[]{:S(2)}) %collective-permute-start.20) | collective-permute-done | bytes 393248 | tf_op jit(solution)/shard_map/ppermute | solution.py:340
  178.8 9.9 %act_partials.4 = (bf16[256,768]{1,0:T(8,128)(2,1)}, bf16[256,768]{1,0:T(8,128)(2,1)}) custom-call(s32[3]{0:T(128)} %pad_add_fusion.1.place_ref, s32[576]{0:T(1024)} %reduce.cols_ref, bf16[48,6144]{1,0:T(8,128)(2,1)} %collective-permute-done.refs_0_.refs_2_, bf16[80,6144]{1,0:T(8,128)(2,1)} %copy-done.2, ...), custom_call_target="tpu_custom_call" | custom-call | flops 1207959552 | bytes 7864320 | tf_op jit(solution)/shard_map/act_partials/pallas_call | solution.py:225
  193.9 11.6 %collective-permute-done.22.refs_6_.refs_0_ = bf16[48,6144]{1,0:T(8,128)(2,1)S(1)} collective-permute-done((bf16[48,6144]{1,0:T(8,128)(2,1)}, bf16[48,6144]{1,0:T(8,128)(2,1)S(1)}, u32[]{:S(2)}, u32[]{:S(2)}) %collective-permute-start.22) | collective-permute-done | bytes 589856 | tf_op jit(solution)/shard_map/ppermute | solution.py:337
  207.0 11.1 %collective-permute-done.25.refs_9_.refs_3_ = bf16[48,6144]{1,0:T(8,128)(2,1)S(1)} collective-permute-done((bf16[48,6144]{1,0:T(8,128)(2,1)}, bf16[48,6144]{1,0:T(8,128)(2,1)S(1)}, u32[]{:S(2)}, u32[]{:S(2)}) %collective-permute-start.25) | collective-permute-done | bytes 589856 | tf_op jit(solution)/shard_map/ppermute | solution.py:337
  218.9 7.5 %weight_terms.7 = bf16[36,128,128]{2,1,0:T(8,128)(2,1)} custom-call(s32[2]{0:T(128)} %pad_add_fusion.2.place_ref, s32[576]{0:T(1024)} %reduce.cols_ref, bf16[256,1536]{1,0:T(8,128)(2,1)} %copy-done.1, bf16[256,1536]{1,0:T(8,128)(2,1)} %copy-done.1, bf16[48,6144]{1,0:T(8,128)(2,1)} %collective-permute-done.refs_0_.refs_2_, bf16[80,6144]{1,0:T(8,128)(2,1)} %copy-done.2, ...), custom_call_target="tpu_custom_call" | custom-call | flops 603979776 | bytes 11010048 | tf_op jit(solution)/shard_map/weight_terms/pallas_call | solution.py:149
  226.5 7.5 %weight_terms.8 = bf16[36,128,128]{2,1,0:T(8,128)(2,1)} custom-call(s32[2]{0:T(128)} %pad_add_fusion.2.place_ref, s32[576]{0:T(1024)} %reduce.cols_ref, bf16[256,1536]{1,0:T(8,128)(2,1)} %copy-done.1, bf16[256,1536]{1,0:T(8,128)(2,1)} %copy-done.1, bf16[48,6144]{1,0:T(8,128)(2,1)} %collective-permute-done.refs_0_.refs_2_, bf16[80,6144]{1,0:T(8,128)(2,1)} %copy-done.2, ...), custom_call_target="tpu_custom_call" | custom-call | flops 603979776 | bytes 11010048 | tf_op jit(solution)/shard_map/weight_terms/pallas_call | solution.py:149
  234.0 10.0 %act_partials.5 = (bf16[256,768]{1,0:T(8,128)(2,1)}, bf16[256,768]{1,0:T(8,128)(2,1)}) custom-call(s32[3]{0:T(128)} %pad_add_fusion.1.place_ref, s32[576]{0:T(1024)} %reduce.cols_ref, bf16[48,6144]{1,0:T(8,128)(2,1)} %copy-done.4, bf16[80,6144]{1,0:T(8,128)(2,1)} %copy-done.3, bf16[80,6144]{1,0:T(8,128)(2,1)} %collective-permute-done.24.refs_8_.refs_2_, ...), custom_call_target="tpu_custom_call" | custom-call | flops 1207959552 | bytes 7864320 | tf_op jit(solution)/shard_map/act_partials/pallas_call | solution.py:225
  256.6 7.8 %collective-permute-done.11 = bf16[64,768]{1,0:T(8,128)(2,1)S(1)} collective-permute-done((bf16[64,768]{1,0:T(8,128)(2,1)S(1)}, bf16[64,768]{1,0:T(8,128)(2,1)S(1)}, u32[]{:S(2)}, u32[]{:S(2)}) %collective-permute-start.11) | collective-permute-done | bytes 98336 | tf_op jit(solution)/shard_map/ppermute | solution.py:337
  276.9 4.8 %collective-permute-done.32 = bf16[128,768]{1,0:T(8,128)(2,1)S(1)} collective-permute-done((bf16[128,768]{1,0:T(8,128)(2,1)S(1)}, bf16[128,768]{1,0:T(8,128)(2,1)S(1)}, u32[]{:S(2)}, u32[]{:S(2)}) %collective-permute-start.32) | collective-permute-done | bytes 196640 | tf_op jit(solution)/shard_map/ppermute | solution.py:340
  282.5 4.3 %collective-permute-start.33 = (bf16[128,768]{1,0:T(8,128)(2,1)}, bf16[128,768]{1,0:T(8,128)(2,1)S(1)}, u32[]{:S(2)}, u32[]{:S(2)}) collective-permute-start(bf16[128,768]{1,0:T(8,128)(2,1)} %add_convert_fusion.7), channel_id=1, source_target_pairs={{0,20},{4,16},{8,28},{12,24},{16,4},{20,0},{24,12},{28,8},{1,21},{... | collective-permute-start | bytes 589832 | tf_op jit(solution)/shard_map/ppermute | solution.py:337
  289.8 11.2 %collective-permute-done.33.refs_0_ = bf16[128,768]{1,0:T(8,128)(2,1)S(1)} collective-permute-done((bf16[128,768]{1,0:T(8,128)(2,1)}, bf16[128,768]{1,0:T(8,128)(2,1)S(1)}, u32[]{:S(2)}, u32[]{:S(2)}) %collective-permute-start.33) | collective-permute-done | bytes 196640 | tf_op jit(solution)/shard_map/ppermute | solution.py:337
  301.6 5.2 %collective-permute-done.34.refs_1_ = bf16[128,768]{1,0:T(8,128)(2,1)} collective-permute-done((bf16[128,768]{1,0:T(8,128)(2,1)S(1)}, bf16[128,768]{1,0:T(8,128)(2,1)}, u32[]{:S(2)}, u32[]{:S(2)}) %collective-permute-start.34) | collective-permute-done | bytes 196640 | tf_op jit(solution)/shard_map/ppermute | solution.py:340
  309.6 9.9 %weight_terms.9.sum_ref = f32[72,128,128]{2,1,0:T(8,128)} custom-call(s32[2]{0:T(128)} %pad_add_fusion.place_ref, s32[576]{0:T(1024)} %reduce.cols_ref, bf16[256,1536]{1,0:T(8,128)(2,1)} %copy-done.7, bf16[256,1536]{1,0:T(8,128)(2,1)} %copy-done.7, bf16[48,6144]{1,0:T(8,128)(2,1)} %collective-permute-done.refs_0_.refs_2_, bf16[80,6144]{1,0:T(8,128)(2,1)} %copy-done.2, ...), custom_call_target="tpu_custom_call" | custom-call | flops 1207959552 | bytes 15728640 | tf_op jit(solution)/shard_map/weight_terms/pallas_call | solution.py:149
  319.5 7.1 %collective-permute-done.31.part_ref = bf16[36,128,128]{2,1,0:T(8,128)(2,1)} collective-permute-done((bf16[36,128,128]{2,1,0:T(8,128)(2,1)S(1)}, bf16[36,128,128]{2,1,0:T(8,128)(2,1)}, u32[]{:S(2)}, u32[]{:S(2)}) %collective-permute-start.31) | collective-permute-done | bytes 1179680 | tf_op jit(solution)/shard_map/ppermute | solution.py:337
  (181 shorter events, 93.7 us)
Async XLA Ops:
  4.8 52.4 %collective-permute-start = (bf16[48,6144]{1,0:T(8,128)(2,1)}, bf16[48,6144]{1,0:T(8,128)(2,1)}, u32[]{:S(2)}, u32[]{:S(2)}) collective-permute-start(bf16[48,6144]{1,0:T(8,128)(2,1)} %fusion.33.refs_2_.refs_0_), channel_id=1, source_target_pairs={{0,16},{4,20},{8,24},{12,28},{16,0},{20,4},{24,8},{28,12},{1,17},{... | collective-permute-start | bytes 1769480 | tf_op jit(solution)/shard_map/ppermute | solution.py:337
  8.8 50.1 %collective-permute-start.6 = (bf16[48,6144]{1,0:T(8,128)(2,1)}, bf16[48,6144]{1,0:T(8,128)(2,1)}, u32[]{:S(2)}, u32[]{:S(2)}) collective-permute-start(bf16[48,6144]{1,0:T(8,128)(2,1)} %fusion.33.refs_2_.refs_0_), channel_id=1, source_target_pairs={{0,4},{4,0},{8,12},{12,8},{16,20},{20,16},{24,28},{28,24},{1,5},{5... | collective-permute-start | bytes 1769480 | tf_op jit(solution)/shard_map/ppermute | solution.py:337
  12.7 64.5 %collective-permute-start.2 = (bf16[80,6144]{1,0:T(8,128)(2,1)}, bf16[80,6144]{1,0:T(8,128)(2,1)S(1)}, u32[]{:S(2)}, u32[]{:S(2)}) collective-permute-start(bf16[80,6144]{1,0:T(8,128)(2,1)} %fusion.11.refs_3_.refs_1_), channel_id=1, source_target_pairs={{0,16},{4,20},{8,24},{12,28},{16,0},{20,4},{24,8},{28,12},{1,17},{... | collective-permute-start | bytes 2949128 | tf_op jit(solution)/shard_map/ppermute | solution.py:337
  16.9 119.0 %collective-permute-start.10 = (bf16[72,128,128]{2,1,0:T(8,128)(2,1)S(1)}, bf16[72,128,128]{2,1,0:T(8,128)(2,1)}, u32[]{:S(2)}, u32[]{:S(2)}) collective-permute-start(bf16[72,128,128]{2,1,0:T(8,128)(2,1)S(1)} %bitcast.21), channel_id=1, source_target_pairs={{0,8},{4,12},{8,0},{12,4},{16,24},{20,28},{24,16},{28,20},{1,9},{5... | collective-permute-start | bytes 7077896 | tf_op jit(solution)/shard_map/ppermute | solution.py:337
  34.8 25.3 %collective-permute-start.5 = (bf16[128,1536]{1,0:T(8,128)(2,1)S(1)}, bf16[128,1536]{1,0:T(8,128)(2,1)S(1)}, u32[]{:S(2)}, u32[]{:S(2)}) collective-permute-start(bf16[128,1536]{1,0:T(8,128)(2,1)S(1)} %pad_maximum_fusion), channel_id=1, source_target_pairs={{0,1},{1,0},{2,3},{3,2},{4,5},{5,4},{6,7},{7,6},{8,9},{9,8},{10,11... | collective-permute-start | bytes 1179656 | tf_op jit(solution)/shard_map/ppermute | solution.py:340
  57.1 56.8 %collective-permute-start.7 = (bf16[80,6144]{1,0:T(8,128)(2,1)}, bf16[80,6144]{1,0:T(8,128)(2,1)}, u32[]{:S(2)}, u32[]{:S(2)}) collective-permute-start(bf16[80,6144]{1,0:T(8,128)(2,1)} %fusion.11.refs_3_.refs_1_), channel_id=1, source_target_pairs={{0,4},{4,0},{8,12},{12,8},{16,20},{20,16},{24,28},{28,24},{1,5},{5... | collective-permute-start | bytes 2949128 | tf_op jit(solution)/shard_map/ppermute | solution.py:337
  58.9 58.6 %collective-permute-start.8 = (bf16[80,6144]{1,0:T(8,128)(2,1)}, bf16[80,6144]{1,0:T(8,128)(2,1)}, u32[]{:S(2)}, u32[]{:S(2)}) collective-permute-start(bf16[80,6144]{1,0:T(8,128)(2,1)} %fusion.6.refs_4_.refs_2_), channel_id=1, source_target_pairs={{0,4},{4,0},{8,12},{12,8},{16,20},{20,16},{24,28},{28,24},{1,5},{5... | collective-permute-start | bytes 2949128 | tf_op jit(solution)/shard_map/ppermute | solution.py:337
  60.1 52.9 %collective-permute-start.9 = (bf16[48,6144]{1,0:T(8,128)(2,1)S(1)}, bf16[48,6144]{1,0:T(8,128)(2,1)S(1)}, u32[]{:S(2)}, u32[]{:S(2)}) collective-permute-start(bf16[48,6144]{1,0:T(8,128)(2,1)S(1)} %copy-done.6), channel_id=1, source_target_pairs={{0,4},{4,0},{8,12},{12,8},{16,20},{20,16},{24,28},{28,24},{1,5},{5... | collective-permute-start | bytes 1769480 | tf_op jit(solution)/shard_map/ppermute | solution.py:337
  77.2 73.3 %collective-permute-start.1 = (bf16[80,6144]{1,0:T(8,128)(2,1)}, bf16[80,6144]{1,0:T(8,128)(2,1)}, u32[]{:S(2)}, u32[]{:S(2)}) collective-permute-start(bf16[80,6144]{1,0:T(8,128)(2,1)} %fusion.6.refs_4_.refs_2_), channel_id=1, source_target_pairs={{0,16},{4,20},{8,24},{12,28},{16,0},{20,4},{24,8},{28,12},{1,17},{... | collective-permute-start | bytes 2949128 | tf_op jit(solution)/shard_map/ppermute | solution.py:337
  113.9 36.7 %collective-permute-start.13 = (bf16[64,768]{1,0:T(8,128)(2,1)}, bf16[64,768]{1,0:T(8,128)(2,1)S(1)}, u32[]{:S(2)}, u32[]{:S(2)}) collective-permute-start(bf16[64,768]{1,0:T(8,128)(2,1)} %get-tuple-element.65), channel_id=1, source_target_pairs={{0,16},{4,20},{8,24},{12,28},{16,0},{20,4},{24,8},{28,12},{1,17},{... | collective-permute-start | bytes 294920 | tf_op jit(solution)/shard_map/ppermute | solution.py:337
  113.9 36.7 %collective-permute-start.14 = (bf16[64,768]{1,0:T(8,128)(2,1)}, bf16[64,768]{1,0:T(8,128)(2,1)S(1)}, u32[]{:S(2)}, u32[]{:S(2)}) collective-permute-start(bf16[64,768]{1,0:T(8,128)(2,1)} %get-tuple-element.64), channel_id=1, source_target_pairs={{0,20},{4,16},{8,28},{12,24},{16,4},{20,0},{24,12},{28,8},{1,21},{... | collective-permute-start | bytes 294920 | tf_op jit(solution)/shard_map/ppermute | solution.py:337
  136.0 42.8 %collective-permute-start.12 = (bf16[48,6144]{1,0:T(8,128)(2,1)}, bf16[48,6144]{1,0:T(8,128)(2,1)}, u32[]{:S(2)}, u32[]{:S(2)}) collective-permute-start(bf16[48,6144]{1,0:T(8,128)(2,1)} %fusion.28.refs_5_.refs_3_), channel_id=1, source_target_pairs={{0,16},{4,20},{8,24},{12,28},{16,0},{20,4},{24,8},{28,12},{1,17},{... | collective-permute-start | bytes 1769480 | tf_op jit(solution)/shard_map/ppermute | solution.py:337
  136.0 71.0 %collective-permute-start.23 = (bf16[80,6144]{1,0:T(8,128)(2,1)S(1)}, bf16[80,6144]{1,0:T(8,128)(2,1)S(1)}, u32[]{:S(2)}, u32[]{:S(2)}) collective-permute-start(bf16[80,6144]{1,0:T(8,128)(2,1)S(1)} %collective-permute-done.2.refs_1_.refs_3_), channel_id=1, source_target_pairs={{0,4},{4,0},{8,12},{12,8},{16,20},{20,16},{24,28},{28,24},{1,5},{5... | collective-permute-start | bytes 2949128 | tf_op jit(solution)/shard_map/ppermute | solution.py:337
  156.4 50.7 %collective-permute-start.24 = (bf16[80,6144]{1,0:T(8,128)(2,1)}, bf16[80,6144]{1,0:T(8,128)(2,1)}, u32[]{:S(2)}, u32[]{:S(2)}) collective-permute-start(bf16[80,6144]{1,0:T(8,128)(2,1)} %collective-permute-done.1.refs_2_.refs_4_), channel_id=1, source_target_pairs={{0,4},{4,0},{8,12},{12,8},{16,20},{20,16},{24,28},{28,24},{1,5},{5... | collective-permute-start | bytes 2949128 | tf_op jit(solution)/shard_map/ppermute | solution.py:337
  189.9 28.2 %collective-permute-start.25 = (bf16[48,6144]{1,0:T(8,128)(2,1)}, bf16[48,6144]{1,0:T(8,128)(2,1)S(1)}, u32[]{:S(2)}, u32[]{:S(2)}) collective-permute-start(bf16[48,6144]{1,0:T(8,128)(2,1)} %collective-permute-done.12.refs_3_.refs_5_), channel_id=1, source_target_pairs={{0,4},{4,0},{8,12},{12,8},{16,20},{20,16},{24,28},{28,24},{1,5},{5... | collective-permute-start | bytes 1769480 | tf_op jit(solution)/shard_map/ppermute | solution.py:337
  191.1 61.2 %collective-permute-start.42 = (bf16[256,768]{1,0:T(8,128)(2,1)}, bf16[256,768]{1,0:T(8,128)(2,1)}, u32[]{:S(2)}, u32[]{:S(2)}) collective-permute-start(bf16[256,768]{1,0:T(8,128)(2,1)} %add_convert_fusion.2), channel_id=1, source_target_pairs={{0,4},{4,0},{8,12},{12,8},{16,20},{20,16},{24,28},{28,24},{1,5},{5... | collective-permute-start | bytes 1179656 | tf_op jit(solution)/shard_map/ppermute | solution.py:337
  205.5 38.6 %collective-permute-start.37 = (bf16[128,768]{1,0:T(8,128)(2,1)}, bf16[128,768]{1,0:T(8,128)(2,1)}, u32[]{:S(2)}, u32[]{:S(2)}) collective-permute-start(bf16[128,768]{1,0:T(8,128)(2,1)} %constant_dynamic-slice_fusion.1), channel_id=1, source_target_pairs={{0,2},{1,3},{2,0},{3,1},{4,6},{5,7},{6,4},{7,5},{8,10},{9,11},{10,... | collective-permute-start | bytes 589832 | tf_op jit(solution)/shard_map/ppermute | solution.py:340
  254.0 21.6 %collective-permute-start.39 = (bf16[128,768]{1,0:T(8,128)(2,1)}, bf16[128,768]{1,0:T(8,128)(2,1)}, u32[]{:S(2)}, u32[]{:S(2)}) collective-permute-start(bf16[128,768]{1,0:T(8,128)(2,1)} %collective-permute-done.38.refs_0_), channel_id=1, source_target_pairs={{0,2},{1,3},{2,0},{3,1},{4,6},{5,7},{6,4},{7,5},{8,10},{9,11},{10,... | collective-permute-start | bytes 589832 | tf_op jit(solution)/shard_map/ppermute | solution.py:340
  269.6 60.7 %collective-permute-start.30 = (bf16[36,128,128]{2,1,0:T(8,128)(2,1)S(1)}, bf16[36,128,128]{2,1,0:T(8,128)(2,1)}, u32[]{:S(2)}, u32[]{:S(2)}) collective-permute-start(bf16[36,128,128]{2,1,0:T(8,128)(2,1)S(1)} %copy-done.15), channel_id=1, source_target_pairs={{0,8},{4,12},{8,0},{12,4},{16,24},{20,28},{24,16},{28,20},{1,9},{5... | collective-permute-start | bytes 3538952 | tf_op jit(solution)/shard_map/ppermute | solution.py:337
  276.4 30.4 %collective-permute-start.29 = (bf16[128,1536]{1,0:T(8,128)(2,1)}, bf16[128,1536]{1,0:T(8,128)(2,1)}, u32[]{:S(2)}, u32[]{:S(2)}) collective-permute-start(bf16[128,1536]{1,0:T(8,128)(2,1)} %pad_maximum_fusion.2), channel_id=1, source_target_pairs={{0,1},{1,0},{2,3},{3,2},{4,5},{5,4},{6,7},{7,6},{8,9},{9,8},{10,11... | collective-permute-start | bytes 1179656 | tf_op jit(solution)/shard_map/ppermute | solution.py:340
  282.5 18.6 %collective-permute-start.33 = (bf16[128,768]{1,0:T(8,128)(2,1)}, bf16[128,768]{1,0:T(8,128)(2,1)S(1)}, u32[]{:S(2)}, u32[]{:S(2)}) collective-permute-start(bf16[128,768]{1,0:T(8,128)(2,1)} %add_convert_fusion.7), channel_id=1, source_target_pairs={{0,20},{4,16},{8,28},{12,24},{16,4},{20,0},{24,12},{28,8},{1,21},{... | collective-permute-start | bytes 589832 | tf_op jit(solution)/shard_map/ppermute | solution.py:337
  286.9 39.7 %collective-permute-start.31 = (bf16[36,128,128]{2,1,0:T(8,128)(2,1)S(1)}, bf16[36,128,128]{2,1,0:T(8,128)(2,1)}, u32[]{:S(2)}, u32[]{:S(2)}) collective-permute-start(bf16[36,128,128]{2,1,0:T(8,128)(2,1)S(1)} %copy-done.16), channel_id=1, source_target_pairs={{0,8},{4,12},{8,0},{12,4},{16,24},{20,28},{24,16},{28,20},{1,9},{5... | collective-permute-start | bytes 3538952 | tf_op jit(solution)/shard_map/ppermute | solution.py:337
  301.5 32.5 %collective-permute-start.35 = (bf16[128,768]{1,0:T(8,128)(2,1)S(1)}, bf16[128,768]{1,0:T(8,128)(2,1)S(1)}, u32[]{:S(2)}, u32[]{:S(2)}) collective-permute-start(bf16[128,768]{1,0:T(8,128)(2,1)S(1)} %collective-permute-done.33.refs_0_), channel_id=1, source_target_pairs={{0,1},{1,0},{2,3},{3,2},{4,5},{5,4},{6,7},{7,6},{8,9},{9,8},{10,11... | collective-permute-start | bytes 589832 | tf_op jit(solution)/shard_map/ppermute | solution.py:340
  306.8 27.2 %collective-permute-start.36 = (bf16[128,768]{1,0:T(8,128)(2,1)}, bf16[128,768]{1,0:T(8,128)(2,1)}, u32[]{:S(2)}, u32[]{:S(2)}) collective-permute-start(bf16[128,768]{1,0:T(8,128)(2,1)} %collective-permute-done.34.refs_1_), channel_id=1, source_target_pairs={{0,1},{1,0},{2,3},{3,2},{4,5},{5,4},{6,7},{7,6},{8,9},{9,8},{10,11... | collective-permute-start | bytes 589832 | tf_op jit(solution)/shard_map/ppermute | solution.py:340
  (47 other events, 631.0 us)

commit v2 on v1

--- a/solution.py
+++ b/solution.py
@@ -79,7 +79,6 @@
 
 
 SIDE, NEAR, FAR = 1, 2, 4
-SETS = (0, SIDE, FAR, FAR | SIDE)
 CHUNKS = (3, 5, 5, 3)
 
 
@@ -133,9 +132,12 @@
     tok = acts[0][0].shape[0]
     step_rows = next(k for k in (3, 2, 1) if count % k == 0)
 
+    def at_of(place_ref):
+        return {"unit": place_ref[0], "near": place_ref[1], "near_next": place_ref[1] + 2}
+
     def act_spec(which):
         def at(s, place_ref, _):
-            return (0, {"unit": place_ref[0], "near": place_ref[1]}.get(which, which))
+            return (0, at_of(place_ref)[which])
 
         return pl.BlockSpec((tok, rows * block), at)
 
@@ -341,10 +343,17 @@
 
     share = tok // tensor_size
 
-    def share_of(unit, bits, *others):
-        whole = after(activations, *others)
-        part = lax.dynamic_slice(whole, (t_place * share, unit * span), (share, span))
-        return swap(part, bits)
+    def share_of(bits, *others):
+        mine = after(activations, *others)
+        parts = [
+            lax.dynamic_slice(
+                mine,
+                (t_place * share, (((place ^ bits) & (FAR | SIDE)) + NEAR * j) * span),
+                (share, span),
+            )
+            for j in (0, 1)
+        ]
+        return swap(jnp.concatenate(parts, axis=1), bits)
 
     def gathered(parts, *others):
         pieces = {0: jnp.concatenate([after(part, *others) for part in parts], axis=1)}
@@ -366,29 +375,15 @@
     for index, part in enumerate(CHUNKS):
         rows_of = slice(cut, cut + part * tok // sum(CHUNKS))
         cut = rows_of.stop
-        pre_part = after(pre_act[rows_of], *hid_own[-1:])
-        hid_own.append(hidden_gradient(pre_part, grad_act[rows_of]))
+        if hid_own:
+            pre_act = after(pre_act, hid_own[-1])
+        hid_own.append(hidden_gradient(pre_act[rows_of], grad_act[rows_of]))
         if index < 2:
             hid_far.append(swap(hid_own[index], FAR))
         hid_side.append(swap(hid_own[-1], SIDE))
 
-    side_share = lax.dynamic_slice_in_dim(activations, t_place * share, share, 0)
-    options = [
-        jnp.concatenate(
-            [side_share[:, (base + NEAR * j) * span : (base + NEAR * j + 1) * span] for j in (0, 1)],
-            axis=1,
-        )
-        for base in SETS
-    ]
-    wanted = (place ^ SIDE) & (FAR | SIDE)
-    chosen = options[0]
-    for base, option in zip(SETS[1:], options[1:]):
-        chosen = jnp.where(wanted == base, option, chosen)
-    side_acts = gathered([swap(after(chosen, hid_own[0]), SIDE)])
-    near_shares = [
-        share_of(place ^ NEAR ^ FAR, FAR, hid_own[1]),
-        share_of(place ^ NEAR ^ FAR ^ SIDE, FAR | SIDE, hid_own[1]),
-    ]
+    side_acts = gathered([share_of(SIDE, hid_own[1])])
+    far_shares = [share_of(FAR, hid_own[1]), share_of(FAR | SIDE, hid_own[1])]
     own_weight = kept_weight[0]
     near_weight = swap(after(own_weight, hid_own[-1]), NEAR)
 
@@ -415,20 +410,18 @@
     def core_sum(keep, give):
         return add_up(keep, partner(give, 1))
 
-    def rest_sum(half, first_bit):
-        bit = first_bit
+    def more_sum(value):
+        bit = 4
         while bit < tensor_size:
-            half = add_up(half, partner(half, bit))
+            value = add_up(value, partner(value, bit))
             bit *= 2
-        return half
+        return value
 
     turn = (t_place // 2) % 2
     token_half = tok // 2
 
-    def quarter_sum(half):
-        keep = lax.dynamic_slice_in_dim(half, turn * token_half, token_half, 0)
-        give = lax.dynamic_slice_in_dim(half, (1 - turn) * token_half, token_half, 0)
-        return rest_sum(add_up(keep, partner(give, 2)), 4)
+    def half_of(value, which):
+        return lax.dynamic_slice_in_dim(value, which * token_half, token_half, 0)
 
     hid_both = [swap(hid_far[0], SIDE)]
     hid_far.append(swap(after(hid_own[2], hid_far[0]), FAR))
@@ -436,69 +429,75 @@
     hid_far.append(swap(after(hid_own[3], hid_far[1]), FAR))
     near_sum = first_terms(after(near_place, hid_far[1]))
     own_sum = first_terms(after(own_place, near_sum))
-    first_acts = acts_of([hid_own, hid_side], own_sum)
-    near_acts = gathered(near_shares, first_acts[0])
-    third = after(hid_far[2], first_acts[0])
+    far_acts = gathered(far_shares, own_sum)
+    third = after(hid_far[2], own_sum)
     hid_both.append(swap(third, SIDE))
-    own_shares = [
-        share_of(place ^ FAR, FAR, third), share_of(place ^ FAR ^ SIDE, FAR | SIDE, third)
-    ]
-    halves = [rest_sum(core_sum(first_acts[2 * k], first_acts[2 * k + 1]), 2) for k in range(2)]
-    fourth = after(hid_far[3], near_acts, *halves)
+    parts = acts_of([hid_own, hid_side], third)
+    near_cores = [core_sum(parts[0], parts[1]), core_sum(parts[2], parts[3])]
+    near_got = [partner(value, 2) for value in near_cores]
+    fourth = after(hid_far[3], far_acts, *near_cores)
     hid_both.append(swap(fourth, SIDE))
-    far_acts = acts_of([hid_far], fourth)
-    far_core = core_sum(far_acts[0], far_acts[1])
+    parts = acts_of([hid_far], fourth)
+    far_core = core_sum(parts[0], parts[1])
+    far_got = partner(half_of(far_core, 1 - turn), 2)
 
     cuts = 2 if rows % 2 == 0 else 1
     came, last = [], far_core
+    there = dict(hids=[hid_far, hid_both])
     for k in range(cuts):
         last = terms(
             after(near_place, last),
-            acts=[(near_acts, 0), (near_acts, 1)],
-            hids=[hid_far, hid_both],
+            acts=[(far_acts, "near"), (far_acts, "near_next")],
             acc=near_sum,
             first_row=k * (rows // cuts),
             count=rows // cuts,
             kind=jnp.bfloat16,
+            **there,
         )
         came.append(swap(last, NEAR))
-    both_acts = acts_of([hid_both], last)
-    both_core = core_sum(both_acts[0], both_acts[1])
-    quarters = []
-    for half, bits in ((far_core, FAR), (both_core, FAR | SIDE)):
-        quarter = swap(quarter_sum(half), bits)
-        quarters.append([quarter, partner(quarter, 2)])
-
-    own_acts = gathered(own_shares, both_core)
+    far_sum = more_sum(add_up(after(half_of(far_core, turn), last), far_got))
+    far_back = swap(far_sum, FAR)
+    parts = acts_of([hid_both], far_sum)
+    both_core = core_sum(parts[0], parts[1])
+    both_got = partner(half_of(both_core, 1 - turn), 2)
     own_sum = terms(
-        own_place,
-        acts=[(own_acts, 0), (own_acts, 1)],
-        hids=[hid_far, hid_both],
+        after(own_place, both_core),
+        acts=[(far_acts, "near"), (far_acts, "near_next")],
         acc=own_sum,
         first_row=0,
         count=rows,
         kind=jnp.float32,
+        **there,
+    )
+    both_sum = more_sum(add_up(after(half_of(both_core, turn), own_sum), both_got))
+    both_back = swap(both_sum, FAR | SIDE)
+    halves = [
+        more_sum(add_up(after(value, both_sum), got)) for value, got in zip(near_cores, near_got)
+    ]
+    unit = (place & (FAR | SIDE)) + NEAR * core
+    mine = [halves[0], swap(halves[1], SIDE)]
+    quarters = []
+    for value in (after(far_back, *halves), both_back):
+        quarters.append([value, partner(value, 2)])
+
+    def put(bits_of, arrays, parts_of, whole):
+        there_units = [unit ^ bits for bits in bits_of]
+        return put_units(
+            there_units + [u ^ NEAR for u in there_units],
+            parts_of * 2,
+            arrays + [partner(value, 1) for value in arrays],
+            whole,
+            activations.shape,
+        )
+
+    zero = core * 0
+    act_grad = put([0, SIDE], mine, [zero, zero], None)
+    act_grad = put(
+        [FAR, FAR, FAR | SIDE, FAR | SIDE], quarters[0] + quarters[1], [turn, 1 - turn] * 2, act_grad
     )
     weight_grad = None
     for k, value in enumerate(came):
         weight_grad = add_part(own_sum, value, k, per_row, weight_grad)
-
-    unit = (place & (FAR | SIDE)) + NEAR * core
-    mine = [halves[0], swap(halves[1], SIDE)]
-    other = [partner(half, 1) for half in mine]
-    units = [unit, unit ^ SIDE]
-    act_grad = put_units(
-        units + [u ^ NEAR for u in units], [core * 0] * 4, mine + other, None, activations.shape
-    )
-    for bits, pair in zip((FAR, FAR | SIDE), quarters):
-        there = unit ^ bits
-        act_grad = put_units(
-            [there, there, there ^ NEAR, there ^ NEAR],
-            [turn, 1 - turn] * 2,
-            pair + [partner(value, 1) for value in pair],
-            act_grad,
-            activations.shape,
-        )
     return (weight_grad[None], act_grad)
 
 

time: 338 us -> 370 us (1.095)
  waiting for transfers between devices: 162 us -> 197 us
  local copies, waits for them, and re-layouts: 16.1 us -> 10.7 us
    ppermute x23 -> x21, waiting for transfers between devices: 131 us -> 172 us  [swap(): return lax.ppermute(value, 'dp', [(d, d ^ bits) for d in range(dp_size)])]
    ppermute x22 -> x20, waiting for transfers between devices: 31.9 us -> 24.2 us  [partner(): lax.ppermute(value, 'tensor', [(t, t ^ bit) for t in range(tensor_size)])]
    pallas_call x3 -> x2, Pallas kernels: 8.75 us -> 6.5 us  [put_units(): pl.pallas_call(functools.partial(put_kernel, count), out_shape=jax.ShapeD...]
    ppermute x22 -> x20, starting transfers between devices: 12.9 us -> 11.2 us  [partner(): lax.ppermute(value, 'tensor', [(t, t ^ bit) for t in range(tensor_size)])]
    ppermute x23 -> x21, starting transfers between devices: 32.7 us -> 33.9 us  [swap(): return lax.ppermute(value, 'dp', [(d, d ^ bits) for d in range(dp_size)])]
  transfers between devices with their start and end apart: 45 -> 41, of which waited for: 17 -> 18; matrix products, arithmetic and copies ran while one was open for 8% -> 5% of each run, Pallas kernels for 27% -> 21%
where the time goes in v2:
time: 370 us; the launch traced here: 367 us
  waiting for transfers between devices  197 us (53%)
  Pallas kernels  90.9 us (25%)
  starting transfers between devices  45.1 us (12%)
  other arithmetic  22.1 us (6%)
  local copies, waits for them, and re-layouts  10.7 us (3%)
    ppermute x21, waiting for transfers between devices, swap(): return lax.ppermute(value, 'dp', [(d, d ^ bits) for d in range(dp_size)])  172 us
    pallas_call x5, Pallas kernels, weight_terms(): pl.pallas_call(functools.partial(weight_term_kernel, per_row, rows, first...  43.4 us
    ppermute x21, starting transfers between devices, swap(): return lax.ppermute(value, 'dp', [(d, d ^ bits) for d in range(dp_size)])  33.9 us
    pallas_call x3, Pallas kernels, act_partials(): pl.pallas_call(functools.partial(act_kernel, per_row, rows, len(hids), le...  33.6 us
    ppermute x20, waiting for transfers between devices, partner(): lax.ppermute(value, 'tensor', [(t, t ^ bit) for t in range(tensor_size)])  24.2 us
    convert_element_type x4, other arithmetic, hidden_gradient(): (grad_act.astype(jnp.float32) * gelu_slope(pre_act)).astype(jnp.bfloat16)  11.3 us
    ppermute x20, starting transfers between devices, partner(): lax.ppermute(value, 'tensor', [(t, t ^ bit) for t in range(tensor_size)])  11.2 us
    pallas_call x2, Pallas kernels, add_part(): pl.pallas_call(add_kernel, out_shape=jax.ShapeDtypeStruct(total.shape, jn...  7.43 us
  transfers between devices with their start and end apart: 41, of which 18 were waited for; matrix products, arithmetic and copies ran while one was open for 5% of the time, Pallas kernels for 21%

profile of v2, /device:TPU:0, one launch (start us, length us, event | category | flops | bytes accessed | tf_op | source)
XLA Modules:
  0.0 366.6 jit_solution(7054677995652467438)
XLA Ops:
  6.3 4.1 %collective-permute-start = (bf16[80,6144]{1,0:T(8,128)(2,1)S(1)}, bf16[80,6144]{1,0:T(8,128)(2,1)S(1)}, u32[]{:S(2)}, u32[]{:S(2)}) collective-permute-start(bf16[80,6144]{1,0:T(8,128)(2,1)S(1)} %fusion.11.refs_3_.refs_1_), channel_id=1, source_target_pairs={{0,16},{4,20},{8,24},{12,28},{16,0},{20,4},{24,8},{28,12},{1,17},{... | collective-permute-start | bytes 2949128 | tf_op jit(solution)/shard_map/ppermute | solution.py:339
  24.6 14.7 %collective-permute-done.3 = bf16[64,1536]{1,0:T(8,128)(2,1)S(1)} collective-permute-done((bf16[64,1536]{1,0:T(8,128)(2,1)}, bf16[64,1536]{1,0:T(8,128)(2,1)S(1)}, u32[]{:S(2)}, u32[]{:S(2)}) %collective-permute-start.3) | collective-permute-done | bytes 196640 | tf_op jit(solution)/shard_map/ppermute | solution.py:339
  48.3 4.9 %collective-permute-done.refs_1_.refs_3_ = bf16[80,6144]{1,0:T(8,128)(2,1)S(1)} collective-permute-done((bf16[80,6144]{1,0:T(8,128)(2,1)S(1)}, bf16[80,6144]{1,0:T(8,128)(2,1)S(1)}, u32[]{:S(2)}, u32[]{:S(2)}) %collective-permute-start) | collective-permute-done | bytes 983072 | tf_op jit(solution)/shard_map/ppermute | solution.py:339
  53.2 19.8 %collective-permute-done.9.refs_9_.refs_7_ = bf16[48,6144]{1,0:T(8,128)(2,1)} collective-permute-done((bf16[48,6144]{1,0:T(8,128)(2,1)}, bf16[48,6144]{1,0:T(8,128)(2,1)}, u32[]{:S(2)}, u32[]{:S(2)}) %collective-permute-start.9) | collective-permute-done | bytes 589856 | tf_op jit(solution)/shard_map/ppermute | solution.py:339
  74.6 9.5 %collective-permute-done.6.refs_6_.refs_4_ = bf16[48,6144]{1,0:T(8,128)(2,1)S(1)} collective-permute-done((bf16[48,6144]{1,0:T(8,128)(2,1)}, bf16[48,6144]{1,0:T(8,128)(2,1)S(1)}, u32[]{:S(2)}, u32[]{:S(2)}) %collective-permute-start.6) | collective-permute-done | bytes 589856 | tf_op jit(solution)/shard_map/ppermute | solution.py:339
  88.1 9.2 %weight_terms.5.refs_10_ = f32[72,128,128]{2,1,0:T(8,128)} custom-call(s32[2]{0:T(128)} %pad_add_fusion.2.place_ref, s32[576]{0:T(1024)} %reduce.cols_ref, bf16[256,6144]{1,0:T(8,128)(2,1)} %refs_0_.3, bf16[256,1536]{1,0:T(8,128)(2,1)} %copy-done.9, bf16[48,6144]{1,0:T(8,128)(2,1)} %fusion.33.refs_2_.refs_0_, bf16[80,6144]{1,0:T(8,128)(2,1)} %copy-done.2, ...), custom_call_target="tpu_custom_call" | custom-call | flops 1207959552 | bytes 15728640 | tf_op jit(solution)/shard_map/weight_terms/pallas_call | solution.py:151
  97.3 9.3 %weight_terms.6.refs_10_ = f32[72,128,128]{2,1,0:T(8,128)} custom-call(s32[2]{0:T(128)} %pad_add_fusion.place_ref, s32[576]{0:T(1024)} %reduce.cols_ref, bf16[256,6144]{1,0:T(8,128)(2,1)} %refs_0_.3, bf16[256,1536]{1,0:T(8,128)(2,1)} %copy-done.9, bf16[48,6144]{1,0:T(8,128)(2,1)} %fusion.33.refs_2_.refs_0_, bf16[80,6144]{1,0:T(8,128)(2,1)} %copy-done.2, ...), custom_call_target="tpu_custom_call" | custom-call | flops 1207959552 | bytes 15728640 | tf_op jit(solution)/shard_map/weight_terms/pallas_call | solution.py:151
  106.6 22.7 %collective-permute-done.10 = bf16[64,1536]{1,0:T(8,128)(2,1)} collective-permute-done((bf16[64,1536]{1,0:T(8,128)(2,1)}, bf16[64,1536]{1,0:T(8,128)(2,1)}, u32[]{:S(2)}, u32[]{:S(2)}) %collective-permute-start.10) | collective-permute-done | bytes 196640 | tf_op jit(solution)/shard_map/ppermute | solution.py:339
  147.1 42.3 %collective-permute-done.14.refs_2_.refs_4_ = bf16[80,6144]{1,0:T(8,128)(2,1)} collective-permute-done((bf16[80,6144]{1,0:T(8,128)(2,1)S(1)}, bf16[80,6144]{1,0:T(8,128)(2,1)}, u32[]{:S(2)}, u32[]{:S(2)}) %collective-permute-start.14) | collective-permute-done | bytes 983072 | tf_op jit(solution)/shard_map/ppermute | solution.py:339
  191.8 13.8 %act_partials.3 = (bf16[256,768]{1,0:T(8,128)(2,1)}, bf16[256,768]{1,0:T(8,128)(2,1)}, bf16[256,768]{1,0:T(8,128)(2,1)}, bf16[256,768]{1,0:T(8,128)(2,1)}) custom-call(s32[3]{0:T(128)} %pad_add_fusion.1.place_ref, s32[576]{0:T(1024)} %reduce.cols_ref, bf16[48,6144]{1,0:T(8,128)(2,1)} %fusion.33.refs_2_.refs_0_, bf16[80,6144]{1,0:T(8,128)(2,1)} %copy-done.2, ...), custom_call_target="tpu_custom_call" | custom-call | flops 2415919104 | bytes 11010048 | tf_op jit(solution)/shard_map/act_partials/pallas_call | solution.py:227
  210.4 9.9 %act_partials.4 = (bf16[256,768]{1,0:T(8,128)(2,1)}, bf16[256,768]{1,0:T(8,128)(2,1)}) custom-call(s32[3]{0:T(128)} %pad_add_fusion.1.place_ref, s32[576]{0:T(1024)} %reduce.cols_ref, bf16[48,6144]{1,0:T(8,128)(2,1)} %copy-done.6, bf16[80,6144]{1,0:T(8,128)(2,1)} %copy-done.1, bf16[80,6144]{1,0:T(8,128)(2,1)} %collective-permute-done.14.refs_2_.refs_4_, ...), custom_call_target="tpu_custom_call" | custom-call | flops 1207959552 | bytes 7864320 | tf_op jit(solution)/shard_map/act_partials/pallas_call | solution.py:227
  225.1 12.7 %collective-permute-done.19.refs_6_.refs_0_ = bf16[48,6144]{1,0:T(8,128)(2,1)S(1)} collective-permute-done((bf16[48,6144]{1,0:T(8,128)(2,1)}, bf16[48,6144]{1,0:T(8,128)(2,1)S(1)}, u32[]{:S(2)}, u32[]{:S(2)}) %collective-permute-start.19) | collective-permute-done | bytes 589856 | tf_op jit(solution)/shard_map/ppermute | solution.py:339
  237.8 11.7 %collective-permute-done.22.refs_9_.refs_3_ = bf16[48,6144]{1,0:T(8,128)(2,1)S(1)} collective-permute-done((bf16[48,6144]{1,0:T(8,128)(2,1)}, bf16[48,6144]{1,0:T(8,128)(2,1)S(1)}, u32[]{:S(2)}, u32[]{:S(2)}) %collective-permute-start.22) | collective-permute-done | bytes 589856 | tf_op jit(solution)/shard_map/ppermute | solution.py:339
  250.4 7.5 %weight_terms.7 = bf16[36,128,128]{2,1,0:T(8,128)(2,1)} custom-call(s32[2]{0:T(128)} %pad_add_fusion.2.place_ref, s32[576]{0:T(1024)} %reduce.cols_ref, bf16[256,3072]{1,0:T(8,128)(2,1)} %copy-done, bf16[256,3072]{1,0:T(8,128)(2,1)} %copy-done, bf16[48,6144]{1,0:T(8,128)(2,1)} %copy-done.6, bf16[80,6144]{1,0:T(8,128)(2,1)} %copy-done.1, ...), custom_call_target="tpu_custom_call" | custom-call | flops 603979776 | bytes 11010048 | tf_op jit(solution)/shard_map/weight_terms/pallas_call | solution.py:151
  257.9 7.5 %weight_terms.8 = bf16[36,128,128]{2,1,0:T(8,128)(2,1)} custom-call(s32[2]{0:T(128)} %pad_add_fusion.2.place_ref, s32[576]{0:T(1024)} %reduce.cols_ref, bf16[256,3072]{1,0:T(8,128)(2,1)} %copy-done, bf16[256,3072]{1,0:T(8,128)(2,1)} %copy-done, bf16[48,6144]{1,0:T(8,128)(2,1)} %copy-done.6, bf16[80,6144]{1,0:T(8,128)(2,1)} %copy-done.1, ...), custom_call_target="tpu_custom_call" | custom-call | flops 603979776 | bytes 11010048 | tf_op jit(solution)/shard_map/weight_terms/pallas_call | solution.py:151
  266.4 9.9 %act_partials.5 = (bf16[256,768]{1,0:T(8,128)(2,1)}, bf16[256,768]{1,0:T(8,128)(2,1)}) custom-call(s32[3]{0:T(128)} %pad_add_fusion.1.place_ref, s32[576]{0:T(1024)} %reduce.cols_ref, bf16[48,6144]{1,0:T(8,128)(2,1)} %copy-done.7, bf16[80,6144]{1,0:T(8,128)(2,1)} %collective-permute-done.20.refs_7_.refs_1_, bf16[80,6144]{1,0:T(8,128)(2,1)} %copy-done.5, ...), custom_call_target="tpu_custom_call" | custom-call | flops 1207959552 | bytes 7864320 | tf_op jit(solution)/shard_map/act_partials/pallas_call | solution.py:227
  282.1 5.6 %collective-permute-start.26 = (bf16[36,128,128]{2,1,0:T(8,128)(2,1)}, bf16[36,128,128]{2,1,0:T(8,128)(2,1)}, u32[]{:S(2)}, u32[]{:S(2)}) collective-permute-start(bf16[36,128,128]{2,1,0:T(8,128)(2,1)} %weight_terms.7), channel_id=1, source_target_pairs={{0,8},{4,12},{8,0},{12,4},{16,24},{20,28},{24,16},{28,20},{1,9},{5... | collective-permute-start | bytes 3538952 | tf_op jit(solution)/shard_map/ppermute | solution.py:339
  287.7 9.8 %weight_terms.9.sum_ref = f32[72,128,128]{2,1,0:T(8,128)} custom-call(s32[2]{0:T(128)} %pad_add_fusion.place_ref, s32[576]{0:T(1024)} %reduce.cols_ref, bf16[256,3072]{1,0:T(8,128)(2,1)} %copy-done, bf16[256,3072]{1,0:T(8,128)(2,1)} %copy-done, bf16[48,6144]{1,0:T(8,128)(2,1)} %copy-done.6, bf16[80,6144]{1,0:T(8,128)(2,1)} %copy-done.1, ...), custom_call_target="tpu_custom_call" | custom-call | flops 1207959552 | bytes 15728640 | tf_op jit(solution)/shard_map/weight_terms/pallas_call | solution.py:151
  297.8 5.6 %collective-permute-done.29 = bf16[256,768]{1,0:T(8,128)(2,1)S(1)} collective-permute-done((bf16[256,768]{1,0:T(8,128)(2,1)S(1)}, bf16[256,768]{1,0:T(8,128)(2,1)S(1)}, u32[]{:S(2)}, u32[]{:S(2)}) %collective-permute-start.29) | collective-permute-done | bytes 393248 | tf_op jit(solution)/shard_map/ppermute | solution.py:342
  305.1 4.8 %collective-permute-done.31.refs_1_ = bf16[128,768]{1,0:T(8,128)(2,1)S(1)} collective-permute-done((bf16[128,768]{1,0:T(8,128)(2,1)}, bf16[128,768]{1,0:T(8,128)(2,1)S(1)}, u32[]{:S(2)}, u32[]{:S(2)}) %collective-permute-start.31) | collective-permute-done | bytes 196640 | tf_op jit(solution)/shard_map/ppermute | solution.py:342
  310.0 31.8 %collective-permute-done.32.refs_2_ = bf16[128,768]{1,0:T(8,128)(2,1)S(1)} collective-permute-done((bf16[128,768]{1,0:T(8,128)(2,1)S(1)}, bf16[128,768]{1,0:T(8,128)(2,1)S(1)}, u32[]{:S(2)}, u32[]{:S(2)}) %collective-permute-start.32) | collective-permute-done | bytes 196640 | tf_op jit(solution)/shard_map/ppermute | solution.py:339
  343.9 3.6 collective-permute-done.33.refs_3_
  350.3 3.7 %add_part.2.refs_0_ = bf16[72,128,128]{2,1,0:T(8,128)(2,1)} custom-call(f32[72,128,128]{2,1,0:T(8,128)} %weight_terms.9.sum_ref, bf16[36,128,128]{2,1,0:T(8,128)(2,1)} %collective-permute-done.26.part_ref), custom_call_target="tpu_custom_call" | custom-call | flops 589824 | bytes 4718592 | tf_op jit(solution)/shard_map/add_part/pallas_call | solution.py:296
  354.0 3.7 %add_part.3 = bf16[72,128,128]{2,1,0:T(8,128)(2,1)} custom-call(f32[72,128,128]{2,1,0:T(8,128)} %weight_terms.9.sum_ref, bf16[36,128,128]{2,1,0:T(8,128)(2,1)} %copy-done.18, bf16[72,128,128]{2,1,0:T(8,128)(2,1)} %add_part.2.refs_0_), custom_call_target="tpu_custom_call", output_to_operand_aliasing={{}: (2, {})} | custom-call | flops 589824 | bytes 4718592 | tf_op jit(solution)/shard_map/add_part/pallas_call | solution.py:296
  (169 shorter events, 86.9 us)
Async XLA Ops:
  6.3 47.0 %collective-permute-start = (bf16[80,6144]{1,0:T(8,128)(2,1)S(1)}, bf16[80,6144]{1,0:T(8,128)(2,1)S(1)}, u32[]{:S(2)}, u32[]{:S(2)}) collective-permute-start(bf16[80,6144]{1,0:T(8,128)(2,1)S(1)} %fusion.11.refs_3_.refs_1_), channel_id=1, source_target_pairs={{0,16},{4,20},{8,24},{12,28},{16,0},{20,4},{24,8},{28,12},{1,17},{... | collective-permute-start | bytes 2949128 | tf_op jit(solution)/shard_map/ppermute | solution.py:339
  10.4 77.6 %collective-permute-start.7 = (bf16[80,6144]{1,0:T(8,128)(2,1)S(1)}, bf16[80,6144]{1,0:T(8,128)(2,1)}, u32[]{:S(2)}, u32[]{:S(2)}) collective-permute-start(bf16[80,6144]{1,0:T(8,128)(2,1)S(1)} %fusion.11.refs_3_.refs_1_), channel_id=1, source_target_pairs={{0,4},{4,0},{8,12},{12,8},{16,20},{20,16},{24,28},{28,24},{1,5},{5... | collective-permute-start | bytes 2949128 | tf_op jit(solution)/shard_map/ppermute | solution.py:339
  13.8 25.5 %collective-permute-start.3 = (bf16[64,1536]{1,0:T(8,128)(2,1)}, bf16[64,1536]{1,0:T(8,128)(2,1)S(1)}, u32[]{:S(2)}, u32[]{:S(2)}) collective-permute-start(bf16[64,1536]{1,0:T(8,128)(2,1)} %pad_maximum_fusion.3), channel_id=1, source_target_pairs={{0,4},{4,0},{8,12},{12,8},{16,20},{20,16},{24,28},{28,24},{1,5},{5... | collective-permute-start | bytes 589832 | tf_op jit(solution)/shard_map/ppermute | solution.py:339
  17.1 68.3 %collective-permute-start.8 = (bf16[80,6144]{1,0:T(8,128)(2,1)S(1)}, bf16[80,6144]{1,0:T(8,128)(2,1)}, u32[]{:S(2)}, u32[]{:S(2)}) collective-permute-start(bf16[80,6144]{1,0:T(8,128)(2,1)S(1)} %fusion.6.refs_4_.refs_2_), channel_id=1, source_target_pairs={{0,4},{4,0},{8,12},{12,8},{16,20},{20,16},{24,28},{28,24},{1,5},{5... | collective-permute-start | bytes 2949128 | tf_op jit(solution)/shard_map/ppermute | solution.py:339
  21.5 51.5 %collective-permute-start.9 = (bf16[48,6144]{1,0:T(8,128)(2,1)}, bf16[48,6144]{1,0:T(8,128)(2,1)}, u32[]{:S(2)}, u32[]{:S(2)}) collective-permute-start(bf16[48,6144]{1,0:T(8,128)(2,1)} %fusion.28.refs_5_.refs_3_), channel_id=1, source_target_pairs={{0,4},{4,0},{8,12},{12,8},{16,20},{20,16},{24,28},{28,24},{1,5},{5... | collective-permute-start | bytes 1769480 | tf_op jit(solution)/shard_map/ppermute | solution.py:339
  46.7 37.4 %collective-permute-start.6 = (bf16[48,6144]{1,0:T(8,128)(2,1)}, bf16[48,6144]{1,0:T(8,128)(2,1)S(1)}, u32[]{:S(2)}, u32[]{:S(2)}) collective-permute-start(bf16[48,6144]{1,0:T(8,128)(2,1)} %fusion.33.refs_2_.refs_0_), channel_id=1, source_target_pairs={{0,4},{4,0},{8,12},{12,8},{16,20},{20,16},{24,28},{28,24},{1,5},{5... | collective-permute-start | bytes 1769480 | tf_op jit(solution)/shard_map/ppermute | solution.py:339
  53.2 80.7 %collective-permute-start.13 = (bf16[48,6144]{1,0:T(8,128)(2,1)}, bf16[48,6144]{1,0:T(8,128)(2,1)S(1)}, u32[]{:S(2)}, u32[]{:S(2)}) collective-permute-start(bf16[48,6144]{1,0:T(8,128)(2,1)} %fusion.33.refs_2_.refs_0_), channel_id=1, source_target_pairs={{0,16},{4,20},{8,24},{12,28},{16,0},{20,4},{24,8},{28,12},{1,17},{... | collective-permute-start | bytes 1769480 | tf_op jit(solution)/shard_map/ppermute | solution.py:339
  73.1 118.7 %collective-permute-start.15 = (bf16[72,128,128]{2,1,0:T(8,128)(2,1)}, bf16[72,128,128]{2,1,0:T(8,128)(2,1)}, u32[]{:S(2)}, u32[]{:S(2)}) collective-permute-start(bf16[72,128,128]{2,1,0:T(8,128)(2,1)} %bitcast.6.refs_8_.refs_4_), channel_id=1, source_target_pairs={{0,8},{4,12},{8,0},{12,4},{16,24},{20,28},{24,16},{28,20},{1,9},{5... | collective-permute-start | bytes 7077896 | tf_op jit(solution)/shard_map/ppermute | solution.py:339
  84.2 45.0 %collective-permute-start.10 = (bf16[64,1536]{1,0:T(8,128)(2,1)}, bf16[64,1536]{1,0:T(8,128)(2,1)}, u32[]{:S(2)}, u32[]{:S(2)}) collective-permute-start(bf16[64,1536]{1,0:T(8,128)(2,1)} %pad_maximum_fusion.4), channel_id=1, source_target_pairs={{0,20},{4,16},{8,28},{12,24},{16,4},{20,0},{24,12},{28,8},{1,21},{... | collective-permute-start | bytes 589832 | tf_op jit(solution)/shard_map/ppermute | solution.py:339
  85.5 45.9 %collective-permute-start.2 = (bf16[64,1536]{1,0:T(8,128)(2,1)}, bf16[64,1536]{1,0:T(8,128)(2,1)S(1)}, u32[]{:S(2)}, u32[]{:S(2)}) collective-permute-start(bf16[64,1536]{1,0:T(8,128)(2,1)} %pad_maximum_fusion.2), channel_id=1, source_target_pairs={{0,16},{4,20},{8,24},{12,28},{16,0},{20,4},{24,8},{28,12},{1,17},{... | collective-permute-start | bytes 589832 | tf_op jit(solution)/shard_map/ppermute | solution.py:339
  133.9 55.4 %collective-permute-start.14 = (bf16[80,6144]{1,0:T(8,128)(2,1)S(1)}, bf16[80,6144]{1,0:T(8,128)(2,1)}, u32[]{:S(2)}, u32[]{:S(2)}) collective-permute-start(bf16[80,6144]{1,0:T(8,128)(2,1)S(1)} %copy-done.4), channel_id=1, source_target_pairs={{0,16},{4,20},{8,24},{12,28},{16,0},{20,4},{24,8},{28,12},{1,17},{... | collective-permute-start | bytes 2949128 | tf_op jit(solution)/shard_map/ppermute | solution.py:339
  140.2 50.6 %collective-permute-start.12 = (bf16[128,3072]{1,0:T(8,128)(2,1)S(1)}, bf16[128,3072]{1,0:T(8,128)(2,1)S(1)}, u32[]{:S(2)}, u32[]{:S(2)}) collective-permute-start(bf16[128,3072]{1,0:T(8,128)(2,1)S(1)} %pad_maximum_fusion), channel_id=1, source_target_pairs={{0,1},{1,0},{2,3},{3,2},{4,5},{5,4},{6,7},{7,6},{8,9},{9,8},{10,11... | collective-permute-start | bytes 2359304 | tf_op jit(solution)/shard_map/ppermute | solution.py:342
  140.9 69.5 %collective-permute-start.1 = (bf16[48,6144]{1,0:T(8,128)(2,1)}, bf16[48,6144]{1,0:T(8,128)(2,1)}, u32[]{:S(2)}, u32[]{:S(2)}) collective-permute-start(bf16[48,6144]{1,0:T(8,128)(2,1)} %fusion.28.refs_5_.refs_3_), channel_id=1, source_target_pairs={{0,16},{4,20},{8,24},{12,28},{16,0},{20,4},{24,8},{28,12},{1,17},{... | collective-permute-start | bytes 1769480 | tf_op jit(solution)/shard_map/ppermute | solution.py:339
  144.2 93.6 %collective-permute-start.20 = (bf16[80,6144]{1,0:T(8,128)(2,1)S(1)}, bf16[80,6144]{1,0:T(8,128)(2,1)}, u32[]{:S(2)}, u32[]{:S(2)}) collective-permute-start(bf16[80,6144]{1,0:T(8,128)(2,1)S(1)} %collective-permute-done.refs_1_.refs_3_), channel_id=1, source_target_pairs={{0,4},{4,0},{8,12},{12,8},{16,20},{20,16},{24,28},{28,24},{1,5},{5... | collective-permute-start | bytes 2949128 | tf_op jit(solution)/shard_map/ppermute | solution.py:339
  189.4 48.5 %collective-permute-start.21 = (bf16[80,6144]{1,0:T(8,128)(2,1)}, bf16[80,6144]{1,0:T(8,128)(2,1)S(1)}, u32[]{:S(2)}, u32[]{:S(2)}) collective-permute-start(bf16[80,6144]{1,0:T(8,128)(2,1)} %collective-permute-done.14.refs_2_.refs_4_), channel_id=1, source_target_pairs={{0,4},{4,0},{8,12},{12,8},{16,20},{20,16},{24,28},{28,24},{1,5},{5... | collective-permute-start | bytes 2949128 | tf_op jit(solution)/shard_map/ppermute | solution.py:339
  221.9 27.6 %collective-permute-start.22 = (bf16[48,6144]{1,0:T(8,128)(2,1)}, bf16[48,6144]{1,0:T(8,128)(2,1)S(1)}, u32[]{:S(2)}, u32[]{:S(2)}) collective-permute-start(bf16[48,6144]{1,0:T(8,128)(2,1)} %collective-permute-done.1.refs_3_.refs_5_), channel_id=1, source_target_pairs={{0,4},{4,0},{8,12},{12,8},{16,20},{20,16},{24,28},{28,24},{1,5},{5... | collective-permute-start | bytes 1769480 | tf_op jit(solution)/shard_map/ppermute | solution.py:339
  224.6 40.8 %collective-permute-start.23 = (bf16[128,768]{1,0:T(8,128)(2,1)S(1)}, bf16[128,768]{1,0:T(8,128)(2,1)}, u32[]{:S(2)}, u32[]{:S(2)}) collective-permute-start(bf16[128,768]{1,0:T(8,128)(2,1)S(1)} %get-tuple-element.75), channel_id=1, source_target_pairs={{0,2},{1,3},{2,0},{3,1},{4,6},{5,7},{6,4},{7,5},{8,10},{9,11},{10,... | collective-permute-start | bytes 589832 | tf_op jit(solution)/shard_map/ppermute | solution.py:342
  281.6 21.8 %collective-permute-start.29 = (bf16[256,768]{1,0:T(8,128)(2,1)S(1)}, bf16[256,768]{1,0:T(8,128)(2,1)S(1)}, u32[]{:S(2)}, u32[]{:S(2)}) collective-permute-start(bf16[256,768]{1,0:T(8,128)(2,1)S(1)} %copy-done.14), channel_id=1, source_target_pairs={{0,2},{1,3},{2,0},{3,1},{4,6},{5,7},{6,4},{7,5},{8,10},{9,11},{10,... | collective-permute-start | bytes 1179656 | tf_op jit(solution)/shard_map/ppermute | solution.py:342
  282.1 21.4 %collective-permute-start.27 = (bf16[128,768]{1,0:T(8,128)(2,1)S(1)}, bf16[128,768]{1,0:T(8,128)(2,1)}, u32[]{:S(2)}, u32[]{:S(2)}) collective-permute-start(bf16[128,768]{1,0:T(8,128)(2,1)S(1)} %add_convert_fusion.7), channel_id=1, source_target_pairs={{0,16},{4,20},{8,24},{12,28},{16,0},{20,4},{24,8},{28,12},{1,17},{... | collective-permute-start | bytes 589832 | tf_op jit(solution)/shard_map/ppermute | solution.py:339
  282.1 65.4 %collective-permute-start.26 = (bf16[36,128,128]{2,1,0:T(8,128)(2,1)}, bf16[36,128,128]{2,1,0:T(8,128)(2,1)}, u32[]{:S(2)}, u32[]{:S(2)}) collective-permute-start(bf16[36,128,128]{2,1,0:T(8,128)(2,1)} %weight_terms.7), channel_id=1, source_target_pairs={{0,8},{4,12},{8,0},{12,4},{16,24},{20,28},{24,16},{28,20},{1,9},{5... | collective-permute-start | bytes 3538952 | tf_op jit(solution)/shard_map/ppermute | solution.py:339
  297.5 50.5 %collective-permute-start.25 = (bf16[36,128,128]{2,1,0:T(8,128)(2,1)S(1)}, bf16[36,128,128]{2,1,0:T(8,128)(2,1)S(1)}, u32[]{:S(2)}, u32[]{:S(2)}) collective-permute-start(bf16[36,128,128]{2,1,0:T(8,128)(2,1)S(1)} %copy-done.17), channel_id=1, source_target_pairs={{0,8},{4,12},{8,0},{12,4},{16,24},{20,28},{24,16},{28,20},{1,9},{5... | collective-permute-start | bytes 3538952 | tf_op jit(solution)/shard_map/ppermute | solution.py:339
  304.0 39.3 %collective-permute-start.38 = (bf16[256,768]{1,0:T(8,128)(2,1)S(1)}, bf16[256,768]{1,0:T(8,128)(2,1)S(1)}, u32[]{:S(2)}, u32[]{:S(2)}) collective-permute-start(bf16[256,768]{1,0:T(8,128)(2,1)S(1)} %add_convert_fusion), channel_id=1, source_target_pairs={{0,4},{4,0},{8,12},{12,8},{16,20},{20,16},{24,28},{28,24},{1,5},{5... | collective-permute-start | bytes 1179656 | tf_op jit(solution)/shard_map/ppermute | solution.py:339
  305.1 36.7 %collective-permute-start.32 = (bf16[128,768]{1,0:T(8,128)(2,1)S(1)}, bf16[128,768]{1,0:T(8,128)(2,1)S(1)}, u32[]{:S(2)}, u32[]{:S(2)}) collective-permute-start(bf16[128,768]{1,0:T(8,128)(2,1)S(1)} %add_convert_fusion.6), channel_id=1, source_target_pairs={{0,20},{4,16},{8,28},{12,24},{16,4},{20,0},{24,12},{28,8},{1,21},{... | collective-permute-start | bytes 589832 | tf_op jit(solution)/shard_map/ppermute | solution.py:339
  310.0 33.4 %collective-permute-start.39 = (bf16[256,768]{1,0:T(8,128)(2,1)S(1)}, bf16[256,768]{1,0:T(8,128)(2,1)S(1)}, u32[]{:S(2)}, u32[]{:S(2)}) collective-permute-start(bf16[256,768]{1,0:T(8,128)(2,1)S(1)} %add_convert_fusion.1.refs_0_), channel_id=1, source_target_pairs={{0,1},{1,0},{2,3},{3,2},{4,5},{5,4},{6,7},{7,6},{8,9},{9,8},{10,11... | collective-permute-start | bytes 1179656 | tf_op jit(solution)/shard_map/ppermute | solution.py:342
  (47 other events, 633.4 us)

commit v3 on v2

--- a/solution.py
+++ b/solution.py
@@ -79,7 +79,7 @@
 
 
 SIDE, NEAR, FAR = 1, 2, 4
-CHUNKS = (3, 5, 5, 3)
+CHUNKS = (6, 5, 3, 2)
 
 
 def columns_of(chunk_refs, spans):
@@ -378,14 +378,14 @@
         if hid_own:
             pre_act = after(pre_act, hid_own[-1])
         hid_own.append(hidden_gradient(pre_act[rows_of], grad_act[rows_of]))
-        if index < 2:
-            hid_far.append(swap(hid_own[index], FAR))
+        if index == 0:
+            hid_far.append(swap(hid_own[0], FAR))
         hid_side.append(swap(hid_own[-1], SIDE))
 
     side_acts = gathered([share_of(SIDE, hid_own[1])])
     far_shares = [share_of(FAR, hid_own[1]), share_of(FAR | SIDE, hid_own[1])]
     own_weight = kept_weight[0]
-    near_weight = swap(after(own_weight, hid_own[-1]), NEAR)
+    near_weight = swap(after(own_weight, hid_own[0]), NEAR)
 
     near_place = jnp.stack([place ^ NEAR, 1 - near]).astype(jnp.int32)
     own_place = jnp.stack([place, near]).astype(jnp.int32)
@@ -424,15 +424,17 @@
         return lax.dynamic_slice_in_dim(value, which * token_half, token_half, 0)
 
     hid_both = [swap(hid_far[0], SIDE)]
-    hid_far.append(swap(after(hid_own[2], hid_far[0]), FAR))
-    hid_both.append(swap(hid_far[1], SIDE))
-    hid_far.append(swap(after(hid_own[3], hid_far[1]), FAR))
-    near_sum = first_terms(after(near_place, hid_far[1]))
+    hid_far.append(swap(after(hid_own[1], hid_far[0]), FAR))
+    near_sum = first_terms(after(near_place, hid_far[0]))
     own_sum = first_terms(after(own_place, near_sum))
     far_acts = gathered(far_shares, own_sum)
-    third = after(hid_far[2], own_sum)
+    second = after(hid_far[1], own_sum)
+    hid_both.append(swap(second, SIDE))
+    hid_far.append(swap(after(hid_own[2], second), FAR))
+    parts = acts_of([hid_own, hid_side], second)
+    third = after(hid_far[2], parts[0])
     hid_both.append(swap(third, SIDE))
-    parts = acts_of([hid_own, hid_side], third)
+    hid_far.append(swap(after(hid_own[3], third), FAR))
     near_cores = [core_sum(parts[0], parts[1]), core_sum(parts[2], parts[3])]
     near_got = [partner(value, 2) for value in near_cores]
     fourth = after(hid_far[3], far_acts, *near_cores)
@@ -476,9 +478,6 @@
     ]
     unit = (place & (FAR | SIDE)) + NEAR * core
     mine = [halves[0], swap(halves[1], SIDE)]
-    quarters = []
-    for value in (after(far_back, *halves), both_back):
-        quarters.append([value, partner(value, 2)])
 
     def put(bits_of, arrays, parts_of, whole):
         there_units = [unit ^ bits for bits in bits_of]
@@ -490,14 +489,21 @@
             activations.shape,
         )
 
+    weight_grad = add_part(own_sum, after(came[0], *halves), 0, per_row, None)
+    far_back = after(far_back, weight_grad)
+    far_pair = [far_back, partner(far_back, 2)]
+    both_back = after(both_back, far_back)
+    both_pair = [both_back, partner(both_back, 2)]
     zero = core * 0
-    act_grad = put([0, SIDE], mine, [zero, zero], None)
+    near_put = put([0, SIDE], mine, [zero, zero], None)
+    for k, value in list(enumerate(came))[1:]:
+        weight_grad = add_part(own_sum, after(value, near_put), k, per_row, weight_grad)
     act_grad = put(
-        [FAR, FAR, FAR | SIDE, FAR | SIDE], quarters[0] + quarters[1], [turn, 1 - turn] * 2, act_grad
-    )
-    weight_grad = None
-    for k, value in enumerate(came):
-        weight_grad = add_part(own_sum, value, k, per_row, weight_grad)
+        [FAR, FAR, FAR | SIDE, FAR | SIDE],
+        far_pair + both_pair,
+        [turn, 1 - turn] * 2,
+        near_put,
+    )
     return (weight_grad[None], act_grad)
 
 

time: 370 us -> 378 us (1.022)
  other arithmetic: 22.1 us -> 29.4 us
    ppermute x21, waiting for transfers between devices: 172 us -> 177 us  [swap(): return lax.ppermute(value, 'dp', [(d, d ^ bits) for d in range(dp_size)])]
  transfers between devices with their start and end apart: 41 -> 41, of which waited for: 18 -> 19; matrix products, arithmetic and copies ran while one was open for 5% -> 10% of each run, Pallas kernels for 21% -> 21%
where the time goes in v3:
time: 378 us; the launch traced here: 375 us
  waiting for transfers between devices  198 us (52%)
  Pallas kernels  91 us (24%)
  starting transfers between devices  41.8 us (11%)
  other arithmetic  29.4 us (8%)
  local copies, waits for them, and re-layouts  13.6 us (4%)
    ppermute x21, waiting for transfers between devices, swap(): return lax.ppermute(value, 'dp', [(d, d ^ bits) for d in range(dp_size)])  177 us
    pallas_call x5, Pallas kernels, weight_terms(): pl.pallas_call(functools.partial(weight_term_kernel, per_row, rows, first...  43.3 us
    pallas_call x3, Pallas kernels, act_partials(): pl.pallas_call(functools.partial(act_kernel, per_row, rows, len(hids), le...  33.7 us
    ppermute x21, starting transfers between devices, swap(): return lax.ppermute(value, 'dp', [(d, d ^ bits) for d in range(dp_size)])  31 us
    ppermute x20, waiting for transfers between devices, partner(): lax.ppermute(value, 'tensor', [(t, t ^ bit) for t in range(tensor_size)])  21.7 us
    convert_element_type x4, other arithmetic, hidden_gradient(): (grad_act.astype(jnp.float32) * gelu_slope(pre_act)).astype(jnp.bfloat16)  12.3 us
    ppermute x20, starting transfers between devices, partner(): lax.ppermute(value, 'tensor', [(t, t ^ bit) for t in range(tensor_size)])  10.8 us
    convert_element_type x8, other arithmetic, add_up(): (left.astype(jnp.float32) + right.astype(jnp.float32)).astype(jnp.bfloat16)  8.75 us
  transfers between devices with their start and end apart: 41, of which 19 were waited for; matrix products, arithmetic and copies ran while one was open for 10% of the time, Pallas kernels for 21%

profile of v3, /device:TPU:0, one launch (start us, length us, event | category | flops | bytes accessed | tf_op | source)
XLA Modules:
  0.0 375.2 jit_solution(11269911467682636361)
XLA Ops:
  3.8 4.1 %collective-permute-start = (bf16[96,6144]{1,0:T(8,128)(2,1)S(1)}, bf16[96,6144]{1,0:T(8,128)(2,1)S(1)}, u32[]{:S(2)}, u32[]{:S(2)}) collective-permute-start(bf16[96,6144]{1,0:T(8,128)(2,1)S(1)} %fusion.6.refs_2_.refs_0_), channel_id=1, source_target_pairs={{0,16},{4,20},{8,24},{12,28},{16,0},{20,4},{24,8},{28,12},{1,17},{... | collective-permute-start | bytes 3538952 | tf_op jit(solution)/shard_map/ppermute | solution.py:339
  9.5 3.8 %fusion.16.refs_3_.refs_1_ = bf16[80,6144]{1,0:T(8,128)(2,1)} fusion(bf16[256,6144]{1,0:T(8,128)(2,1)} %param.6, bf16[256,6144]{1,0:T(8,128)(2,1)} %param.7), kind=kLoop, calls=%fused_computation.28 | loop fusion | flops 9830400 | bytes 2949120 | tf_op jit(solution)/shard_map/convert_element_type | solution.py:25
  26.9 35.2 %collective-permute-done.2 = bf16[64,1536]{1,0:T(8,128)(2,1)} collective-permute-done((bf16[64,1536]{1,0:T(8,128)(2,1)}, bf16[64,1536]{1,0:T(8,128)(2,1)}, u32[]{:S(2)}, u32[]{:S(2)}) %collective-permute-start.2) | collective-permute-done | bytes 196640 | tf_op jit(solution)/shard_map/ppermute | solution.py:339
  74.6 8.3 %collective-permute-done.8.refs_9_.refs_7_ = bf16[32,6144]{1,0:T(8,128)(2,1)S(1)} collective-permute-done((bf16[32,6144]{1,0:T(8,128)(2,1)S(1)}, bf16[32,6144]{1,0:T(8,128)(2,1)S(1)}, u32[]{:S(2)}, u32[]{:S(2)}) %collective-permute-start.8) | collective-permute-done | bytes 393248 | tf_op jit(solution)/shard_map/ppermute | solution.py:339
  83.0 3.8 %collective-permute-start.13 = (bf16[64,1536]{1,0:T(8,128)(2,1)}, bf16[64,1536]{1,0:T(8,128)(2,1)}, u32[]{:S(2)}, u32[]{:S(2)}) collective-permute-start(bf16[64,1536]{1,0:T(8,128)(2,1)} %pad_maximum_fusion.4), channel_id=1, source_target_pairs={{0,20},{4,16},{8,28},{12,24},{16,4},{20,0},{24,12},{28,8},{1,21},{... | collective-permute-start | bytes 589832 | tf_op jit(solution)/shard_map/ppermute | solution.py:339
  87.8 9.3 %weight_terms.5.refs_10_ = f32[72,128,128]{2,1,0:T(8,128)} custom-call(s32[2]{0:T(128)} %pad_add_fusion.2.place_ref, s32[576]{0:T(1024)} %reduce.cols_ref, bf16[256,6144]{1,0:T(8,128)(2,1)} %refs_0_.3, bf16[256,1536]{1,0:T(8,128)(2,1)} %copy-done.6, bf16[96,6144]{1,0:T(8,128)(2,1)} %copy-done.2, bf16[80,6144]{1,0:T(8,128)(2,1)} %fusion.16.refs_3_.refs_1_, ...), custom_call_target="tpu_custom_call" | custom-call | flops 1207959552 | bytes 15728640 | tf_op jit(solution)/shard_map/weight_terms/pallas_call | solution.py:151
  97.1 9.1 %weight_terms.6.refs_10_ = f32[72,128,128]{2,1,0:T(8,128)} custom-call(s32[2]{0:T(128)} %pad_add_fusion.place_ref, s32[576]{0:T(1024)} %reduce.cols_ref, bf16[256,6144]{1,0:T(8,128)(2,1)} %refs_0_.3, bf16[256,1536]{1,0:T(8,128)(2,1)} %copy-done.6, bf16[96,6144]{1,0:T(8,128)(2,1)} %copy-done.2, bf16[80,6144]{1,0:T(8,128)(2,1)} %fusion.16.refs_3_.refs_1_, ...), custom_call_target="tpu_custom_call" | custom-call | flops 1207959552 | bytes 15728640 | tf_op jit(solution)/shard_map/weight_terms/pallas_call | solution.py:151
  106.2 24.5 %collective-permute-done.12 = bf16[64,1536]{1,0:T(8,128)(2,1)} collective-permute-done((bf16[64,1536]{1,0:T(8,128)(2,1)}, bf16[64,1536]{1,0:T(8,128)(2,1)}, u32[]{:S(2)}, u32[]{:S(2)}) %collective-permute-start.12) | collective-permute-done | bytes 196640 | tf_op jit(solution)/shard_map/ppermute | solution.py:339
  147.7 36.2 %collective-permute-done.1.refs_1_.refs_3_ = bf16[80,6144]{1,0:T(8,128)(2,1)} collective-permute-done((bf16[80,6144]{1,0:T(8,128)(2,1)}, bf16[80,6144]{1,0:T(8,128)(2,1)}, u32[]{:S(2)}, u32[]{:S(2)}) %collective-permute-start.1) | collective-permute-done | bytes 983072 | tf_op jit(solution)/shard_map/ppermute | solution.py:339
  185.4 13.7 %act_partials.3 = (bf16[256,768]{1,0:T(8,128)(2,1)}, bf16[256,768]{1,0:T(8,128)(2,1)}, bf16[256,768]{1,0:T(8,128)(2,1)}, bf16[256,768]{1,0:T(8,128)(2,1)}) custom-call(s32[3]{0:T(128)} %pad_add_fusion.1.place_ref, s32[576]{0:T(1024)} %reduce.cols_ref, bf16[96,6144]{1,0:T(8,128)(2,1)} %copy-done.2, bf16[80,6144]{1,0:T(8,128)(2,1)} %fusion.16.refs_3_.refs_1_, ...), custom_call_target="tpu_custom_call" | custom-call | flops 2415919104 | bytes 11010048 | tf_op jit(solution)/shard_map/act_partials/pallas_call | solution.py:227
  201.8 8.4 %collective-permute-done.9.refs_2_.refs_4_ = bf16[48,6144]{1,0:T(8,128)(2,1)S(1)} collective-permute-done((bf16[48,6144]{1,0:T(8,128)(2,1)}, bf16[48,6144]{1,0:T(8,128)(2,1)S(1)}, u32[]{:S(2)}, u32[]{:S(2)}) %collective-permute-start.9) | collective-permute-done | bytes 589856 | tf_op jit(solution)/shard_map/ppermute | solution.py:339
  213.2 15.3 %collective-permute-done.11.refs_3_.refs_5_ = bf16[32,6144]{1,0:T(8,128)(2,1)} collective-permute-done((bf16[32,6144]{1,0:T(8,128)(2,1)}, bf16[32,6144]{1,0:T(8,128)(2,1)}, u32[]{:S(2)}, u32[]{:S(2)}) %collective-permute-start.11) | collective-permute-done | bytes 393248 | tf_op jit(solution)/shard_map/ppermute | solution.py:339
  228.5 9.9 %act_partials.4 = (bf16[256,768]{1,0:T(8,128)(2,1)}, bf16[256,768]{1,0:T(8,128)(2,1)}) custom-call(s32[3]{0:T(128)} %pad_add_fusion.1.place_ref, s32[576]{0:T(1024)} %reduce.cols_ref, bf16[96,6144]{1,0:T(8,128)(2,1)} %copy-done.1, bf16[80,6144]{1,0:T(8,128)(2,1)} %collective-permute-done.1.refs_1_.refs_3_, bf16[48,6144]{1,0:T(8,128)(2,1)} %copy-done.4, ...), custom_call_target="tpu_custom_call" | custom-call | flops 1207959552 | bytes 7864320 | tf_op jit(solution)/shard_map/act_partials/pallas_call | solution.py:227
  243.0 12.7 %collective-permute-done.21.refs_8_.refs_2_ = bf16[48,6144]{1,0:T(8,128)(2,1)S(1)} collective-permute-done((bf16[48,6144]{1,0:T(8,128)(2,1)}, bf16[48,6144]{1,0:T(8,128)(2,1)S(1)}, u32[]{:S(2)}, u32[]{:S(2)}) %collective-permute-start.21) | collective-permute-done | bytes 589856 | tf_op jit(solution)/shard_map/ppermute | solution.py:339
  255.6 7.5 %collective-permute-done.22.refs_9_.refs_3_ = bf16[32,6144]{1,0:T(8,128)(2,1)S(1)} collective-permute-done((bf16[32,6144]{1,0:T(8,128)(2,1)}, bf16[32,6144]{1,0:T(8,128)(2,1)S(1)}, u32[]{:S(2)}, u32[]{:S(2)}) %collective-permute-start.22) | collective-permute-done | bytes 393248 | tf_op jit(solution)/shard_map/ppermute | solution.py:339
  263.9 7.5 %weight_terms.7 = bf16[36,128,128]{2,1,0:T(8,128)(2,1)} custom-call(s32[2]{0:T(128)} %pad_add_fusion.2.place_ref, s32[576]{0:T(1024)} %reduce.cols_ref, bf16[256,3072]{1,0:T(8,128)(2,1)} %copy-done, bf16[256,3072]{1,0:T(8,128)(2,1)} %copy-done, bf16[96,6144]{1,0:T(8,128)(2,1)} %copy-done.1, bf16[80,6144]{1,0:T(8,128)(2,1)} %collective-permute-done.1.refs_1_.refs_3_, ...), custom_call_target="tpu_custom_call" | custom-call | flops 603979776 | bytes 11010048 | tf_op jit(solution)/shard_map/weight_terms/pallas_call | solution.py:151
  271.4 7.6 %weight_terms.8 = bf16[36,128,128]{2,1,0:T(8,128)(2,1)} custom-call(s32[2]{0:T(128)} %pad_add_fusion.2.place_ref, s32[576]{0:T(1024)} %reduce.cols_ref, bf16[256,3072]{1,0:T(8,128)(2,1)} %copy-done, bf16[256,3072]{1,0:T(8,128)(2,1)} %copy-done, bf16[96,6144]{1,0:T(8,128)(2,1)} %copy-done.1, bf16[80,6144]{1,0:T(8,128)(2,1)} %collective-permute-done.1.refs_1_.refs_3_, ...), custom_call_target="tpu_custom_call" | custom-call | flops 603979776 | bytes 11010048 | tf_op jit(solution)/shard_map/weight_terms/pallas_call | solution.py:151
  279.8 10.1 %act_partials.5 = (bf16[256,768]{1,0:T(8,128)(2,1)}, bf16[256,768]{1,0:T(8,128)(2,1)}) custom-call(s32[3]{0:T(128)} %pad_add_fusion.1.place_ref, s32[576]{0:T(1024)} %reduce.cols_ref, bf16[96,6144]{1,0:T(8,128)(2,1)} %collective-permute-done.19.refs_6_.refs_0_, bf16[80,6144]{1,0:T(8,128)(2,1)} %collective-permute-done.20.refs_7_.refs_1_, ...), custom_call_target="tpu_custom_call" | custom-call | flops 1207959552 | bytes 7864320 | tf_op jit(solution)/shard_map/act_partials/pallas_call | solution.py:227
  297.3 9.8 %weight_terms.9.sum_ref = f32[72,128,128]{2,1,0:T(8,128)} custom-call(s32[2]{0:T(128)} %pad_add_fusion.place_ref, s32[576]{0:T(1024)} %reduce.cols_ref, bf16[256,3072]{1,0:T(8,128)(2,1)} %copy-done, bf16[256,3072]{1,0:T(8,128)(2,1)} %copy-done, bf16[96,6144]{1,0:T(8,128)(2,1)} %copy-done.1, bf16[80,6144]{1,0:T(8,128)(2,1)} %collective-permute-done.1.refs_1_.refs_3_, ...), custom_call_target="tpu_custom_call" | custom-call | flops 1207959552 | bytes 15728640 | tf_op jit(solution)/shard_map/weight_terms/pallas_call | solution.py:151
  321.4 6.0 %collective-permute-done.32.part_ref = bf16[36,128,128]{2,1,0:T(8,128)(2,1)} collective-permute-done((bf16[36,128,128]{2,1,0:T(8,128)(2,1)S(1)}, bf16[36,128,128]{2,1,0:T(8,128)(2,1)}, u32[]{:S(2)}, u32[]{:S(2)}) %collective-permute-start.32) | collective-permute-done | bytes 1179680 | tf_op jit(solution)/shard_map/ppermute | solution.py:339
  327.9 3.7 add_part.2.refs_0_
  331.6 15.3 %collective-permute-done.33.refs_0_ = bf16[128,768]{1,0:T(8,128)(2,1)} collective-permute-done((bf16[128,768]{1,0:T(8,128)(2,1)}, bf16[128,768]{1,0:T(8,128)(2,1)}, u32[]{:S(2)}, u32[]{:S(2)}) %collective-permute-start.33) | collective-permute-done | bytes 196640 | tf_op jit(solution)/shard_map/ppermute | solution.py:339
  352.6 5.9 %collective-permute-done.36.refs_3_ = bf16[128,768]{1,0:T(8,128)(2,1)S(1)} collective-permute-done((bf16[128,768]{1,0:T(8,128)(2,1)}, bf16[128,768]{1,0:T(8,128)(2,1)S(1)}, u32[]{:S(2)}, u32[]{:S(2)}) %collective-permute-start.36) | collective-permute-done | bytes 196640 | tf_op jit(solution)/shard_map/ppermute | solution.py:342
  366.5 3.7 add_part.3
  (163 shorter events, 102.5 us)
Async XLA Ops:
  3.8 69.0 %collective-permute-start = (bf16[96,6144]{1,0:T(8,128)(2,1)S(1)}, bf16[96,6144]{1,0:T(8,128)(2,1)S(1)}, u32[]{:S(2)}, u32[]{:S(2)}) collective-permute-start(bf16[96,6144]{1,0:T(8,128)(2,1)S(1)} %fusion.6.refs_2_.refs_0_), channel_id=1, source_target_pairs={{0,16},{4,20},{8,24},{12,28},{16,0},{20,4},{24,8},{28,12},{1,17},{... | collective-permute-start | bytes 3538952 | tf_op jit(solution)/shard_map/ppermute | solution.py:339
  8.0 78.8 %collective-permute-start.5 = (bf16[96,6144]{1,0:T(8,128)(2,1)S(1)}, bf16[96,6144]{1,0:T(8,128)(2,1)S(1)}, u32[]{:S(2)}, u32[]{:S(2)}) collective-permute-start(bf16[96,6144]{1,0:T(8,128)(2,1)S(1)} %fusion.6.refs_2_.refs_0_), channel_id=1, source_target_pairs={{0,4},{4,0},{8,12},{12,8},{16,20},{20,16},{24,28},{28,24},{1,5},{5... | collective-permute-start | bytes 3538952 | tf_op jit(solution)/shard_map/ppermute | solution.py:339
  13.2 73.5 %collective-permute-start.6 = (bf16[80,6144]{1,0:T(8,128)(2,1)}, bf16[80,6144]{1,0:T(8,128)(2,1)}, u32[]{:S(2)}, u32[]{:S(2)}) collective-permute-start(bf16[80,6144]{1,0:T(8,128)(2,1)} %fusion.16.refs_3_.refs_1_), channel_id=1, source_target_pairs={{0,4},{4,0},{8,12},{12,8},{16,20},{20,16},{24,28},{28,24},{1,5},{5... | collective-permute-start | bytes 2949128 | tf_op jit(solution)/shard_map/ppermute | solution.py:339
  16.4 45.8 %collective-permute-start.2 = (bf16[64,1536]{1,0:T(8,128)(2,1)}, bf16[64,1536]{1,0:T(8,128)(2,1)}, u32[]{:S(2)}, u32[]{:S(2)}) collective-permute-start(bf16[64,1536]{1,0:T(8,128)(2,1)} %pad_maximum_fusion.2), channel_id=1, source_target_pairs={{0,4},{4,0},{8,12},{12,8},{16,20},{20,16},{24,28},{28,24},{1,5},{5... | collective-permute-start | bytes 589832 | tf_op jit(solution)/shard_map/ppermute | solution.py:339
  20.7 62.2 %collective-permute-start.7 = (bf16[48,6144]{1,0:T(8,128)(2,1)}, bf16[48,6144]{1,0:T(8,128)(2,1)}, u32[]{:S(2)}, u32[]{:S(2)}) collective-permute-start(bf16[48,6144]{1,0:T(8,128)(2,1)} %fusion.27.refs_4_.refs_2_), channel_id=1, source_target_pairs={{0,4},{4,0},{8,12},{12,8},{16,20},{20,16},{24,28},{28,24},{1,5},{5... | collective-permute-start | bytes 1769480 | tf_op jit(solution)/shard_map/ppermute | solution.py:339
  72.9 112.5 %collective-permute-start.10 = (bf16[72,128,128]{2,1,0:T(8,128)(2,1)}, bf16[72,128,128]{2,1,0:T(8,128)(2,1)}, u32[]{:S(2)}, u32[]{:S(2)}) collective-permute-start(bf16[72,128,128]{2,1,0:T(8,128)(2,1)} %bitcast.6.refs_8_.refs_4_), channel_id=1, source_target_pairs={{0,8},{4,12},{8,0},{12,4},{16,24},{20,28},{24,16},{28,20},{1,9},{5... | collective-permute-start | bytes 7077896 | tf_op jit(solution)/shard_map/ppermute | solution.py:339
  82.9 47.8 %collective-permute-start.12 = (bf16[64,1536]{1,0:T(8,128)(2,1)}, bf16[64,1536]{1,0:T(8,128)(2,1)}, u32[]{:S(2)}, u32[]{:S(2)}) collective-permute-start(bf16[64,1536]{1,0:T(8,128)(2,1)} %pad_maximum_fusion.3), channel_id=1, source_target_pairs={{0,16},{4,20},{8,24},{12,28},{16,0},{20,4},{24,8},{28,12},{1,17},{... | collective-permute-start | bytes 589832 | tf_op jit(solution)/shard_map/ppermute | solution.py:339
  83.0 51.2 %collective-permute-start.13 = (bf16[64,1536]{1,0:T(8,128)(2,1)}, bf16[64,1536]{1,0:T(8,128)(2,1)}, u32[]{:S(2)}, u32[]{:S(2)}) collective-permute-start(bf16[64,1536]{1,0:T(8,128)(2,1)} %pad_maximum_fusion.4), channel_id=1, source_target_pairs={{0,20},{4,16},{8,28},{12,24},{16,4},{20,0},{24,12},{28,8},{1,21},{... | collective-permute-start | bytes 589832 | tf_op jit(solution)/shard_map/ppermute | solution.py:339
  138.2 45.7 %collective-permute-start.1 = (bf16[80,6144]{1,0:T(8,128)(2,1)}, bf16[80,6144]{1,0:T(8,128)(2,1)}, u32[]{:S(2)}, u32[]{:S(2)}) collective-permute-start(bf16[80,6144]{1,0:T(8,128)(2,1)} %fusion.16.refs_3_.refs_1_), channel_id=1, source_target_pairs={{0,16},{4,20},{8,24},{12,28},{16,0},{20,4},{24,8},{28,12},{1,17},{... | collective-permute-start | bytes 2949128 | tf_op jit(solution)/shard_map/ppermute | solution.py:339
  141.6 101.4 %collective-permute-start.19 = (bf16[96,6144]{1,0:T(8,128)(2,1)S(1)}, bf16[96,6144]{1,0:T(8,128)(2,1)}, u32[]{:S(2)}, u32[]{:S(2)}) collective-permute-start(bf16[96,6144]{1,0:T(8,128)(2,1)S(1)} %collective-permute-done.refs_0_.refs_2_), channel_id=1, source_target_pairs={{0,4},{4,0},{8,12},{12,8},{16,20},{20,16},{24,28},{28,24},{1,5},{5... | collective-permute-start | bytes 3538952 | tf_op jit(solution)/shard_map/ppermute | solution.py:339
  147.4 52.2 %collective-permute-start.15 = (bf16[128,3072]{1,0:T(8,128)(2,1)}, bf16[128,3072]{1,0:T(8,128)(2,1)}, u32[]{:S(2)}, u32[]{:S(2)}) collective-permute-start(bf16[128,3072]{1,0:T(8,128)(2,1)} %pad_maximum_fusion), channel_id=1, source_target_pairs={{0,1},{1,0},{2,3},{3,2},{4,5},{5,4},{6,7},{7,6},{8,9},{9,8},{10,11... | collective-permute-start | bytes 2359304 | tf_op jit(solution)/shard_map/ppermute | solution.py:342
  183.9 59.1 %collective-permute-start.20 = (bf16[80,6144]{1,0:T(8,128)(2,1)}, bf16[80,6144]{1,0:T(8,128)(2,1)}, u32[]{:S(2)}, u32[]{:S(2)}) collective-permute-start(bf16[80,6144]{1,0:T(8,128)(2,1)} %collective-permute-done.1.refs_1_.refs_3_), channel_id=1, source_target_pairs={{0,4},{4,0},{8,12},{12,8},{16,20},{20,16},{24,28},{28,24},{1,5},{5... | collective-permute-start | bytes 2949128 | tf_op jit(solution)/shard_map/ppermute | solution.py:339
  185.4 24.8 %collective-permute-start.9 = (bf16[48,6144]{1,0:T(8,128)(2,1)}, bf16[48,6144]{1,0:T(8,128)(2,1)S(1)}, u32[]{:S(2)}, u32[]{:S(2)}) collective-permute-start(bf16[48,6144]{1,0:T(8,128)(2,1)} %fusion.27.refs_4_.refs_2_), channel_id=1, source_target_pairs={{0,16},{4,20},{8,24},{12,28},{16,0},{20,4},{24,8},{28,12},{1,17},{... | collective-permute-start | bytes 1769480 | tf_op jit(solution)/shard_map/ppermute | solution.py:339
  210.2 18.3 %collective-permute-start.11 = (bf16[32,6144]{1,0:T(8,128)(2,1)}, bf16[32,6144]{1,0:T(8,128)(2,1)}, u32[]{:S(2)}, u32[]{:S(2)}) collective-permute-start(bf16[32,6144]{1,0:T(8,128)(2,1)} %fusion.38.refs_5_.refs_3_), channel_id=1, source_target_pairs={{0,16},{4,20},{8,24},{12,28},{16,0},{20,4},{24,8},{28,12},{1,17},{... | collective-permute-start | bytes 1179656 | tf_op jit(solution)/shard_map/ppermute | solution.py:339
  239.7 23.4 %collective-permute-start.22 = (bf16[32,6144]{1,0:T(8,128)(2,1)}, bf16[32,6144]{1,0:T(8,128)(2,1)S(1)}, u32[]{:S(2)}, u32[]{:S(2)}) collective-permute-start(bf16[32,6144]{1,0:T(8,128)(2,1)} %collective-permute-done.11.refs_3_.refs_5_), channel_id=1, source_target_pairs={{0,4},{4,0},{8,12},{12,8},{16,20},{20,16},{24,28},{28,24},{1,5},{5... | collective-permute-start | bytes 1179656 | tf_op jit(solution)/shard_map/ppermute | solution.py:339
  242.4 36.6 %collective-permute-start.23 = (bf16[128,768]{1,0:T(8,128)(2,1)S(1)}, bf16[128,768]{1,0:T(8,128)(2,1)S(1)}, u32[]{:S(2)}, u32[]{:S(2)}) collective-permute-start(bf16[128,768]{1,0:T(8,128)(2,1)S(1)} %get-tuple-element.85), channel_id=1, source_target_pairs={{0,2},{1,3},{2,0},{3,1},{4,6},{5,7},{6,4},{7,5},{8,10},{9,11},{10,... | collective-permute-start | bytes 589832 | tf_op jit(solution)/shard_map/ppermute | solution.py:342
  290.0 37.4 %collective-permute-start.32 = (bf16[36,128,128]{2,1,0:T(8,128)(2,1)S(1)}, bf16[36,128,128]{2,1,0:T(8,128)(2,1)}, u32[]{:S(2)}, u32[]{:S(2)}) collective-permute-start(bf16[36,128,128]{2,1,0:T(8,128)(2,1)S(1)} %copy-done.14), channel_id=1, source_target_pairs={{0,8},{4,12},{8,0},{12,4},{16,24},{20,28},{24,16},{28,20},{1,9},{5... | collective-permute-start | bytes 3538952 | tf_op jit(solution)/shard_map/ppermute | solution.py:339
  295.8 22.1 %collective-permute-start.27 = (bf16[256,768]{1,0:T(8,128)(2,1)S(1)}, bf16[256,768]{1,0:T(8,128)(2,1)}, u32[]{:S(2)}, u32[]{:S(2)}) collective-permute-start(bf16[256,768]{1,0:T(8,128)(2,1)S(1)} %copy-done.11), channel_id=1, source_target_pairs={{0,2},{1,3},{2,0},{3,1},{4,6},{5,7},{6,4},{7,5},{8,10},{9,11},{10,... | collective-permute-start | bytes 1179656 | tf_op jit(solution)/shard_map/ppermute | solution.py:342
  296.3 70.1 %collective-permute-start.25 = (bf16[36,128,128]{2,1,0:T(8,128)(2,1)S(1)}, bf16[36,128,128]{2,1,0:T(8,128)(2,1)}, u32[]{:S(2)}, u32[]{:S(2)}) collective-permute-start(bf16[36,128,128]{2,1,0:T(8,128)(2,1)S(1)} %copy-done.13), channel_id=1, source_target_pairs={{0,8},{4,12},{8,0},{12,4},{16,24},{20,28},{24,16},{28,20},{1,9},{5... | collective-permute-start | bytes 3538952 | tf_op jit(solution)/shard_map/ppermute | solution.py:339
  312.0 35.0 %collective-permute-start.33 = (bf16[128,768]{1,0:T(8,128)(2,1)}, bf16[128,768]{1,0:T(8,128)(2,1)}, u32[]{:S(2)}, u32[]{:S(2)}) collective-permute-start(bf16[128,768]{1,0:T(8,128)(2,1)} %add_convert_fusion.7), channel_id=1, source_target_pairs={{0,16},{4,20},{8,24},{12,28},{16,0},{20,4},{24,8},{28,12},{1,17},{... | collective-permute-start | bytes 589832 | tf_op jit(solution)/shard_map/ppermute | solution.py:339
  317.9 32.7 %collective-permute-start.35 = (bf16[128,768]{1,0:T(8,128)(2,1)}, bf16[128,768]{1,0:T(8,128)(2,1)}, u32[]{:S(2)}, u32[]{:S(2)}) collective-permute-start(bf16[128,768]{1,0:T(8,128)(2,1)} %add_convert_fusion.6), channel_id=1, source_target_pairs={{0,20},{4,16},{8,28},{12,24},{16,4},{20,0},{24,12},{28,8},{1,21},{... | collective-permute-start | bytes 589832 | tf_op jit(solution)/shard_map/ppermute | solution.py:339
  327.4 25.2 %collective-permute-start.30 = (bf16[256,768]{1,0:T(8,128)(2,1)S(1)}, bf16[256,768]{1,0:T(8,128)(2,1)S(1)}, u32[]{:S(2)}, u32[]{:S(2)}) collective-permute-start(bf16[256,768]{1,0:T(8,128)(2,1)S(1)} %add_convert_fusion.1.refs_0_), channel_id=1, source_target_pairs={{0,1},{1,0},{2,3},{3,2},{4,5},{5,4},{6,7},{7,6},{8,9},{9,8},{10,11... | collective-permute-start | bytes 1179656 | tf_op jit(solution)/shard_map/ppermute | solution.py:342
  327.4 34.0 %collective-permute-start.31 = (bf16[256,768]{1,0:T(8,128)(2,1)S(1)}, bf16[256,768]{1,0:T(8,128)(2,1)S(1)}, u32[]{:S(2)}, u32[]{:S(2)}) collective-permute-start(bf16[256,768]{1,0:T(8,128)(2,1)S(1)} %collective-permute-done.29.refs_1_), channel_id=1, source_target_pairs={{0,1},{1,0},{2,3},{3,2},{4,5},{5,4},{6,7},{7,6},{8,9},{9,8},{10,11... | collective-permute-start | bytes 1179656 | tf_op jit(solution)/shard_map/ppermute | solution.py:342
  352.6 17.6 %collective-permute-start.39 = (bf16[128,768]{1,0:T(8,128)(2,1)}, bf16[128,768]{1,0:T(8,128)(2,1)S(1)}, u32[]{:S(2)}, u32[]{:S(2)}) collective-permute-start(bf16[128,768]{1,0:T(8,128)(2,1)} %collective-permute-done.35.refs_2_), channel_id=1, source_target_pairs={{0,1},{1,0},{2,3},{3,2},{4,5},{5,4},{6,7},{7,6},{8,9},{9,8},{10,11... | collective-permute-start | bytes 589832 | tf_op jit(solution)/shard_map/ppermute | solution.py:342
  (44 other events, 486.9 us)

commit v4 on v2

--- a/solution.py
+++ b/solution.py
@@ -432,53 +432,51 @@
     far_acts = gathered(far_shares, own_sum)
     third = after(hid_far[2], own_sum)
     hid_both.append(swap(third, SIDE))
-    parts = acts_of([hid_own, hid_side], third)
+    fourth = after(hid_far[3], third)
+    hid_both.append(swap(fourth, SIDE))
+    parts = acts_of([hid_own, hid_side], fourth)
     near_cores = [core_sum(parts[0], parts[1]), core_sum(parts[2], parts[3])]
     near_got = [partner(value, 2) for value in near_cores]
-    fourth = after(hid_far[3], far_acts, *near_cores)
-    hid_both.append(swap(fourth, SIDE))
-    parts = acts_of([hid_far], fourth)
+    parts = acts_of([hid_far], far_acts, *near_cores)
     far_core = core_sum(parts[0], parts[1])
     far_got = partner(half_of(far_core, 1 - turn), 2)
 
     cuts = 2 if rows % 2 == 0 else 1
-    came, last = [], far_core
-    there = dict(hids=[hid_far, hid_both])
-    for k in range(cuts):
-        last = terms(
-            after(near_place, last),
-            acts=[(far_acts, "near"), (far_acts, "near_next")],
+    there = dict(
+        acts=[(far_acts, "near"), (far_acts, "near_next")], hids=[hid_far, hid_both]
+    )
+
+    def near_part(k, *others):
+        part = terms(
+            after(near_place, *others),
             acc=near_sum,
             first_row=k * (rows // cuts),
             count=rows // cuts,
             kind=jnp.bfloat16,
             **there,
         )
-        came.append(swap(last, NEAR))
-    far_sum = more_sum(add_up(after(half_of(far_core, turn), last), far_got))
-    far_back = swap(far_sum, FAR)
-    parts = acts_of([hid_both], far_sum)
+        return part, swap(part, NEAR)
+
+    last, got = near_part(0, far_core)
+    came = [got]
+    parts = acts_of([hid_both], last)
     both_core = core_sum(parts[0], parts[1])
     both_got = partner(half_of(both_core, 1 - turn), 2)
+    far_sum = more_sum(add_up(after(half_of(far_core, turn), both_core), far_got))
+    far_back = swap(far_sum, FAR)
+    for k in range(1, cuts):
+        last, got = near_part(k, far_sum)
+        came.append(got)
+    both_sum = more_sum(add_up(after(half_of(both_core, turn), last), both_got))
+    both_back = swap(both_sum, FAR | SIDE)
     own_sum = terms(
-        after(own_place, both_core),
-        acts=[(far_acts, "near"), (far_acts, "near_next")],
-        acc=own_sum,
-        first_row=0,
-        count=rows,
-        kind=jnp.float32,
-        **there,
-    )
-    both_sum = more_sum(add_up(after(half_of(both_core, turn), own_sum), both_got))
-    both_back = swap(both_sum, FAR | SIDE)
+        after(own_place, both_sum), acc=own_sum, first_row=0, count=rows, kind=jnp.float32, **there
+    )
     halves = [
-        more_sum(add_up(after(value, both_sum), got)) for value, got in zip(near_cores, near_got)
+        more_sum(add_up(after(value, own_sum), got)) for value, got in zip(near_cores, near_got)
     ]
     unit = (place & (FAR | SIDE)) + NEAR * core
     mine = [halves[0], swap(halves[1], SIDE)]
-    quarters = []
-    for value in (after(far_back, *halves), both_back):
-        quarters.append([value, partner(value, 2)])
 
     def put(bits_of, arrays, parts_of, whole):
         there_units = [unit ^ bits for bits in bits_of]
@@ -490,14 +488,21 @@
             activations.shape,
         )
 
+    weight_grad = add_part(own_sum, after(came[0], *halves), 0, per_row, None)
+    far_back = after(far_back, weight_grad)
+    far_pair = [far_back, partner(far_back, 2)]
+    both_back = after(both_back, far_back)
+    both_pair = [both_back, partner(both_back, 2)]
     zero = core * 0
-    act_grad = put([0, SIDE], mine, [zero, zero], None)
+    near_put = put([0, SIDE], mine, [zero, zero], None)
     act_grad = put(
-        [FAR, FAR, FAR | SIDE, FAR | SIDE], quarters[0] + quarters[1], [turn, 1 - turn] * 2, act_grad
-    )
-    weight_grad = None
-    for k, value in enumerate(came):
-        weight_grad = add_part(own_sum, value, k, per_row, weight_grad)
+        [FAR, FAR, FAR | SIDE, FAR | SIDE],
+        far_pair + both_pair,
+        [turn, 1 - turn] * 2,
+        near_put,
+    )
+    for k in range(1, cuts):
+        weight_grad = add_part(own_sum, after(came[k], near_put), k, per_row, weight_grad)
     return (weight_grad[None], act_grad)
 
 

time: 370 us -> 372 us (level)
    ppermute x20, waiting for transfers between devices: 24.2 us -> 34.2 us  [partner(): lax.ppermute(value, 'tensor', [(t, t ^ bit) for t in range(tensor_size)])]
    ppermute x21, waiting for transfers between devices: 172 us -> 166 us  [swap(): return lax.ppermute(value, 'dp', [(d, d ^ bits) for d in range(dp_size)])]
  transfers between devices with their start and end apart: 41 -> 41, of which waited for: 18 -> 20; matrix products, arithmetic and copies ran while one was open for 5% -> 6% of each run, Pallas kernels for 21% -> 19%
where the time goes in v4:
time: 372 us; the launch traced here: 369 us
  waiting for transfers between devices  200 us (54%)
  Pallas kernels  90.9 us (24%)
  starting transfers between devices  44.2 us (12%)
  other arithmetic  22.2 us (6%)
  local copies, waits for them, and re-layouts  11.1 us (3%)
    ppermute x21, waiting for transfers between devices, swap(): return lax.ppermute(value, 'dp', [(d, d ^ bits) for d in range(dp_size)])  166 us
    pallas_call x5, Pallas kernels, weight_terms(): pl.pallas_call(functools.partial(weight_term_kernel, per_row, rows, first...  43.4 us
    ppermute x20, waiting for transfers between devices, partner(): lax.ppermute(value, 'tensor', [(t, t ^ bit) for t in range(tensor_size)])  34.2 us
    pallas_call x3, Pallas kernels, act_partials(): pl.pallas_call(functools.partial(act_kernel, per_row, rows, len(hids), le...  33.6 us
    ppermute x21, starting transfers between devices, swap(): return lax.ppermute(value, 'dp', [(d, d ^ bits) for d in range(dp_size)])  31.5 us
    ppermute x20, starting transfers between devices, partner(): lax.ppermute(value, 'tensor', [(t, t ^ bit) for t in range(tensor_size)])  12.7 us
    convert_element_type x4, other arithmetic, hidden_gradient(): (grad_act.astype(jnp.float32) * gelu_slope(pre_act)).astype(jnp.bfloat16)  11.3 us
    pallas_call x2, Pallas kernels, add_part(): pl.pallas_call(add_kernel, out_shape=jax.ShapeDtypeStruct(total.shape, jn...  7.44 us
  transfers between devices with their start and end apart: 41, of which 20 were waited for; matrix products, arithmetic and copies ran while one was open for 6% of the time, Pallas kernels for 19%

profile of v4, /device:TPU:0, one launch (start us, length us, event | category | flops | bytes accessed | tf_op | source)
XLA Modules:
  0.0 369.4 jit_solution(7385532848809543992)
XLA Ops:
  6.3 4.1 %collective-permute-start.1 = (bf16[80,6144]{1,0:T(8,128)(2,1)S(1)}, bf16[80,6144]{1,0:T(8,128)(2,1)S(1)}, u32[]{:S(2)}, u32[]{:S(2)}) collective-permute-start(bf16[80,6144]{1,0:T(8,128)(2,1)S(1)} %fusion.11.refs_3_.refs_1_), channel_id=1, source_target_pairs={{0,16},{4,20},{8,24},{12,28},{16,0},{20,4},{24,8},{28,12},{1,17},{... | collective-permute-start | bytes 2949128 | tf_op jit(solution)/shard_map/ppermute | solution.py:339
  24.6 14.6 %collective-permute-done.2 = bf16[64,1536]{1,0:T(8,128)(2,1)S(1)} collective-permute-done((bf16[64,1536]{1,0:T(8,128)(2,1)}, bf16[64,1536]{1,0:T(8,128)(2,1)S(1)}, u32[]{:S(2)}, u32[]{:S(2)}) %collective-permute-start.2) | collective-permute-done | bytes 196640 | tf_op jit(solution)/shard_map/ppermute | solution.py:339
  41.5 3.5 collective-permute-done.3
  48.3 4.9 %collective-permute-done.1.refs_1_.refs_3_ = bf16[80,6144]{1,0:T(8,128)(2,1)S(1)} collective-permute-done((bf16[80,6144]{1,0:T(8,128)(2,1)S(1)}, bf16[80,6144]{1,0:T(8,128)(2,1)S(1)}, u32[]{:S(2)}, u32[]{:S(2)}) %collective-permute-start.1) | collective-permute-done | bytes 983072 | tf_op jit(solution)/shard_map/ppermute | solution.py:339
  53.3 19.8 %collective-permute-done.8.refs_9_.refs_7_ = bf16[48,6144]{1,0:T(8,128)(2,1)} collective-permute-done((bf16[48,6144]{1,0:T(8,128)(2,1)}, bf16[48,6144]{1,0:T(8,128)(2,1)}, u32[]{:S(2)}, u32[]{:S(2)}) %collective-permute-start.8) | collective-permute-done | bytes 589856 | tf_op jit(solution)/shard_map/ppermute | solution.py:339
  74.7 9.5 %collective-permute-done.5.refs_6_.refs_4_ = bf16[48,6144]{1,0:T(8,128)(2,1)S(1)} collective-permute-done((bf16[48,6144]{1,0:T(8,128)(2,1)}, bf16[48,6144]{1,0:T(8,128)(2,1)S(1)}, u32[]{:S(2)}, u32[]{:S(2)}) %collective-permute-start.5) | collective-permute-done | bytes 589856 | tf_op jit(solution)/shard_map/ppermute | solution.py:339
  88.1 9.3 %weight_terms.5.refs_10_ = f32[72,128,128]{2,1,0:T(8,128)} custom-call(s32[2]{0:T(128)} %pad_add_fusion.2.place_ref, s32[576]{0:T(1024)} %reduce.cols_ref, bf16[256,6144]{1,0:T(8,128)(2,1)} %refs_0_.3, bf16[256,1536]{1,0:T(8,128)(2,1)} %copy-done.10, bf16[48,6144]{1,0:T(8,128)(2,1)} %fusion.33.refs_2_.refs_0_, bf16[80,6144]{1,0:T(8,128)(2,1)} %copy-done.2, ...), custom_call_target="tpu_custom_call" | custom-call | flops 1207959552 | bytes 15728640 | tf_op jit(solution)/shard_map/weight_terms/pallas_call | solution.py:151
  97.3 9.3 %weight_terms.6.refs_10_ = f32[72,128,128]{2,1,0:T(8,128)} custom-call(s32[2]{0:T(128)} %pad_add_fusion.place_ref, s32[576]{0:T(1024)} %reduce.cols_ref, bf16[256,6144]{1,0:T(8,128)(2,1)} %refs_0_.3, bf16[256,1536]{1,0:T(8,128)(2,1)} %copy-done.10, bf16[48,6144]{1,0:T(8,128)(2,1)} %fusion.33.refs_2_.refs_0_, bf16[80,6144]{1,0:T(8,128)(2,1)} %copy-done.2, ...), custom_call_target="tpu_custom_call" | custom-call | flops 1207959552 | bytes 15728640 | tf_op jit(solution)/shard_map/weight_terms/pallas_call | solution.py:151
  106.6 22.7 %collective-permute-done.9 = bf16[64,1536]{1,0:T(8,128)(2,1)} collective-permute-done((bf16[64,1536]{1,0:T(8,128)(2,1)}, bf16[64,1536]{1,0:T(8,128)(2,1)}, u32[]{:S(2)}, u32[]{:S(2)}) %collective-permute-start.9) | collective-permute-done | bytes 196640 | tf_op jit(solution)/shard_map/ppermute | solution.py:339
  147.1 42.3 %collective-permute-done.14.refs_2_.refs_4_ = bf16[80,6144]{1,0:T(8,128)(2,1)} collective-permute-done((bf16[80,6144]{1,0:T(8,128)(2,1)S(1)}, bf16[80,6144]{1,0:T(8,128)(2,1)}, u32[]{:S(2)}, u32[]{:S(2)}) %collective-permute-start.14) | collective-permute-done | bytes 983072 | tf_op jit(solution)/shard_map/ppermute | solution.py:339
  190.9 10.9 %collective-permute-done.12.refs_3_.refs_5_ = bf16[48,6144]{1,0:T(8,128)(2,1)S(1)} collective-permute-done((bf16[48,6144]{1,0:T(8,128)(2,1)}, bf16[48,6144]{1,0:T(8,128)(2,1)S(1)}, u32[]{:S(2)}, u32[]{:S(2)}) %collective-permute-start.12) | collective-permute-done | bytes 589856 | tf_op jit(solution)/shard_map/ppermute | solution.py:339
  202.9 13.7 %act_partials.3 = (bf16[256,768]{1,0:T(8,128)(2,1)}, bf16[256,768]{1,0:T(8,128)(2,1)}, bf16[256,768]{1,0:T(8,128)(2,1)}, bf16[256,768]{1,0:T(8,128)(2,1)}) custom-call(s32[3]{0:T(128)} %pad_add_fusion.1.place_ref, s32[576]{0:T(1024)} %reduce.cols_ref, bf16[48,6144]{1,0:T(8,128)(2,1)} %fusion.33.refs_2_.refs_0_, bf16[80,6144]{1,0:T(8,128)(2,1)} %copy-done.2, ...), custom_call_target="tpu_custom_call" | custom-call | flops 2415919104 | bytes 11010048 | tf_op jit(solution)/shard_map/act_partials/pallas_call | solution.py:227
  221.7 9.9 %act_partials.4 = (bf16[256,768]{1,0:T(8,128)(2,1)}, bf16[256,768]{1,0:T(8,128)(2,1)}) custom-call(s32[3]{0:T(128)} %pad_add_fusion.1.place_ref, s32[576]{0:T(1024)} %reduce.cols_ref, bf16[48,6144]{1,0:T(8,128)(2,1)} %copy-done.6, bf16[80,6144]{1,0:T(8,128)(2,1)} %copy-done.1, bf16[80,6144]{1,0:T(8,128)(2,1)} %collective-permute-done.14.refs_2_.refs_4_, ...), custom_call_target="tpu_custom_call" | custom-call | flops 1207959552 | bytes 7864320 | tf_op jit(solution)/shard_map/act_partials/pallas_call | solution.py:227
  236.0 13.3 %collective-permute-done.19.refs_6_.refs_0_ = bf16[48,6144]{1,0:T(8,128)(2,1)S(1)} collective-permute-done((bf16[48,6144]{1,0:T(8,128)(2,1)}, bf16[48,6144]{1,0:T(8,128)(2,1)S(1)}, u32[]{:S(2)}, u32[]{:S(2)}) %collective-permute-start.19) | collective-permute-done | bytes 589856 | tf_op jit(solution)/shard_map/ppermute | solution.py:339
  249.3 11.7 %collective-permute-done.22.refs_9_.refs_3_ = bf16[48,6144]{1,0:T(8,128)(2,1)S(1)} collective-permute-done((bf16[48,6144]{1,0:T(8,128)(2,1)}, bf16[48,6144]{1,0:T(8,128)(2,1)S(1)}, u32[]{:S(2)}, u32[]{:S(2)}) %collective-permute-start.22) | collective-permute-done | bytes 589856 | tf_op jit(solution)/shard_map/ppermute | solution.py:339
  262.8 7.5 %weight_terms.7 = bf16[36,128,128]{2,1,0:T(8,128)(2,1)} custom-call(s32[2]{0:T(128)} %pad_add_fusion.2.place_ref, s32[576]{0:T(1024)} %reduce.cols_ref, bf16[256,3072]{1,0:T(8,128)(2,1)} %copy-done, bf16[256,3072]{1,0:T(8,128)(2,1)} %copy-done, bf16[48,6144]{1,0:T(8,128)(2,1)} %copy-done.6, bf16[80,6144]{1,0:T(8,128)(2,1)} %copy-done.1, ...), custom_call_target="tpu_custom_call" | custom-call | flops 603979776 | bytes 11010048 | tf_op jit(solution)/shard_map/weight_terms/pallas_call | solution.py:151
  270.3 10.0 %act_partials.5 = (bf16[256,768]{1,0:T(8,128)(2,1)}, bf16[256,768]{1,0:T(8,128)(2,1)}) custom-call(s32[3]{0:T(128)} %pad_add_fusion.1.place_ref, s32[576]{0:T(1024)} %reduce.cols_ref, bf16[48,6144]{1,0:T(8,128)(2,1)} %copy-done.8, bf16[80,6144]{1,0:T(8,128)(2,1)} %collective-permute-done.20.refs_7_.refs_1_, bf16[80,6144]{1,0:T(8,128)(2,1)} %copy-done.5, ...), custom_call_target="tpu_custom_call" | custom-call | flops 1207959552 | bytes 7864320 | tf_op jit(solution)/shard_map/act_partials/pallas_call | solution.py:227
  286.8 18.4 %collective-permute-done.24 = bf16[128,768]{1,0:T(8,128)(2,1)S(1)} collective-permute-done((bf16[128,768]{1,0:T(8,128)(2,1)S(1)}, bf16[128,768]{1,0:T(8,128)(2,1)S(1)}, u32[]{:S(2)}, u32[]{:S(2)}) %collective-permute-start.24) | collective-permute-done | bytes 196640 | tf_op jit(solution)/shard_map/ppermute | solution.py:342
  305.2 7.5 %weight_terms.8 = bf16[36,128,128]{2,1,0:T(8,128)(2,1)} custom-call(s32[2]{0:T(128)} %pad_add_fusion.2.place_ref, s32[576]{0:T(1024)} %reduce.cols_ref, bf16[256,3072]{1,0:T(8,128)(2,1)} %copy-done, bf16[256,3072]{1,0:T(8,128)(2,1)} %copy-done, bf16[48,6144]{1,0:T(8,128)(2,1)} %copy-done.6, bf16[80,6144]{1,0:T(8,128)(2,1)} %copy-done.1, ...), custom_call_target="tpu_custom_call" | custom-call | flops 603979776 | bytes 11010048 | tf_op jit(solution)/shard_map/weight_terms/pallas_call | solution.py:151
  312.8 9.8 %weight_terms.9.sum_ref = f32[72,128,128]{2,1,0:T(8,128)} custom-call(s32[2]{0:T(128)} %pad_add_fusion.place_ref, s32[576]{0:T(1024)} %reduce.cols_ref, bf16[256,3072]{1,0:T(8,128)(2,1)} %copy-done, bf16[256,3072]{1,0:T(8,128)(2,1)} %copy-done, bf16[48,6144]{1,0:T(8,128)(2,1)} %copy-done.6, bf16[80,6144]{1,0:T(8,128)(2,1)} %copy-done.1, ...), custom_call_target="tpu_custom_call" | custom-call | flops 1207959552 | bytes 15728640 | tf_op jit(solution)/shard_map/weight_terms/pallas_call | solution.py:151
  328.3 9.8 %collective-permute-done.29.refs_1_ = bf16[256,768]{1,0:T(8,128)(2,1)S(1)} collective-permute-done((bf16[256,768]{1,0:T(8,128)(2,1)S(1)}, bf16[256,768]{1,0:T(8,128)(2,1)S(1)}, u32[]{:S(2)}, u32[]{:S(2)}) %collective-permute-start.29) | collective-permute-done | bytes 393248 | tf_op jit(solution)/shard_map/ppermute | solution.py:339
  338.6 3.7 %add_part.2.refs_0_ = bf16[72,128,128]{2,1,0:T(8,128)(2,1)} custom-call(f32[72,128,128]{2,1,0:T(8,128)} %weight_terms.9.sum_ref, bf16[36,128,128]{2,1,0:T(8,128)(2,1)} %collective-permute-done.32.part_ref), custom_call_target="tpu_custom_call" | custom-call | flops 589824 | bytes 4718592 | tf_op jit(solution)/shard_map/add_part/pallas_call | solution.py:296
  348.1 5.4 %collective-permute-done.36.refs_3_ = bf16[128,768]{1,0:T(8,128)(2,1)S(1)} collective-permute-done((bf16[128,768]{1,0:T(8,128)(2,1)S(1)}, bf16[128,768]{1,0:T(8,128)(2,1)S(1)}, u32[]{:S(2)}, u32[]{:S(2)}) %collective-permute-start.36) | collective-permute-done | bytes 196640 | tf_op jit(solution)/shard_map/ppermute | solution.py:342
  360.6 3.7 %add_part.3 = bf16[72,128,128]{2,1,0:T(8,128)(2,1)} custom-call(f32[72,128,128]{2,1,0:T(8,128)} %weight_terms.9.sum_ref, bf16[36,128,128]{2,1,0:T(8,128)(2,1)} %collective-permute-done.26.part_ref, bf16[72,128,128]{2,1,0:T(8,128)(2,1)} %add_part.2.refs_0_), custom_call_target="tpu_custom_call", output_to_operand_aliasing={{}: (2, {})} | custom-call | flops 589824 | bytes 4718592 | tf_op jit(solution)/shard_map/add_part/pallas_call | solution.py:296
  (177 shorter events, 92.7 us)
Async XLA Ops:
  6.3 47.0 %collective-permute-start.1 = (bf16[80,6144]{1,0:T(8,128)(2,1)S(1)}, bf16[80,6144]{1,0:T(8,128)(2,1)S(1)}, u32[]{:S(2)}, u32[]{:S(2)}) collective-permute-start(bf16[80,6144]{1,0:T(8,128)(2,1)S(1)} %fusion.11.refs_3_.refs_1_), channel_id=1, source_target_pairs={{0,16},{4,20},{8,24},{12,28},{16,0},{20,4},{24,8},{28,12},{1,17},{... | collective-permute-start | bytes 2949128 | tf_op jit(solution)/shard_map/ppermute | solution.py:339
  10.4 77.6 %collective-permute-start.6 = (bf16[80,6144]{1,0:T(8,128)(2,1)S(1)}, bf16[80,6144]{1,0:T(8,128)(2,1)}, u32[]{:S(2)}, u32[]{:S(2)}) collective-permute-start(bf16[80,6144]{1,0:T(8,128)(2,1)S(1)} %fusion.11.refs_3_.refs_1_), channel_id=1, source_target_pairs={{0,4},{4,0},{8,12},{12,8},{16,20},{20,16},{24,28},{28,24},{1,5},{5... | collective-permute-start | bytes 2949128 | tf_op jit(solution)/shard_map/ppermute | solution.py:339
  13.8 25.5 %collective-permute-start.2 = (bf16[64,1536]{1,0:T(8,128)(2,1)}, bf16[64,1536]{1,0:T(8,128)(2,1)S(1)}, u32[]{:S(2)}, u32[]{:S(2)}) collective-permute-start(bf16[64,1536]{1,0:T(8,128)(2,1)} %pad_maximum_fusion.3), channel_id=1, source_target_pairs={{0,4},{4,0},{8,12},{12,8},{16,20},{20,16},{24,28},{28,24},{1,5},{5... | collective-permute-start | bytes 589832 | tf_op jit(solution)/shard_map/ppermute | solution.py:339
  17.1 68.4 %collective-permute-start.7 = (bf16[80,6144]{1,0:T(8,128)(2,1)S(1)}, bf16[80,6144]{1,0:T(8,128)(2,1)}, u32[]{:S(2)}, u32[]{:S(2)}) collective-permute-start(bf16[80,6144]{1,0:T(8,128)(2,1)S(1)} %fusion.6.refs_4_.refs_2_), channel_id=1, source_target_pairs={{0,4},{4,0},{8,12},{12,8},{16,20},{20,16},{24,28},{28,24},{1,5},{5... | collective-permute-start | bytes 2949128 | tf_op jit(solution)/shard_map/ppermute | solution.py:339
  21.6 51.5 %collective-permute-start.8 = (bf16[48,6144]{1,0:T(8,128)(2,1)}, bf16[48,6144]{1,0:T(8,128)(2,1)}, u32[]{:S(2)}, u32[]{:S(2)}) collective-permute-start(bf16[48,6144]{1,0:T(8,128)(2,1)} %fusion.28.refs_5_.refs_3_), channel_id=1, source_target_pairs={{0,4},{4,0},{8,12},{12,8},{16,20},{20,16},{24,28},{28,24},{1,5},{5... | collective-permute-start | bytes 1769480 | tf_op jit(solution)/shard_map/ppermute | solution.py:339
  46.8 37.4 %collective-permute-start.5 = (bf16[48,6144]{1,0:T(8,128)(2,1)}, bf16[48,6144]{1,0:T(8,128)(2,1)S(1)}, u32[]{:S(2)}, u32[]{:S(2)}) collective-permute-start(bf16[48,6144]{1,0:T(8,128)(2,1)} %fusion.33.refs_2_.refs_0_), channel_id=1, source_target_pairs={{0,4},{4,0},{8,12},{12,8},{16,20},{20,16},{24,28},{28,24},{1,5},{5... | collective-permute-start | bytes 1769480 | tf_op jit(solution)/shard_map/ppermute | solution.py:339
  53.3 80.7 %collective-permute-start.13 = (bf16[48,6144]{1,0:T(8,128)(2,1)}, bf16[48,6144]{1,0:T(8,128)(2,1)S(1)}, u32[]{:S(2)}, u32[]{:S(2)}) collective-permute-start(bf16[48,6144]{1,0:T(8,128)(2,1)} %fusion.33.refs_2_.refs_0_), channel_id=1, source_target_pairs={{0,16},{4,20},{8,24},{12,28},{16,0},{20,4},{24,8},{28,12},{1,17},{... | collective-permute-start | bytes 1769480 | tf_op jit(solution)/shard_map/ppermute | solution.py:339
  73.1 129.8 %collective-permute-start.15 = (bf16[72,128,128]{2,1,0:T(8,128)(2,1)}, bf16[72,128,128]{2,1,0:T(8,128)(2,1)}, u32[]{:S(2)}, u32[]{:S(2)}) collective-permute-start(bf16[72,128,128]{2,1,0:T(8,128)(2,1)} %bitcast.6.refs_8_.refs_4_), channel_id=1, source_target_pairs={{0,8},{4,12},{8,0},{12,4},{16,24},{20,28},{24,16},{28,20},{1,9},{5... | collective-permute-start | bytes 7077896 | tf_op jit(solution)/shard_map/ppermute | solution.py:339
  84.2 45.0 %collective-permute-start.9 = (bf16[64,1536]{1,0:T(8,128)(2,1)}, bf16[64,1536]{1,0:T(8,128)(2,1)}, u32[]{:S(2)}, u32[]{:S(2)}) collective-permute-start(bf16[64,1536]{1,0:T(8,128)(2,1)} %pad_maximum_fusion.4), channel_id=1, source_target_pairs={{0,20},{4,16},{8,28},{12,24},{16,4},{20,0},{24,12},{28,8},{1,21},{... | collective-permute-start | bytes 589832 | tf_op jit(solution)/shard_map/ppermute | solution.py:339
  85.5 45.9 %collective-permute-start = (bf16[64,1536]{1,0:T(8,128)(2,1)}, bf16[64,1536]{1,0:T(8,128)(2,1)S(1)}, u32[]{:S(2)}, u32[]{:S(2)}) collective-permute-start(bf16[64,1536]{1,0:T(8,128)(2,1)} %pad_maximum_fusion.2), channel_id=1, source_target_pairs={{0,16},{4,20},{8,24},{12,28},{16,0},{20,4},{24,8},{28,12},{1,17},{... | collective-permute-start | bytes 589832 | tf_op jit(solution)/shard_map/ppermute | solution.py:339
  133.9 55.4 %collective-permute-start.14 = (bf16[80,6144]{1,0:T(8,128)(2,1)S(1)}, bf16[80,6144]{1,0:T(8,128)(2,1)}, u32[]{:S(2)}, u32[]{:S(2)}) collective-permute-start(bf16[80,6144]{1,0:T(8,128)(2,1)S(1)} %copy-done.4), channel_id=1, source_target_pairs={{0,16},{4,20},{8,24},{12,28},{16,0},{20,4},{24,8},{28,12},{1,17},{... | collective-permute-start | bytes 2949128 | tf_op jit(solution)/shard_map/ppermute | solution.py:339
  140.2 61.6 %collective-permute-start.11 = (bf16[128,3072]{1,0:T(8,128)(2,1)S(1)}, bf16[128,3072]{1,0:T(8,128)(2,1)S(1)}, u32[]{:S(2)}, u32[]{:S(2)}) collective-permute-start(bf16[128,3072]{1,0:T(8,128)(2,1)S(1)} %pad_maximum_fusion), channel_id=1, source_target_pairs={{0,1},{1,0},{2,3},{3,2},{4,5},{5,4},{6,7},{7,6},{8,9},{9,8},{10,11... | collective-permute-start | bytes 2359304 | tf_op jit(solution)/shard_map/ppermute | solution.py:342
  140.9 60.9 %collective-permute-start.12 = (bf16[48,6144]{1,0:T(8,128)(2,1)}, bf16[48,6144]{1,0:T(8,128)(2,1)S(1)}, u32[]{:S(2)}, u32[]{:S(2)}) collective-permute-start(bf16[48,6144]{1,0:T(8,128)(2,1)} %fusion.28.refs_5_.refs_3_), channel_id=1, source_target_pairs={{0,16},{4,20},{8,24},{12,28},{16,0},{20,4},{24,8},{28,12},{1,17},{... | collective-permute-start | bytes 1769480 | tf_op jit(solution)/shard_map/ppermute | solution.py:339
  144.3 105.0 %collective-permute-start.20 = (bf16[80,6144]{1,0:T(8,128)(2,1)S(1)}, bf16[80,6144]{1,0:T(8,128)(2,1)}, u32[]{:S(2)}, u32[]{:S(2)}) collective-permute-start(bf16[80,6144]{1,0:T(8,128)(2,1)S(1)} %collective-permute-done.1.refs_1_.refs_3_), channel_id=1, source_target_pairs={{0,4},{4,0},{8,12},{12,8},{16,20},{20,16},{24,28},{28,24},{1,5},{5... | collective-permute-start | bytes 2949128 | tf_op jit(solution)/shard_map/ppermute | solution.py:339
  189.4 71.7 %collective-permute-start.21 = (bf16[80,6144]{1,0:T(8,128)(2,1)}, bf16[80,6144]{1,0:T(8,128)(2,1)S(1)}, u32[]{:S(2)}, u32[]{:S(2)}) collective-permute-start(bf16[80,6144]{1,0:T(8,128)(2,1)} %collective-permute-done.14.refs_2_.refs_4_), channel_id=1, source_target_pairs={{0,4},{4,0},{8,12},{12,8},{16,20},{20,16},{24,28},{28,24},{1,5},{5... | collective-permute-start | bytes 2949128 | tf_op jit(solution)/shard_map/ppermute | solution.py:339
  234.4 26.7 %collective-permute-start.22 = (bf16[48,6144]{1,0:T(8,128)(2,1)}, bf16[48,6144]{1,0:T(8,128)(2,1)S(1)}, u32[]{:S(2)}, u32[]{:S(2)}) collective-permute-start(bf16[48,6144]{1,0:T(8,128)(2,1)} %copy-done.7), channel_id=1, source_target_pairs={{0,4},{4,0},{8,12},{12,8},{16,20},{20,16},{24,28},{28,24},{1,5},{5... | collective-permute-start | bytes 1769480 | tf_op jit(solution)/shard_map/ppermute | solution.py:339
  280.5 42.2 %collective-permute-start.28 = (bf16[256,768]{1,0:T(8,128)(2,1)S(1)}, bf16[256,768]{1,0:T(8,128)(2,1)}, u32[]{:S(2)}, u32[]{:S(2)}) collective-permute-start(bf16[256,768]{1,0:T(8,128)(2,1)S(1)} %copy-done.15), channel_id=1, source_target_pairs={{0,2},{1,3},{2,0},{3,1},{4,6},{5,7},{6,4},{7,5},{8,10},{9,11},{10,... | collective-permute-start | bytes 1179656 | tf_op jit(solution)/shard_map/ppermute | solution.py:342
  280.9 47.3 %collective-permute-start.27 = (bf16[256,768]{1,0:T(8,128)(2,1)S(1)}, bf16[256,768]{1,0:T(8,128)(2,1)S(1)}, u32[]{:S(2)}, u32[]{:S(2)}) collective-permute-start(bf16[256,768]{1,0:T(8,128)(2,1)S(1)} %copy-done.14), channel_id=1, source_target_pairs={{0,2},{1,3},{2,0},{3,1},{4,6},{5,7},{6,4},{7,5},{8,10},{9,11},{10,... | collective-permute-start | bytes 1179656 | tf_op jit(solution)/shard_map/ppermute | solution.py:342
  282.6 55.5 %collective-permute-start.32 = (bf16[36,128,128]{2,1,0:T(8,128)(2,1)S(1)}, bf16[36,128,128]{2,1,0:T(8,128)(2,1)}, u32[]{:S(2)}, u32[]{:S(2)}) collective-permute-start(bf16[36,128,128]{2,1,0:T(8,128)(2,1)S(1)} %copy-done.18), channel_id=1, source_target_pairs={{0,8},{4,12},{8,0},{12,4},{16,24},{20,28},{24,16},{28,20},{1,9},{5... | collective-permute-start | bytes 3538952 | tf_op jit(solution)/shard_map/ppermute | solution.py:339
  282.6 22.6 %collective-permute-start.24 = (bf16[128,768]{1,0:T(8,128)(2,1)S(1)}, bf16[128,768]{1,0:T(8,128)(2,1)S(1)}, u32[]{:S(2)}, u32[]{:S(2)}) collective-permute-start(bf16[128,768]{1,0:T(8,128)(2,1)S(1)} %get-tuple-element.79), channel_id=1, source_target_pairs={{0,2},{1,3},{2,0},{3,1},{4,6},{5,7},{6,4},{7,5},{8,10},{9,11},{10,... | collective-permute-start | bytes 589832 | tf_op jit(solution)/shard_map/ppermute | solution.py:342
  285.8 26.9 %collective-permute-start.25 = (bf16[128,768]{1,0:T(8,128)(2,1)S(1)}, bf16[128,768]{1,0:T(8,128)(2,1)S(1)}, u32[]{:S(2)}, u32[]{:S(2)}) collective-permute-start(bf16[128,768]{1,0:T(8,128)(2,1)S(1)} %get-tuple-element.81), channel_id=1, source_target_pairs={{0,2},{1,3},{2,0},{3,1},{4,6},{5,7},{6,4},{7,5},{8,10},{9,11},{10,... | collective-permute-start | bytes 589832 | tf_op jit(solution)/shard_map/ppermute | solution.py:342
  312.7 47.9 %collective-permute-start.26 = (bf16[36,128,128]{2,1,0:T(8,128)(2,1)}, bf16[36,128,128]{2,1,0:T(8,128)(2,1)}, u32[]{:S(2)}, u32[]{:S(2)}) collective-permute-start(bf16[36,128,128]{2,1,0:T(8,128)(2,1)} %weight_terms.8), channel_id=1, source_target_pairs={{0,8},{4,12},{8,0},{12,4},{16,24},{20,28},{24,16},{28,20},{1,9},{5... | collective-permute-start | bytes 3538952 | tf_op jit(solution)/shard_map/ppermute | solution.py:339
  325.3 18.2 %collective-permute-start.33 = (bf16[128,768]{1,0:T(8,128)(2,1)S(1)}, bf16[128,768]{1,0:T(8,128)(2,1)S(1)}, u32[]{:S(2)}, u32[]{:S(2)}) collective-permute-start(bf16[128,768]{1,0:T(8,128)(2,1)S(1)} %add_convert_fusion.7), channel_id=1, source_target_pairs={{0,16},{4,20},{8,24},{12,28},{16,0},{20,4},{24,8},{28,12},{1,17},{... | collective-permute-start | bytes 589832 | tf_op jit(solution)/shard_map/ppermute | solution.py:339
  328.1 17.9 %collective-permute-start.35 = (bf16[128,768]{1,0:T(8,128)(2,1)S(1)}, bf16[128,768]{1,0:T(8,128)(2,1)S(1)}, u32[]{:S(2)}, u32[]{:S(2)}) collective-permute-start(bf16[128,768]{1,0:T(8,128)(2,1)S(1)} %add_convert_fusion.6), channel_id=1, source_target_pairs={{0,20},{4,16},{8,28},{12,24},{16,4},{20,0},{24,12},{28,8},{1,21},{... | collective-permute-start | bytes 589832 | tf_op jit(solution)/shard_map/ppermute | solution.py:339
  (51 other events, 548.3 us)

commit v5 on v2

--- a/solution.py
+++ b/solution.py
@@ -476,9 +476,6 @@
     ]
     unit = (place & (FAR | SIDE)) + NEAR * core
     mine = [halves[0], swap(halves[1], SIDE)]
-    quarters = []
-    for value in (after(far_back, *halves), both_back):
-        quarters.append([value, partner(value, 2)])
 
     def put(bits_of, arrays, parts_of, whole):
         there_units = [unit ^ bits for bits in bits_of]
@@ -490,14 +487,21 @@
             activations.shape,
         )
 
+    weight_grad = add_part(own_sum, after(came[0], *halves), 0, per_row, None)
     zero = core * 0
-    act_grad = put([0, SIDE], mine, [zero, zero], None)
+    near_put = put([0, SIDE], mine, [zero, zero], None)
+    far_back = after(far_back, weight_grad, near_put)
+    far_got = partner(far_back, 2)
+    both_back = after(both_back, far_back)
+    both_got = partner(both_back, 2)
+    for k in range(1, cuts):
+        weight_grad = add_part(own_sum, after(came[k], both_back), k, per_row, weight_grad)
     act_grad = put(
-        [FAR, FAR, FAR | SIDE, FAR | SIDE], quarters[0] + quarters[1], [turn, 1 - turn] * 2, act_grad
-    )
-    weight_grad = None
-    for k, value in enumerate(came):
-        weight_grad = add_part(own_sum, value, k, per_row, weight_grad)
+        [FAR, FAR, FAR | SIDE, FAR | SIDE],
+        [far_back, after(far_got, weight_grad), both_back, after(both_got, weight_grad)],
+        [turn, 1 - turn] * 2,
+        near_put,
+    )
     return (weight_grad[None], act_grad)
 
 

time: 370 us -> 362 us (0.978)
  waiting for transfers between devices: 197 us -> 183 us
    ppermute x21, waiting for transfers between devices: 172 us -> 163 us  [swap(): return lax.ppermute(value, 'dp', [(d, d ^ bits) for d in range(dp_size)])]
    ppermute x20, waiting for transfers between devices: 24.2 us -> 20 us  [partner(): lax.ppermute(value, 'tensor', [(t, t ^ bit) for t in range(tensor_size)])]
  transfers between devices with their start and end apart: 41 -> 41, of which waited for: 18 -> 23; matrix products, arithmetic and copies ran while one was open for 5% -> 7% of each run, Pallas kernels for 21% -> 22%
where the time goes in v5:
time: 362 us; the launch traced here: 359 us
  waiting for transfers between devices  183 us (51%)
  Pallas kernels  91.1 us (25%)
  starting transfers between devices  47.6 us (13%)
  other arithmetic  25.8 us (7%)
  local copies, waits for them, and re-layouts  9.95 us (3%)
    ppermute x21, waiting for transfers between devices, swap(): return lax.ppermute(value, 'dp', [(d, d ^ bits) for d in range(dp_size)])  163 us
    pallas_call x5, Pallas kernels, weight_terms(): pl.pallas_call(functools.partial(weight_term_kernel, per_row, rows, first...  43.5 us
    ppermute x21, starting transfers between devices, swap(): return lax.ppermute(value, 'dp', [(d, d ^ bits) for d in range(dp_size)])  37 us
    pallas_call x3, Pallas kernels, act_partials(): pl.pallas_call(functools.partial(act_kernel, per_row, rows, len(hids), le...  33.7 us
    ppermute x20, waiting for transfers between devices, partner(): lax.ppermute(value, 'tensor', [(t, t ^ bit) for t in range(tensor_size)])  20 us
    convert_element_type x4, other arithmetic, hidden_gradient(): (grad_act.astype(jnp.float32) * gelu_slope(pre_act)).astype(jnp.bfloat16)  11.3 us
    ppermute x20, starting transfers between devices, partner(): lax.ppermute(value, 'tensor', [(t, t ^ bit) for t in range(tensor_size)])  10.6 us
    convert_element_type x8, other arithmetic, add_up(): (left.astype(jnp.float32) + right.astype(jnp.float32)).astype(jnp.bfloat16)  9.81 us
  transfers between devices with their start and end apart: 41, of which 23 were waited for; matrix products, arithmetic and copies ran while one was open for 7% of the time, Pallas kernels for 22%

profile of v5, /device:TPU:0, one launch (start us, length us, event | category | flops | bytes accessed | tf_op | source)
XLA Modules:
  0.0 358.6 jit_solution(10140735717884260622)
XLA Ops:
  6.3 4.1 %collective-permute-start = (bf16[80,6144]{1,0:T(8,128)(2,1)S(1)}, bf16[80,6144]{1,0:T(8,128)(2,1)S(1)}, u32[]{:S(2)}, u32[]{:S(2)}) collective-permute-start(bf16[80,6144]{1,0:T(8,128)(2,1)S(1)} %fusion.11.refs_3_.refs_1_), channel_id=1, source_target_pairs={{0,16},{4,20},{8,24},{12,28},{16,0},{20,4},{24,8},{28,12},{1,17},{... | collective-permute-start | bytes 2949128 | tf_op jit(solution)/shard_map/ppermute | solution.py:339
  24.6 14.6 %collective-permute-done.3 = bf16[64,1536]{1,0:T(8,128)(2,1)S(1)} collective-permute-done((bf16[64,1536]{1,0:T(8,128)(2,1)}, bf16[64,1536]{1,0:T(8,128)(2,1)S(1)}, u32[]{:S(2)}, u32[]{:S(2)}) %collective-permute-start.3) | collective-permute-done | bytes 196640 | tf_op jit(solution)/shard_map/ppermute | solution.py:339
  48.3 4.9 %collective-permute-done.refs_1_.refs_3_ = bf16[80,6144]{1,0:T(8,128)(2,1)S(1)} collective-permute-done((bf16[80,6144]{1,0:T(8,128)(2,1)S(1)}, bf16[80,6144]{1,0:T(8,128)(2,1)S(1)}, u32[]{:S(2)}, u32[]{:S(2)}) %collective-permute-start) | collective-permute-done | bytes 983072 | tf_op jit(solution)/shard_map/ppermute | solution.py:339
  53.2 19.8 %collective-permute-done.9.refs_9_.refs_7_ = bf16[48,6144]{1,0:T(8,128)(2,1)} collective-permute-done((bf16[48,6144]{1,0:T(8,128)(2,1)}, bf16[48,6144]{1,0:T(8,128)(2,1)}, u32[]{:S(2)}, u32[]{:S(2)}) %collective-permute-start.9) | collective-permute-done | bytes 589856 | tf_op jit(solution)/shard_map/ppermute | solution.py:339
  74.6 9.5 %collective-permute-done.6.refs_6_.refs_4_ = bf16[48,6144]{1,0:T(8,128)(2,1)S(1)} collective-permute-done((bf16[48,6144]{1,0:T(8,128)(2,1)}, bf16[48,6144]{1,0:T(8,128)(2,1)S(1)}, u32[]{:S(2)}, u32[]{:S(2)}) %collective-permute-start.6) | collective-permute-done | bytes 589856 | tf_op jit(solution)/shard_map/ppermute | solution.py:339
  88.0 9.3 %weight_terms.5.refs_10_ = f32[72,128,128]{2,1,0:T(8,128)} custom-call(s32[2]{0:T(128)} %pad_add_fusion.2.place_ref, s32[576]{0:T(1024)} %reduce.cols_ref, bf16[256,6144]{1,0:T(8,128)(2,1)} %refs_0_.3, bf16[256,1536]{1,0:T(8,128)(2,1)} %copy-done.9, bf16[48,6144]{1,0:T(8,128)(2,1)} %fusion.33.refs_2_.refs_0_, bf16[80,6144]{1,0:T(8,128)(2,1)} %copy-done.2, ...), custom_call_target="tpu_custom_call" | custom-call | flops 1207959552 | bytes 15728640 | tf_op jit(solution)/shard_map/weight_terms/pallas_call | solution.py:151
  97.3 9.3 %weight_terms.6.refs_10_ = f32[72,128,128]{2,1,0:T(8,128)} custom-call(s32[2]{0:T(128)} %pad_add_fusion.place_ref, s32[576]{0:T(1024)} %reduce.cols_ref, bf16[256,6144]{1,0:T(8,128)(2,1)} %refs_0_.3, bf16[256,1536]{1,0:T(8,128)(2,1)} %copy-done.9, bf16[48,6144]{1,0:T(8,128)(2,1)} %fusion.33.refs_2_.refs_0_, bf16[80,6144]{1,0:T(8,128)(2,1)} %copy-done.2, ...), custom_call_target="tpu_custom_call" | custom-call | flops 1207959552 | bytes 15728640 | tf_op jit(solution)/shard_map/weight_terms/pallas_call | solution.py:151
  106.6 22.7 %collective-permute-done.10 = bf16[64,1536]{1,0:T(8,128)(2,1)} collective-permute-done((bf16[64,1536]{1,0:T(8,128)(2,1)}, bf16[64,1536]{1,0:T(8,128)(2,1)}, u32[]{:S(2)}, u32[]{:S(2)}) %collective-permute-start.10) | collective-permute-done | bytes 196640 | tf_op jit(solution)/shard_map/ppermute | solution.py:339
  133.9 3.4 collective-permute-start.14
  147.1 42.2 %collective-permute-done.14.refs_2_.refs_4_ = bf16[80,6144]{1,0:T(8,128)(2,1)} collective-permute-done((bf16[80,6144]{1,0:T(8,128)(2,1)S(1)}, bf16[80,6144]{1,0:T(8,128)(2,1)}, u32[]{:S(2)}, u32[]{:S(2)}) %collective-permute-start.14) | collective-permute-done | bytes 983072 | tf_op jit(solution)/shard_map/ppermute | solution.py:339
  191.8 13.8 %act_partials.3 = (bf16[256,768]{1,0:T(8,128)(2,1)}, bf16[256,768]{1,0:T(8,128)(2,1)}, bf16[256,768]{1,0:T(8,128)(2,1)}, bf16[256,768]{1,0:T(8,128)(2,1)}) custom-call(s32[3]{0:T(128)} %pad_add_fusion.1.place_ref, s32[576]{0:T(1024)} %reduce.cols_ref, bf16[48,6144]{1,0:T(8,128)(2,1)} %fusion.33.refs_2_.refs_0_, bf16[80,6144]{1,0:T(8,128)(2,1)} %copy-done.2, ...), custom_call_target="tpu_custom_call" | custom-call | flops 2415919104 | bytes 11010048 | tf_op jit(solution)/shard_map/act_partials/pallas_call | solution.py:227
  210.3 9.9 %act_partials.4 = (bf16[256,768]{1,0:T(8,128)(2,1)}, bf16[256,768]{1,0:T(8,128)(2,1)}) custom-call(s32[3]{0:T(128)} %pad_add_fusion.1.place_ref, s32[576]{0:T(1024)} %reduce.cols_ref, bf16[48,6144]{1,0:T(8,128)(2,1)} %copy-done.6, bf16[80,6144]{1,0:T(8,128)(2,1)} %copy-done.1, bf16[80,6144]{1,0:T(8,128)(2,1)} %collective-permute-done.14.refs_2_.refs_4_, ...), custom_call_target="tpu_custom_call" | custom-call | flops 1207959552 | bytes 7864320 | tf_op jit(solution)/shard_map/act_partials/pallas_call | solution.py:227
  225.1 12.7 %collective-permute-done.19.refs_6_.refs_0_ = bf16[48,6144]{1,0:T(8,128)(2,1)S(1)} collective-permute-done((bf16[48,6144]{1,0:T(8,128)(2,1)}, bf16[48,6144]{1,0:T(8,128)(2,1)S(1)}, u32[]{:S(2)}, u32[]{:S(2)}) %collective-permute-start.19) | collective-permute-done | bytes 589856 | tf_op jit(solution)/shard_map/ppermute | solution.py:339
  237.8 11.7 %collective-permute-done.22.refs_9_.refs_3_ = bf16[48,6144]{1,0:T(8,128)(2,1)S(1)} collective-permute-done((bf16[48,6144]{1,0:T(8,128)(2,1)}, bf16[48,6144]{1,0:T(8,128)(2,1)S(1)}, u32[]{:S(2)}, u32[]{:S(2)}) %collective-permute-start.22) | collective-permute-done | bytes 589856 | tf_op jit(solution)/shard_map/ppermute | solution.py:339
  250.4 7.5 %weight_terms.7 = bf16[36,128,128]{2,1,0:T(8,128)(2,1)} custom-call(s32[2]{0:T(128)} %pad_add_fusion.2.place_ref, s32[576]{0:T(1024)} %reduce.cols_ref, bf16[256,3072]{1,0:T(8,128)(2,1)} %copy-done, bf16[256,3072]{1,0:T(8,128)(2,1)} %copy-done, bf16[48,6144]{1,0:T(8,128)(2,1)} %copy-done.6, bf16[80,6144]{1,0:T(8,128)(2,1)} %copy-done.1, ...), custom_call_target="tpu_custom_call" | custom-call | flops 603979776 | bytes 11010048 | tf_op jit(solution)/shard_map/weight_terms/pallas_call | solution.py:151
  257.9 7.5 %weight_terms.8 = bf16[36,128,128]{2,1,0:T(8,128)(2,1)} custom-call(s32[2]{0:T(128)} %pad_add_fusion.2.place_ref, s32[576]{0:T(1024)} %reduce.cols_ref, bf16[256,3072]{1,0:T(8,128)(2,1)} %copy-done, bf16[256,3072]{1,0:T(8,128)(2,1)} %copy-done, bf16[48,6144]{1,0:T(8,128)(2,1)} %copy-done.6, bf16[80,6144]{1,0:T(8,128)(2,1)} %copy-done.1, ...), custom_call_target="tpu_custom_call" | custom-call | flops 603979776 | bytes 11010048 | tf_op jit(solution)/shard_map/weight_terms/pallas_call | solution.py:151
  266.4 10.1 %act_partials.5 = (bf16[256,768]{1,0:T(8,128)(2,1)}, bf16[256,768]{1,0:T(8,128)(2,1)}) custom-call(s32[3]{0:T(128)} %pad_add_fusion.1.place_ref, s32[576]{0:T(1024)} %reduce.cols_ref, bf16[48,6144]{1,0:T(8,128)(2,1)} %copy-done.7, bf16[80,6144]{1,0:T(8,128)(2,1)} %collective-permute-done.20.refs_7_.refs_1_, bf16[80,6144]{1,0:T(8,128)(2,1)} %copy-done.5, ...), custom_call_target="tpu_custom_call" | custom-call | flops 1207959552 | bytes 7864320 | tf_op jit(solution)/shard_map/act_partials/pallas_call | solution.py:227
  285.0 10.0 %weight_terms.9.sum_ref = f32[72,128,128]{2,1,0:T(8,128)} custom-call(s32[2]{0:T(128)} %pad_add_fusion.place_ref, s32[576]{0:T(1024)} %reduce.cols_ref, bf16[256,3072]{1,0:T(8,128)(2,1)} %copy-done, bf16[256,3072]{1,0:T(8,128)(2,1)} %copy-done, bf16[48,6144]{1,0:T(8,128)(2,1)} %copy-done.6, bf16[80,6144]{1,0:T(8,128)(2,1)} %copy-done.1, ...), custom_call_target="tpu_custom_call" | custom-call | flops 1207959552 | bytes 15728640 | tf_op jit(solution)/shard_map/weight_terms/pallas_call | solution.py:151
  298.7 5.7 %collective-permute-done.30 = bf16[256,768]{1,0:T(8,128)(2,1)} collective-permute-done((bf16[256,768]{1,0:T(8,128)(2,1)S(1)}, bf16[256,768]{1,0:T(8,128)(2,1)}, u32[]{:S(2)}, u32[]{:S(2)}) %collective-permute-start.30) | collective-permute-done | bytes 393248 | tf_op jit(solution)/shard_map/ppermute | solution.py:342
  307.9 3.5 collective-permute-start.28
  311.8 3.4 collective-permute-start.27
  316.0 3.7 %add_part.2.refs_0_ = bf16[72,128,128]{2,1,0:T(8,128)(2,1)} custom-call(f32[72,128,128]{2,1,0:T(8,128)} %weight_terms.9.sum_ref, bf16[36,128,128]{2,1,0:T(8,128)(2,1)} %collective-permute-done.29.part_ref), custom_call_target="tpu_custom_call" | custom-call | flops 589824 | bytes 4718592 | tf_op jit(solution)/shard_map/add_part/pallas_call | solution.py:296
  323.6 17.1 %collective-permute-done.28.refs_0_ = bf16[128,768]{1,0:T(8,128)(2,1)S(1)} collective-permute-done((bf16[128,768]{1,0:T(8,128)(2,1)S(1)}, bf16[128,768]{1,0:T(8,128)(2,1)S(1)}, u32[]{:S(2)}, u32[]{:S(2)}) %collective-permute-start.28) | collective-permute-done | bytes 196640 | tf_op jit(solution)/shard_map/ppermute | solution.py:339
  346.0 3.7 %add_part.3 = bf16[72,128,128]{2,1,0:T(8,128)(2,1)} custom-call(f32[72,128,128]{2,1,0:T(8,128)} %weight_terms.9.sum_ref, bf16[36,128,128]{2,1,0:T(8,128)(2,1)} %collective-permute-done.25.part_ref, bf16[72,128,128]{2,1,0:T(8,128)(2,1)} %add_part.2.refs_0_), custom_call_target="tpu_custom_call", output_to_operand_aliasing={{}: (2, {})} | custom-call | flops 589824 | bytes 4718592 | tf_op jit(solution)/shard_map/add_part/pallas_call | solution.py:296
  (171 shorter events, 97.1 us)
Async XLA Ops:
  6.3 47.0 %collective-permute-start = (bf16[80,6144]{1,0:T(8,128)(2,1)S(1)}, bf16[80,6144]{1,0:T(8,128)(2,1)S(1)}, u32[]{:S(2)}, u32[]{:S(2)}) collective-permute-start(bf16[80,6144]{1,0:T(8,128)(2,1)S(1)} %fusion.11.refs_3_.refs_1_), channel_id=1, source_target_pairs={{0,16},{4,20},{8,24},{12,28},{16,0},{20,4},{24,8},{28,12},{1,17},{... | collective-permute-start | bytes 2949128 | tf_op jit(solution)/shard_map/ppermute | solution.py:339
  10.4 77.6 %collective-permute-start.7 = (bf16[80,6144]{1,0:T(8,128)(2,1)S(1)}, bf16[80,6144]{1,0:T(8,128)(2,1)}, u32[]{:S(2)}, u32[]{:S(2)}) collective-permute-start(bf16[80,6144]{1,0:T(8,128)(2,1)S(1)} %fusion.11.refs_3_.refs_1_), channel_id=1, source_target_pairs={{0,4},{4,0},{8,12},{12,8},{16,20},{20,16},{24,28},{28,24},{1,5},{5... | collective-permute-start | bytes 2949128 | tf_op jit(solution)/shard_map/ppermute | solution.py:339
  13.8 25.4 %collective-permute-start.3 = (bf16[64,1536]{1,0:T(8,128)(2,1)}, bf16[64,1536]{1,0:T(8,128)(2,1)S(1)}, u32[]{:S(2)}, u32[]{:S(2)}) collective-permute-start(bf16[64,1536]{1,0:T(8,128)(2,1)} %pad_maximum_fusion.3), channel_id=1, source_target_pairs={{0,4},{4,0},{8,12},{12,8},{16,20},{20,16},{24,28},{28,24},{1,5},{5... | collective-permute-start | bytes 589832 | tf_op jit(solution)/shard_map/ppermute | solution.py:339
  17.2 68.3 %collective-permute-start.8 = (bf16[80,6144]{1,0:T(8,128)(2,1)S(1)}, bf16[80,6144]{1,0:T(8,128)(2,1)}, u32[]{:S(2)}, u32[]{:S(2)}) collective-permute-start(bf16[80,6144]{1,0:T(8,128)(2,1)S(1)} %fusion.6.refs_4_.refs_2_), channel_id=1, source_target_pairs={{0,4},{4,0},{8,12},{12,8},{16,20},{20,16},{24,28},{28,24},{1,5},{5... | collective-permute-start | bytes 2949128 | tf_op jit(solution)/shard_map/ppermute | solution.py:339
  21.6 51.5 %collective-permute-start.9 = (bf16[48,6144]{1,0:T(8,128)(2,1)}, bf16[48,6144]{1,0:T(8,128)(2,1)}, u32[]{:S(2)}, u32[]{:S(2)}) collective-permute-start(bf16[48,6144]{1,0:T(8,128)(2,1)} %fusion.28.refs_5_.refs_3_), channel_id=1, source_target_pairs={{0,4},{4,0},{8,12},{12,8},{16,20},{20,16},{24,28},{28,24},{1,5},{5... | collective-permute-start | bytes 1769480 | tf_op jit(solution)/shard_map/ppermute | solution.py:339
  46.7 37.4 %collective-permute-start.6 = (bf16[48,6144]{1,0:T(8,128)(2,1)}, bf16[48,6144]{1,0:T(8,128)(2,1)S(1)}, u32[]{:S(2)}, u32[]{:S(2)}) collective-permute-start(bf16[48,6144]{1,0:T(8,128)(2,1)} %fusion.33.refs_2_.refs_0_), channel_id=1, source_target_pairs={{0,4},{4,0},{8,12},{12,8},{16,20},{20,16},{24,28},{28,24},{1,5},{5... | collective-permute-start | bytes 1769480 | tf_op jit(solution)/shard_map/ppermute | solution.py:339
  53.2 80.7 %collective-permute-start.13 = (bf16[48,6144]{1,0:T(8,128)(2,1)}, bf16[48,6144]{1,0:T(8,128)(2,1)S(1)}, u32[]{:S(2)}, u32[]{:S(2)}) collective-permute-start(bf16[48,6144]{1,0:T(8,128)(2,1)} %fusion.33.refs_2_.refs_0_), channel_id=1, source_target_pairs={{0,16},{4,20},{8,24},{12,28},{16,0},{20,4},{24,8},{28,12},{1,17},{... | collective-permute-start | bytes 1769480 | tf_op jit(solution)/shard_map/ppermute | solution.py:339
  73.1 118.7 %collective-permute-start.15 = (bf16[72,128,128]{2,1,0:T(8,128)(2,1)}, bf16[72,128,128]{2,1,0:T(8,128)(2,1)}, u32[]{:S(2)}, u32[]{:S(2)}) collective-permute-start(bf16[72,128,128]{2,1,0:T(8,128)(2,1)} %bitcast.6.refs_8_.refs_4_), channel_id=1, source_target_pairs={{0,8},{4,12},{8,0},{12,4},{16,24},{20,28},{24,16},{28,20},{1,9},{5... | collective-permute-start | bytes 7077896 | tf_op jit(solution)/shard_map/ppermute | solution.py:339
  84.2 45.0 %collective-permute-start.10 = (bf16[64,1536]{1,0:T(8,128)(2,1)}, bf16[64,1536]{1,0:T(8,128)(2,1)}, u32[]{:S(2)}, u32[]{:S(2)}) collective-permute-start(bf16[64,1536]{1,0:T(8,128)(2,1)} %pad_maximum_fusion.4), channel_id=1, source_target_pairs={{0,20},{4,16},{8,28},{12,24},{16,4},{20,0},{24,12},{28,8},{1,21},{... | collective-permute-start | bytes 589832 | tf_op jit(solution)/shard_map/ppermute | solution.py:339
  85.5 45.9 %collective-permute-start.2 = (bf16[64,1536]{1,0:T(8,128)(2,1)}, bf16[64,1536]{1,0:T(8,128)(2,1)S(1)}, u32[]{:S(2)}, u32[]{:S(2)}) collective-permute-start(bf16[64,1536]{1,0:T(8,128)(2,1)} %pad_maximum_fusion.2), channel_id=1, source_target_pairs={{0,16},{4,20},{8,24},{12,28},{16,0},{20,4},{24,8},{28,12},{1,17},{... | collective-permute-start | bytes 589832 | tf_op jit(solution)/shard_map/ppermute | solution.py:339
  133.9 55.4 %collective-permute-start.14 = (bf16[80,6144]{1,0:T(8,128)(2,1)S(1)}, bf16[80,6144]{1,0:T(8,128)(2,1)}, u32[]{:S(2)}, u32[]{:S(2)}) collective-permute-start(bf16[80,6144]{1,0:T(8,128)(2,1)S(1)} %copy-done.4), channel_id=1, source_target_pairs={{0,16},{4,20},{8,24},{12,28},{16,0},{20,4},{24,8},{28,12},{1,17},{... | collective-permute-start | bytes 2949128 | tf_op jit(solution)/shard_map/ppermute | solution.py:339
  140.2 50.6 %collective-permute-start.12 = (bf16[128,3072]{1,0:T(8,128)(2,1)S(1)}, bf16[128,3072]{1,0:T(8,128)(2,1)S(1)}, u32[]{:S(2)}, u32[]{:S(2)}) collective-permute-start(bf16[128,3072]{1,0:T(8,128)(2,1)S(1)} %pad_maximum_fusion), channel_id=1, source_target_pairs={{0,1},{1,0},{2,3},{3,2},{4,5},{5,4},{6,7},{7,6},{8,9},{9,8},{10,11... | collective-permute-start | bytes 2359304 | tf_op jit(solution)/shard_map/ppermute | solution.py:342
  141.0 69.4 %collective-permute-start.1 = (bf16[48,6144]{1,0:T(8,128)(2,1)}, bf16[48,6144]{1,0:T(8,128)(2,1)}, u32[]{:S(2)}, u32[]{:S(2)}) collective-permute-start(bf16[48,6144]{1,0:T(8,128)(2,1)} %fusion.28.refs_5_.refs_3_), channel_id=1, source_target_pairs={{0,16},{4,20},{8,24},{12,28},{16,0},{20,4},{24,8},{28,12},{1,17},{... | collective-permute-start | bytes 1769480 | tf_op jit(solution)/shard_map/ppermute | solution.py:339
  144.3 93.5 %collective-permute-start.20 = (bf16[80,6144]{1,0:T(8,128)(2,1)S(1)}, bf16[80,6144]{1,0:T(8,128)(2,1)}, u32[]{:S(2)}, u32[]{:S(2)}) collective-permute-start(bf16[80,6144]{1,0:T(8,128)(2,1)S(1)} %collective-permute-done.refs_1_.refs_3_), channel_id=1, source_target_pairs={{0,4},{4,0},{8,12},{12,8},{16,20},{20,16},{24,28},{28,24},{1,5},{5... | collective-permute-start | bytes 2949128 | tf_op jit(solution)/shard_map/ppermute | solution.py:339
  189.3 48.5 %collective-permute-start.21 = (bf16[80,6144]{1,0:T(8,128)(2,1)}, bf16[80,6144]{1,0:T(8,128)(2,1)S(1)}, u32[]{:S(2)}, u32[]{:S(2)}) collective-permute-start(bf16[80,6144]{1,0:T(8,128)(2,1)} %collective-permute-done.14.refs_2_.refs_4_), channel_id=1, source_target_pairs={{0,4},{4,0},{8,12},{12,8},{16,20},{20,16},{24,28},{28,24},{1,5},{5... | collective-permute-start | bytes 2949128 | tf_op jit(solution)/shard_map/ppermute | solution.py:339
  221.4 16.4 %collective-permute-start.19 = (bf16[48,6144]{1,0:T(8,128)(2,1)}, bf16[48,6144]{1,0:T(8,128)(2,1)S(1)}, u32[]{:S(2)}, u32[]{:S(2)}) collective-permute-start(bf16[48,6144]{1,0:T(8,128)(2,1)} %copy-done.6), channel_id=1, source_target_pairs={{0,4},{4,0},{8,12},{12,8},{16,20},{20,16},{24,28},{28,24},{1,5},{5... | collective-permute-start | bytes 1769480 | tf_op jit(solution)/shard_map/ppermute | solution.py:339
  221.9 27.6 %collective-permute-start.22 = (bf16[48,6144]{1,0:T(8,128)(2,1)}, bf16[48,6144]{1,0:T(8,128)(2,1)S(1)}, u32[]{:S(2)}, u32[]{:S(2)}) collective-permute-start(bf16[48,6144]{1,0:T(8,128)(2,1)} %collective-permute-done.1.refs_3_.refs_5_), channel_id=1, source_target_pairs={{0,4},{4,0},{8,12},{12,8},{16,20},{20,16},{24,28},{28,24},{1,5},{5... | collective-permute-start | bytes 1769480 | tf_op jit(solution)/shard_map/ppermute | solution.py:339
  224.6 40.8 %collective-permute-start.23 = (bf16[128,768]{1,0:T(8,128)(2,1)S(1)}, bf16[128,768]{1,0:T(8,128)(2,1)}, u32[]{:S(2)}, u32[]{:S(2)}) collective-permute-start(bf16[128,768]{1,0:T(8,128)(2,1)S(1)} %get-tuple-element.85), channel_id=1, source_target_pairs={{0,2},{1,3},{2,0},{3,1},{4,6},{5,7},{6,4},{7,5},{8,10},{9,11},{10,... | collective-permute-start | bytes 589832 | tf_op jit(solution)/shard_map/ppermute | solution.py:342
  280.7 16.0 %collective-permute-start.31 = (bf16[256,768]{1,0:T(8,128)(2,1)S(1)}, bf16[256,768]{1,0:T(8,128)(2,1)}, u32[]{:S(2)}, u32[]{:S(2)}) collective-permute-start(bf16[256,768]{1,0:T(8,128)(2,1)S(1)} %copy-done.14), channel_id=1, source_target_pairs={{0,2},{1,3},{2,0},{3,1},{4,6},{5,7},{6,4},{7,5},{8,10},{9,11},{10,... | collective-permute-start | bytes 1179656 | tf_op jit(solution)/shard_map/ppermute | solution.py:342
  282.3 22.1 %collective-permute-start.30 = (bf16[256,768]{1,0:T(8,128)(2,1)S(1)}, bf16[256,768]{1,0:T(8,128)(2,1)}, u32[]{:S(2)}, u32[]{:S(2)}) collective-permute-start(bf16[256,768]{1,0:T(8,128)(2,1)S(1)} %copy-done.13), channel_id=1, source_target_pairs={{0,2},{1,3},{2,0},{3,1},{4,6},{5,7},{6,4},{7,5},{8,10},{9,11},{10,... | collective-permute-start | bytes 1179656 | tf_op jit(solution)/shard_map/ppermute | solution.py:342
  282.8 29.1 %collective-permute-start.29 = (bf16[36,128,128]{2,1,0:T(8,128)(2,1)S(1)}, bf16[36,128,128]{2,1,0:T(8,128)(2,1)}, u32[]{:S(2)}, u32[]{:S(2)}) collective-permute-start(bf16[36,128,128]{2,1,0:T(8,128)(2,1)S(1)} %copy-done.18), channel_id=1, source_target_pairs={{0,8},{4,12},{8,0},{12,4},{16,24},{20,28},{24,16},{28,20},{1,9},{5... | collective-permute-start | bytes 3538952 | tf_op jit(solution)/shard_map/ppermute | solution.py:339
  284.9 61.0 %collective-permute-start.25 = (bf16[36,128,128]{2,1,0:T(8,128)(2,1)S(1)}, bf16[36,128,128]{2,1,0:T(8,128)(2,1)}, u32[]{:S(2)}, u32[]{:S(2)}) collective-permute-start(bf16[36,128,128]{2,1,0:T(8,128)(2,1)S(1)} %copy-done.17), channel_id=1, source_target_pairs={{0,8},{4,12},{8,0},{12,4},{16,24},{20,28},{24,16},{28,20},{1,9},{5... | collective-permute-start | bytes 3538952 | tf_op jit(solution)/shard_map/ppermute | solution.py:339
  307.9 32.9 %collective-permute-start.28 = (bf16[128,768]{1,0:T(8,128)(2,1)S(1)}, bf16[128,768]{1,0:T(8,128)(2,1)S(1)}, u32[]{:S(2)}, u32[]{:S(2)}) collective-permute-start(bf16[128,768]{1,0:T(8,128)(2,1)S(1)} %add_convert_fusion.7), channel_id=1, source_target_pairs={{0,16},{4,20},{8,24},{12,28},{16,0},{20,4},{24,8},{28,12},{1,17},{... | collective-permute-start | bytes 589832 | tf_op jit(solution)/shard_map/ppermute | solution.py:339
  311.8 31.6 %collective-permute-start.27 = (bf16[128,768]{1,0:T(8,128)(2,1)}, bf16[128,768]{1,0:T(8,128)(2,1)S(1)}, u32[]{:S(2)}, u32[]{:S(2)}) collective-permute-start(bf16[128,768]{1,0:T(8,128)(2,1)} %add_convert_fusion.6), channel_id=1, source_target_pairs={{0,20},{4,16},{8,28},{12,24},{16,4},{20,0},{24,12},{28,8},{1,21},{... | collective-permute-start | bytes 589832 | tf_op jit(solution)/shard_map/ppermute | solution.py:339
  (48 other events, 471.8 us)
